TPU v7x, 512 devices: a whole 4x4x16 slice. The times are simulated.
512 devices in a mesh: tm: 8 (over x, core), dp: 64 (over z, y).
Axes of the slice: x: 4, y: 4, z: 16, core: 2. Of those that a mesh axis runs over, the one named last changes fastest.
Arguments:
- edge_feat: bfloat16 [8, 8192, 186], P('tm', 'dp'), may hold values from -6 to 6
- endpoint_slots: int32 [8, 2, 8192], P('tm', None, 'dp'), may hold values from 0 to 2047, as said below
- neighbor_slots: int32 [8, 20, 8192], P('tm', None, 'dp'), may hold values from 0 to 2047, as said below
- neighbor_gap: int32 [8, 20, 8192], P('tm', None, 'dp'), may hold values from 0 to 999
- score_grad: float32 [8, 8192], P('tm', 'dp'), may hold values from -1.5 to 1.5
- node_list: int32 [8, 64, 2048], P('tm', 'dp'), may hold values from 0 to 128, as said below
- memory0: float32 [8192, 256], P('dp'), may hold values from -6 to 6
- msg_weight: bfloat16 [186, 256], replicated, may hold values from -0.4375 to 0.4375
- gate_weight: bfloat16 [256, 512], replicated, may hold values from -0.375 to 0.375
- gate_bias: float32 [512], replicated, may hold values from -4 to 4
- omega: float32 [256], replicated, may hold values from 0.001 to 1
- attn_weights: bfloat16 [4, 256, 256], replicated, may hold values from -0.375 to 0.375
- pred_weights: bfloat16 [2, 256, 256], replicated, may hold values from -0.375 to 0.375
- pred_out: float32 [256], replicated, may hold values from -0.375 to 0.375
Outputs:
- scores: float32 [8, 8192], P('tm', 'dp')
- new_memory: float32 [8, 8192, 256], P('tm', 'dp')
- grad_out_proj: float32 [256, 256], replicated
- grad_pred: float32 [2, 256, 256], replicated
Inputs may be any that keep to these rules, and one draw needn't show every extreme that they name: `node_list`: each block of 32 slots (one device's requests to one owner) holds distinct rows first and 128 in the empty slots after them; every block holds at least one row; in each mini-batch some owner's block is full from every device. `endpoint_slots`: every slot points at a non-empty entry of its device's node list. `neighbor_slots`: every slot points at a non-empty entry of its device's node list.
All inputs are finite; a program needn't handle non-finite values.
Results may differ from a plain program's by a relative error of at most 0.017.
Values may be sent and summed in bfloat16 or wider, within the bound.
No kernel may reach another device: no remote copies, remote signals or barrier semaphores. Data moves between devices by JAX's collectives and lax.ppermute only.
A program may use at most 64 MiB of HBM per device.

v0:
```python
import math

import jax
import jax.numpy as jnp
from jax import lax
from jax.sharding import PartitionSpec as P

HEADS = 2


def shifted(value, axis, steps):
    count = lax.axis_size(axis)
    initial, last = (max(0, -steps), min(count, count - steps))
    return lax.ppermute(value, axis, [(source, source + steps) for source in range(initial, last)])


def local_step(
    slot_rows,
    end_slots,
    near_slots,
    near_gaps,
    cot_rows,
    omega,
    attn_weights,
    pred_weights,
    pred_out,
):
    feat_width = slot_rows.shape[1]
    events = end_slots.shape[1]
    near_count = near_slots.shape[0] // 2
    head_dim = feat_width // HEADS
    self_rows = jnp.take(slot_rows, end_slots, axis=0)
    near_rows = jnp.take(slot_rows, near_slots, axis=0).reshape(2, near_count, events, feat_width)
    phases = near_gaps.reshape(2, near_count, events).astype(jnp.float32)[..., None] * omega
    near_feat = (near_rows.astype(jnp.float32) + jnp.cos(phases)).astype(jnp.bfloat16)
    query_proj = jnp.einsum(
        "pea,ab->peb", self_rows, attn_weights[0], preferred_element_type=jnp.float32
    )
    key_proj = jnp.einsum(
        "pkea,ab->pkeb", near_feat, attn_weights[1], preferred_element_type=jnp.float32
    )
    value_proj = jnp.einsum(
        "pkea,ab->pkeb", near_feat, attn_weights[2], preferred_element_type=jnp.float32
    )
    query_heads = query_proj.reshape(2, 1, events, HEADS, head_dim)
    key_heads = key_proj.reshape(2, near_count, events, HEADS, head_dim)
    value_heads = value_proj.reshape(2, near_count, events, HEADS, head_dim)
    att_logits = jnp.sum(query_heads * key_heads, axis=-1) / math.sqrt(head_dim)
    weights_att = jax.nn.softmax(att_logits, axis=1)
    mixed_heads = (
        jnp.sum(weights_att[..., None] * value_heads, axis=1)
        .reshape(2, events, feat_width)
        .astype(jnp.bfloat16)
    )
    state_full = self_rows.astype(jnp.float32) + jnp.einsum(
        "pea,ab->peb", mixed_heads, attn_weights[3], preferred_element_type=jnp.float32
    )
    state_bf = state_full.astype(jnp.bfloat16)
    pre_pred = jnp.dot(state_bf[0], pred_weights[0], preferred_element_type=jnp.float32) + jnp.dot(
        state_bf[1], pred_weights[1], preferred_element_type=jnp.float32
    )
    sigmoid_pre = jax.nn.sigmoid(pre_pred)
    logit_out = jnp.sum(pre_pred * sigmoid_pre * pred_out, axis=-1)
    grad_pre = (
        cot_rows[:, None] * pred_out * (sigmoid_pre * (1.0 + pre_pred * (1.0 - sigmoid_pre)))
    ).astype(jnp.bfloat16)
    grad_first = jnp.einsum("ea,eb->ab", state_bf[0], grad_pre, preferred_element_type=jnp.float32)
    grad_second = jnp.einsum("ea,eb->ab", state_bf[1], grad_pre, preferred_element_type=jnp.float32)
    grad_state = jnp.einsum(
        "eb,pab->pea", grad_pre, pred_weights, preferred_element_type=jnp.float32
    ).astype(jnp.bfloat16)
    grad_out_proj = jnp.einsum(
        "pea,peb->ab", mixed_heads, grad_state, preferred_element_type=jnp.float32
    )
    return (logit_out, grad_out_proj, jnp.stack([grad_first, grad_second]))


def per_device(
    edge_feat,
    endpoint_slots,
    neighbor_slots,
    neighbor_gap,
    score_grad,
    node_list,
    memory0,
    msg_weight,
    gate_weight,
    gate_bias,
    omega,
    attn_weights,
    pred_weights,
    pred_out,
):
    groups = lax.axis_size("dp")
    node_dev, feat_width = memory0.shape
    list_len = node_list.shape[2]
    per_owner = list_len // groups
    requests = node_list[0, 0].reshape(groups, per_owner)
    wanted = lax.all_to_all(requests, "dp", split_axis=0, concat_axis=0, tiled=True)
    message = jnp.dot(edge_feat[0], msg_weight, preferred_element_type=jnp.float32).astype(
        jnp.bfloat16
    )
    message_wide = message.astype(jnp.float32)
    end_slots = endpoint_slots[0]
    flat_ends = end_slots.reshape(-1)
    slot_sums = (
        jnp.zeros((list_len, feat_width), jnp.float32)
        .at[flat_ends]
        .add(jnp.concatenate([message_wide, message_wide]))
    )
    slot_tally = jnp.zeros((list_len,), jnp.float32).at[flat_ends].add(1.0)
    got_sums, got_tally = (
        lax.all_to_all(
            slot_sums.reshape(groups, per_owner, feat_width),
            "dp",
            split_axis=0,
            concat_axis=0,
            tiled=True,
        ),
        lax.all_to_all(
            slot_tally.reshape(groups, per_owner), "dp", split_axis=0, concat_axis=0, tiled=True
        ),
    )
    picker = (wanted.reshape(-1)[:, None] == jnp.arange(node_dev)[None, :]).astype(jnp.bfloat16)
    flat_sums = got_sums.reshape(-1, feat_width)
    sums_high = flat_sums.astype(jnp.bfloat16)
    sums_low = (flat_sums - sums_high.astype(jnp.float32)).astype(jnp.bfloat16)
    totals = jnp.einsum(
        "sn,sd->nd", picker, sums_high, preferred_element_type=jnp.float32
    ) + jnp.einsum("sn,sd->nd", picker, sums_low, preferred_element_type=jnp.float32)
    counts = jnp.dot(
        got_tally.reshape(-1), picker.astype(jnp.float32), precision=lax.Precision.HIGHEST
    )
    touched = (counts > 0.5).astype(jnp.float32)
    mean_msg = (totals / jnp.maximum(counts, 1.0)[:, None]).astype(jnp.bfloat16)
    pre_gate = jnp.dot(mean_msg, gate_weight, preferred_element_type=jnp.float32) + gate_bias
    update = jax.nn.sigmoid(pre_gate[:, :feat_width]) * touched[:, None]
    candidate = jnp.tanh(pre_gate[:, feat_width:])
    decay_rate = 1.0 - update
    inject = update * candidate
    section_index = lax.axis_index("tm")
    before = memory0
    for relay_step in range(lax.axis_size("tm") - 1):
        moved_state = shifted((decay_rate * before + inject).astype(jnp.bfloat16), "tm", 1).astype(
            jnp.float32
        )
        before = jnp.where(section_index == 0, memory0, moved_state)
    new_memory = decay_rate * before + inject
    memory_bf = before.astype(jnp.bfloat16)
    full_table = lax.all_gather(memory_bf, "dp", axis=0, tiled=True)
    owner_of = jnp.arange(list_len, dtype=jnp.int32) // per_owner
    global_row = owner_of * node_dev + jnp.minimum(node_list[0, 0], node_dev - 1)
    slot_rows = jnp.take(full_table, global_row, axis=0)
    logit_out, grad_out, grad_pair = local_step(
        slot_rows,
        end_slots,
        neighbor_slots[0],
        neighbor_gap[0],
        score_grad[0],
        omega,
        attn_weights,
        pred_weights,
        pred_out,
    )
    grad_out, grad_pair = lax.psum((grad_out, grad_pair), ("tm", "dp"))
    return (logit_out[None, :], new_memory[None], grad_out, grad_pair)


def solution(mesh):
    in_specs = (
        P("tm", "dp", None),
        P("tm", None, "dp"),
        P("tm", None, "dp"),
        P("tm", None, "dp"),
        P("tm", "dp"),
        P("tm", "dp", None),
        P("dp", None),
        P(),
        P(),
        P(),
        P(),
        P(),
        P(),
        P(),
    )
    out_specs = (P("tm", "dp"), P("tm", "dp", None), P(), P())
    return jax.shard_map(
        per_device, mesh=mesh, in_specs=in_specs, out_specs=out_specs, check_vma=False
    )
```

profile of v0, /device:TPU:1, one launch (start us, length us, event | category | flops | bytes accessed | tf_op | source)
XLA Modules:
  0.0 856.3 jit_solution(11601709572848172272)
XLA Ops:
  7.7 1.4 broadcast_minimum_fusion
  9.8 19.3 %all-to-all-start = ((s32[64,1,32]{2,1,0:T(1,128)}), s32[64,1,32]{2,1,0:T(1,128)S(1)}, u32[]{:S(2)}, u32[]{:S(2)}) async-start(s32[64,1,32]{2,1,0:T(1,128)} %bitcast.2), calls=%async_computation | async-start | bytes 65536 | tf_op jit(solution)/shard_map/all_to_all | solution.py:99
  29.7 2.0 scatter_custom_fusion.1
  32.4 10.0 %all-to-all-done = s32[64,1,32]{2,1,0:T(1,128)S(1)} async-done(((s32[64,1,32]{2,1,0:T(1,128)}), s32[64,1,32]{2,1,0:T(1,128)S(1)}, u32[]{:S(2)}, u32[]{:S(2)}) %all-to-all-start) | async-done | bytes 8224 | tf_op jit(solution)/shard_map/all_to_all | solution.py:99
  42.4 4.6 all-to-all-start.2
  48.1 3.4 scatter_custom_fusion
  51.5 9.0 %all-to-all-done.2 = f32[64,1,32]{2,1,0:T(1,128)S(1)} async-done(((f32[64,1,32]{2,1,0:T(1,128)}), f32[64,1,32]{2,1,0:T(1,128)S(1)}, u32[]{:S(2)}, u32[]{:S(2)}) %all-to-all-start.2) | async-done | bytes 8224 | tf_op jit(solution)/shard_map/all_to_all | solution.py:120
  60.5 5.5 all-to-all-start.1
  68.9 90.8 %all-to-all-done.1 = f32[64,32,256]{2,1,0:T(8,128)S(1)} async-done(((f32[64,32,256]{2,1,0:T(8,128)}), f32[64,32,256]{2,1,0:T(8,128)S(1)}, u32[]{:S(2)}, u32[]{:S(2)}) %all-to-all-start.1) | async-done | bytes 2097184 | tf_op jit(solution)/shard_map/all_to_all | solution.py:113
  161.8 10.8 %collective-permute-start = (bf16[128,256]{1,0:T(8,128)(2,1)S(1)}, bf16[128,256]{1,0:T(8,128)(2,1)S(1)}, u32[]{:S(2)}, u32[]{:S(2)}) collective-permute-start(bf16[128,256]{1,0:T(8,128)(2,1)S(1)} %get-tuple-element.6), channel_id=1, source_target_pairs={{0,64},{64,128},{128,192},{192,256},{256,320},{320,384},{384,448},... | collective-permute-start | bytes 196616 | tf_op jit(solution)/shard_map/ppermute | solution.py:14
  172.6 1.3 collective-permute-done
  174.0 4.3 collective-permute-start.1
  178.3 1.3 collective-permute-done.1
  179.7 4.4 collective-permute-start.2
  184.1 1.3 collective-permute-done.2
  185.5 4.3 collective-permute-start.3
  189.8 1.3 collective-permute-done.3
  191.2 4.3 collective-permute-start.4
  195.5 1.3 collective-permute-done.4
  196.9 4.3 collective-permute-start.5
  201.2 1.3 collective-permute-done.5
  202.6 4.3 collective-permute-start.6
  206.8 1.3 collective-permute-done.6
  211.0 128.7 %all-gather.2.cloned.1.call-done = bf16[8192,256]{1,0:T(8,128)(2,1)} async-done(((bf16[128,256]{1,0:T(8,128)(2,1)}), bf16[8192,256]{1,0:T(8,128)(2,1)}) %all-gather.2.cloned.1.call-update) | async-done | bytes 4194320 | tf_op jit(solution)/shard_map/all_gather | solution.py:150
  339.6 9.4 %gather_fusion = bf16[2048,256]{1,0:T(8,128)(2,1)S(1)} fusion(bf16[8192,256]{1,0:T(8,128)(2,1)} %all-gather.2.cloned.1.call-done, s32[2048]{0:T(1024)S(1)} %broadcast_clamp_fusion), kind=kCustom, calls=%fused_computation | custom fusion | bytes 2105344 | tf_op jit(solution)/shard_map/jit(_take)/gather | solution.py:153
  349.5 7.6 gather_fusion.2
  357.1 1.2 gather_fusion.1
  358.5 10.1 %add_convert_fusion = bf16[20,128,256]{2,1,0:T(8,128)(2,1)S(1)} fusion(f32[256]{0:T(256)S(1)} %copy-done.10, f32[20,128]{1,0:T(8,128)S(1)} %bitcast.137, bf16[20,128,256]{2,1,0:T(8,128)(2,1)S(1)} %bitcast.127, pred[20,128]{1,0:T(8,128)(4,1)S(1)} %compare_and_fusion), kind=kLoop, calls=%fused_computation.7 | loop fusion | flops 3276800 | bytes 2635264 | tf_op jit(solution)/shard_map/convert_element_type | solution.py:35
  370.8 1.1 fusion.1
  376.1 469.8 %all-reduce.3.cloned.1.call-done = (f32[256,256]{1,0:T(8,128)}, f32[2,256,256]{2,1,0:T(8,128)}) async-done(((f32[256,256]{1,0:T(8,128)}, f32[2,256,256]{2,1,0:T(8,128)}), (f32[256,256]{1,0:T(8,128)}, f32[2,256,256]{2,1,0:T(8,128)})) %all-reduce.3.cloned.1.call-update) | async-done | bytes 786448 | tf_op jit(solution)/shard_map/psum | solution.py:165
  845.9 1.7 copy.58
  847.6 1.9 copy.59
  (86 shorter events, 18.8 us)
Async XLA Ops:
  7.2 153.5 %copy-start = (bf16[256,512]{1,0:T(8,128)(2,1)S(1)}, bf16[256,512]{1,0:T(8,128)(2,1)}, u32[]{:S(2)}) copy-start(bf16[256,512]{1,0:T(8,128)(2,1)} %param.22) | copy-start | bytes 786436
  9.8 32.7 %all-to-all-start = ((s32[64,1,32]{2,1,0:T(1,128)}), s32[64,1,32]{2,1,0:T(1,128)S(1)}, u32[]{:S(2)}, u32[]{:S(2)}) async-start(s32[64,1,32]{2,1,0:T(1,128)} %bitcast.2), calls=%async_computation | async-start | bytes 65536 | tf_op jit(solution)/shard_map/all_to_all | solution.py:99
  42.4 18.1 %all-to-all-start.2 = ((f32[64,1,32]{2,1,0:T(1,128)}), f32[64,1,32]{2,1,0:T(1,128)S(1)}, u32[]{:S(2)}, u32[]{:S(2)}) async-start(f32[64,1,32]{2,1,0:T(1,128)} %bitcast.8), calls=%async_computation.2 | async-start | bytes 65536 | tf_op jit(solution)/shard_map/all_to_all | solution.py:120
  60.5 99.1 %all-to-all-start.1 = ((f32[64,32,256]{2,1,0:T(8,128)}), f32[64,32,256]{2,1,0:T(8,128)S(1)}, u32[]{:S(2)}, u32[]{:S(2)}) async-start(f32[64,32,256]{2,1,0:T(8,128)} %bitcast.6), calls=%async_computation.1 | async-start | bytes 4194304 | tf_op jit(solution)/shard_map/all_to_all | solution.py:113
  66.1 273.6 %all-gather.2.cloned.1.call-start = ((), (), s32[]{:S(2)}) async-start(), calls=%async_computation.3 | async-start | bytes 4259840 | tf_op jit(solution)/shard_map/all_gather | solution.py:150
  68.9 91.9 %copy-start.11 = (f32[512]{0:T(512)S(1)}, f32[512]{0:T(512)}, u32[]{:S(2)}) copy-start(f32[512]{0:T(512)} %param.23) | copy-start | bytes 6148
  159.9 1.8 copy-start.1
  161.7 47.4 %copy-start.8 = (s32[1,20,128]{2,0,1:T(1,128)S(1)}, s32[1,20,128]{2,0,1:T(1,128)}, u32[]{:S(2)}) copy-start(s32[1,20,128]{2,0,1:T(1,128)} %param.17) | copy-start | bytes 30724
  161.7 47.4 %copy-start.2 = (bf16[4,256,256]{2,1,0:T(8,128)(2,1)S(1)}, bf16[4,256,256]{2,1,0:T(8,128)(2,1)}, u32[]{:S(2)}) copy-start(bf16[4,256,256]{2,1,0:T(8,128)(2,1)} %param.25) | copy-start | bytes 1572868
  161.8 12.1 %collective-permute-start = (bf16[128,256]{1,0:T(8,128)(2,1)S(1)}, bf16[128,256]{1,0:T(8,128)(2,1)S(1)}, u32[]{:S(2)}, u32[]{:S(2)}) collective-permute-start(bf16[128,256]{1,0:T(8,128)(2,1)S(1)} %get-tuple-element.6), channel_id=1, source_target_pairs={{0,64},{64,128},{128,192},{192,256},{256,320},{320,384},{384,448},... | collective-permute-start | bytes 196616 | tf_op jit(solution)/shard_map/ppermute | solution.py:14
  174.0 5.6 collective-permute-start.1
  179.7 31.1 %copy-start.9 = (s32[1,2,128]{2,1,0:T(2,128)S(1)}, s32[1,2,128]{2,1,0:T(2,128)}, u32[]{:S(2)}) copy-start(s32[1,2,128]{2,1,0:T(2,128)} %param.15) | copy-start | bytes 3076
  179.7 31.1 %copy-start.6 = (s32[1,20,128]{2,0,1:T(1,128)S(1)}, s32[1,20,128]{2,0,1:T(1,128)}, u32[]{:S(2)}) copy-start(s32[1,20,128]{2,0,1:T(1,128)} %param.16) | copy-start | bytes 30724
  179.7 31.2 %copy-start.7 = (s32[1,1,2048]{2,1,0:T(1,128)S(1)}, s32[1,1,2048]{2,1,0:T(1,128)}, u32[]{:S(2)}) copy-start(s32[1,1,2048]{2,1,0:T(1,128)} %param.19) | copy-start | bytes 24580
  179.7 5.7 collective-permute-start.2
  185.5 5.6 collective-permute-start.3
  191.2 5.6 collective-permute-start.4
  196.9 5.6 collective-permute-start.5
  202.6 5.6 collective-permute-start.6
  208.8 637.1 %all-reduce.3.cloned.1.call-start = ((), (), s32[]{:S(2)}) async-start(), calls=%async_computation.4 | async-start | bytes 1572864 | tf_op jit(solution)/shard_map/psum | solution.py:165
  349.5 9.0 %copy-start.10 = (f32[256]{0:T(256)S(1)}, f32[256]{0:T(256)}, u32[]{:S(2)}) copy-start(f32[256]{0:T(256)} %param.24) | copy-start | bytes 3076
  358.2 10.5 %copy-start.4 = (bf16[256,256]{1,0:T(8,128)(2,1)S(1)}, bf16[256,256]{1,0:T(8,128)(2,1)}, u32[]{:S(2)}) copy-start(bf16[256,256]{1,0:T(8,128)(2,1)} %copy.39) | copy-start | bytes 393220
  368.6 0.9 copy-start.3
  369.2 2.7 copy-start.5
  369.6 2.6 copy-start.12
  369.6 3.4 copy-start.13
Sparse Core Ops, SparseCore 0:
  208.9 130.6 all-gather.1
  375.5 470.3 all-reduce.2
where the time goes:
time: 858 us; the launch traced here: 856 us
  waiting for transfers between devices  718 us (84%)
  starting transfers between devices  66.1 us (8%)
  local copies, waits for them, and re-layouts  26.3 us (3%)
  other arithmetic  22.7 us (3%)
  between operations  14.6 us (2%)
  matrix products  9.08 us (1%)
    psum x1, waiting for transfers between devices, per_device(): grad_out, grad_pair = lax.psum((grad_out, grad_pair), ('tm', 'dp'))  470 us
    all_gather x1, waiting for transfers between devices, per_device(): full_table = lax.all_gather(memory_bf, 'dp', axis=0, tiled=True)  129 us
    all_to_all x1, waiting for transfers between devices, per_device(): lax.all_to_all(slot_sums.reshape(groups, per_owner, feat_width), 'dp', sp...  90.8 us
    ppermute x7, starting transfers between devices, shifted(): lax.ppermute(value, axis, [(source, source + steps) for source in range(i...  36.5 us
    all_to_all x1, starting transfers between devices, per_device(): lax.all_to_all(requests, 'dp', split_axis=0, concat_axis=0, tiled=True)  19.3 us
  transfers between devices with their start and end apart: 12, of which 12 were waited for; matrix products, arithmetic and copies ran while one was open for 1% of the time, Pallas kernels for 0%

commit v1 on v0

--- a/solution.py
+++ b/solution.py
@@ -6,12 +6,6 @@
 from jax.sharding import PartitionSpec as P
 
 HEADS = 2
-
-
-def shifted(value, axis, steps):
-    count = lax.axis_size(axis)
-    initial, last = (max(0, -steps), min(count, count - steps))
-    return lax.ppermute(value, axis, [(source, source + steps) for source in range(initial, last)])
 
 
 def local_step(
@@ -75,6 +69,24 @@
     return (logit_out, grad_out_proj, jnp.stack([grad_first, grad_second]))
 
 
+def exchange(value, axis):
+    return lax.all_to_all(value, axis, split_axis=0, concat_axis=0, tiled=True)
+
+
+def sum_everywhere(grads):
+    parts, spots = lax.axis_size("tm"), lax.axis_size("dp")
+    rows, width = grads.shape
+    own = rows // parts
+    pieces = exchange(grads.astype(jnp.bfloat16).reshape(parts, own, width), "tm")
+    mine = jnp.sum(pieces.astype(jnp.float32), axis=0).astype(jnp.bfloat16)
+    cells = own * width // spots // 128
+    pieces = exchange(mine.reshape(spots, cells, 128), "dp")
+    mine = jnp.sum(pieces.astype(jnp.float32), axis=0).astype(jnp.bfloat16)
+    whole = exchange(jnp.broadcast_to(mine[None], (spots, cells, 128)), "dp")
+    whole = whole.reshape(own, width)
+    return lax.all_gather(whole, "tm", axis=0, tiled=True).astype(jnp.float32)
+
+
 def per_device(
     edge_feat,
     endpoint_slots,
@@ -92,45 +104,36 @@
     pred_out,
 ):
     groups = lax.axis_size("dp")
+    batches = lax.axis_size("tm")
     node_dev, feat_width = memory0.shape
     list_len = node_list.shape[2]
     per_owner = list_len // groups
     requests = node_list[0, 0].reshape(groups, per_owner)
-    wanted = lax.all_to_all(requests, "dp", split_axis=0, concat_axis=0, tiled=True)
     message = jnp.dot(edge_feat[0], msg_weight, preferred_element_type=jnp.float32).astype(
         jnp.bfloat16
     )
-    message_wide = message.astype(jnp.float32)
     end_slots = endpoint_slots[0]
-    flat_ends = end_slots.reshape(-1)
-    slot_sums = (
-        jnp.zeros((list_len, feat_width), jnp.float32)
-        .at[flat_ends]
-        .add(jnp.concatenate([message_wide, message_wide]))
-    )
-    slot_tally = jnp.zeros((list_len,), jnp.float32).at[flat_ends].add(1.0)
-    got_sums, got_tally = (
-        lax.all_to_all(
-            slot_sums.reshape(groups, per_owner, feat_width),
-            "dp",
-            split_axis=0,
-            concat_axis=0,
-            tiled=True,
-        ),
-        lax.all_to_all(
-            slot_tally.reshape(groups, per_owner), "dp", split_axis=0, concat_axis=0, tiled=True
-        ),
-    )
-    picker = (wanted.reshape(-1)[:, None] == jnp.arange(node_dev)[None, :]).astype(jnp.bfloat16)
-    flat_sums = got_sums.reshape(-1, feat_width)
-    sums_high = flat_sums.astype(jnp.bfloat16)
-    sums_low = (flat_sums - sums_high.astype(jnp.float32)).astype(jnp.bfloat16)
+    slot_of = jnp.arange(list_len, dtype=jnp.int32)[:, None]
+    hits = (end_slots[0][None, :] == slot_of).astype(jnp.float32) + (
+        end_slots[1][None, :] == slot_of
+    ).astype(jnp.float32)
+    slot_tally = jnp.sum(hits, axis=1).astype(jnp.int32)
+    slot_sums = jnp.dot(
+        hits.astype(jnp.bfloat16), message, preferred_element_type=jnp.float32
+    ).astype(jnp.bfloat16)
+    small = exchange(
+        jnp.concatenate([requests, slot_tally.reshape(groups, per_owner)], axis=1), "dp"
+    )
+    got_sums = exchange(slot_sums.reshape(groups, per_owner, feat_width), "dp")
+    wanted = small[:, :per_owner].reshape(-1)
+    got_tally = small[:, per_owner:].reshape(-1)
+    picker = (wanted[:, None] == jnp.arange(node_dev)[None, :]).astype(jnp.bfloat16)
     totals = jnp.einsum(
-        "sn,sd->nd", picker, sums_high, preferred_element_type=jnp.float32
-    ) + jnp.einsum("sn,sd->nd", picker, sums_low, preferred_element_type=jnp.float32)
-    counts = jnp.dot(
-        got_tally.reshape(-1), picker.astype(jnp.float32), precision=lax.Precision.HIGHEST
-    )
+        "sn,sd->nd", picker, got_sums.reshape(-1, feat_width), preferred_element_type=jnp.float32
+    )
+    counts = jnp.sum(
+        jnp.where(wanted[:, None] == jnp.arange(node_dev)[None, :], got_tally[:, None], 0), axis=0
+    ).astype(jnp.float32)
     touched = (counts > 0.5).astype(jnp.float32)
     mean_msg = (totals / jnp.maximum(counts, 1.0)[:, None]).astype(jnp.bfloat16)
     pre_gate = jnp.dot(mean_msg, gate_weight, preferred_element_type=jnp.float32) + gate_bias
@@ -139,18 +142,29 @@
     decay_rate = 1.0 - update
     inject = update * candidate
     section_index = lax.axis_index("tm")
-    before = memory0
-    for relay_step in range(lax.axis_size("tm") - 1):
-        moved_state = shifted((decay_rate * before + inject).astype(jnp.bfloat16), "tm", 1).astype(
-            jnp.float32
-        )
-        before = jnp.where(section_index == 0, memory0, moved_state)
+    share = node_dev // batches
+    steps = exchange(
+        jnp.concatenate(
+            [
+                decay_rate.astype(jnp.bfloat16).reshape(batches, share, feat_width),
+                inject.astype(jnp.bfloat16).reshape(batches, share, feat_width),
+            ],
+            axis=1,
+        ),
+        "tm",
+    ).astype(jnp.float32)
+    state = lax.dynamic_slice_in_dim(memory0, section_index * share, share, axis=0)
+    states = []
+    for batch in range(batches):
+        states.append(state.astype(jnp.bfloat16))
+        state = steps[batch, :share] * state + steps[batch, share:]
+    memory_bf = exchange(jnp.stack(states), "tm").reshape(node_dev, feat_width)
+    before = jnp.where(section_index == 0, memory0, memory_bf.astype(jnp.float32))
     new_memory = decay_rate * before + inject
-    memory_bf = before.astype(jnp.bfloat16)
-    full_table = lax.all_gather(memory_bf, "dp", axis=0, tiled=True)
-    owner_of = jnp.arange(list_len, dtype=jnp.int32) // per_owner
-    global_row = owner_of * node_dev + jnp.minimum(node_list[0, 0], node_dev - 1)
-    slot_rows = jnp.take(full_table, global_row, axis=0)
+    sent_rows = jnp.dot(picker, memory_bf, preferred_element_type=jnp.float32).astype(jnp.bfloat16)
+    slot_rows = exchange(sent_rows.reshape(groups, per_owner, feat_width), "dp").reshape(
+        list_len, feat_width
+    )
     logit_out, grad_out, grad_pair = local_step(
         slot_rows,
         end_slots,
@@ -162,8 +176,9 @@
         pred_weights,
         pred_out,
     )
-    grad_out, grad_pair = lax.psum((grad_out, grad_pair), ("tm", "dp"))
-    return (logit_out[None, :], new_memory[None], grad_out, grad_pair)
+    grads = sum_everywhere(jnp.concatenate([grad_out[None], grad_pair]).reshape(-1, feat_width))
+    grads = grads.reshape(3, feat_width, feat_width)
+    return (logit_out[None, :], new_memory[None], grads[0], grads[1:])
 
 
 def solution(mesh):

time: 858 us -> 274 us (0.32)
  waiting for transfers between devices: 718 us -> 142 us
  blocking collectives: 0 us -> 39.7 us
  starting transfers between devices: 66.1 us -> 50.1 us
  between operations: 14.6 us -> 1.11 us
  local copies, waits for them, and re-layouts: 26.3 us -> 14.5 us
    psum x1 -> x0, waiting for transfers between devices: 470 us -> none  [per_device(): grad_out, grad_pair = lax.psum((grad_out, grad_pair), ('tm', 'dp'))]
    all_gather x1 -> x0, waiting for transfers between devices: 129 us -> none  [per_device(): full_table = lax.all_gather(memory_bf, 'dp', axis=0, tiled=True)]
    ppermute x7 -> x0, starting transfers between devices: 36.5 us -> none  [shifted(): lax.ppermute(value, axis, [(source, source + steps) for source in range(i...]
    all_to_all x3 -> x6, waiting for transfers between devices: 110 us -> 142 us  [exchange(): return lax.all_to_all(value, axis, split_axis=0, concat_axis=0, tiled=True)]
    all_to_all x0 -> x2, blocking collectives: none -> 23.3 us  [exchange(): return lax.all_to_all(value, axis, split_axis=0, concat_axis=0, tiled=True)]
    all_to_all x3 -> x6, starting transfers between devices: 29.4 us -> 50.1 us  [exchange(): return lax.all_to_all(value, axis, split_axis=0, concat_axis=0, tiled=True)]
    all_gather x0 -> x1, blocking collectives: none -> 16.4 us  [sum_everywhere(): return lax.all_gather(whole, 'tm', axis=0, tiled=True).astype(jnp.float32)]
    gather x1 -> x0, local copies, waits for them, and re-layouts: 9.36 us -> none  [per_device(): slot_rows = jnp.take(full_table, global_row, axis=0)]
  transfers between devices with their start and end apart: 12 -> 6, of which waited for: 12 -> 6; matrix products, arithmetic and copies ran while one was open for 1% -> 2% of each run, Pallas kernels for 0% -> 0%
where the time goes in v1:
time: 274 us; the launch traced here: 273 us
  waiting for transfers between devices  142 us (52%)
  starting transfers between devices  50.1 us (18%)
  blocking collectives  39.7 us (14%)
  other arithmetic  15.7 us (6%)
  local copies, waits for them, and re-layouts  14.5 us (5%)
  matrix products  9.86 us (4%)
    all_to_all x6, waiting for transfers between devices, exchange(): return lax.all_to_all(value, axis, split_axis=0, concat_axis=0, tiled=True)  142 us
    all_to_all x6, starting transfers between devices, exchange(): return lax.all_to_all(value, axis, split_axis=0, concat_axis=0, tiled=True)  50.1 us
    all_to_all x2, blocking collectives, exchange(): return lax.all_to_all(value, axis, split_axis=0, concat_axis=0, tiled=True)  23.3 us
    all_gather x1, blocking collectives, sum_everywhere(): return lax.all_gather(whole, 'tm', axis=0, tiled=True).astype(jnp.float32)  16.4 us
    convert_element_type x1, other arithmetic, local_step(): (near_rows.astype(jnp.float32) + jnp.cos(phases)).astype(jnp.bfloat16)  10.1 us
    gather x1, local copies, waits for them, and re-layouts, local_step(): jnp.take(slot_rows, near_slots, axis=0)  7.57 us
  transfers between devices with their start and end apart: 6, of which 6 were waited for; matrix products, arithmetic and copies ran while one was open for 2% of the time, Pallas kernels for 0%

profile of v1, /device:TPU:1, one launch (start us, length us, event | category | flops | bytes accessed | tf_op | source)
XLA Modules:
  0.0 273.3 jit_solution(15879573352199052210)
XLA Ops:
  0.6 0.8 slice_bitcast_fusion.24
  2.4 1.4 reduce.7
  3.8 0.7 pad_add_fusion
  4.5 19.3 %all-to-all-start = ((s32[64,1,64]{2,1,0:T(1,128)}), s32[64,1,64]{2,1,0:T(1,128)S(1)}, u32[]{:S(2)}, u32[]{:S(2)}) async-start(s32[64,1,64]{2,1,0:T(1,128)} %bitcast.4), calls=%async_computation | async-start | bytes 65536 | tf_op jit(solution)/shard_map/all_to_all | solution.py:73
  23.8 2.6 convolution_convert_fusion
  26.3 10.8 %all-to-all-done = s32[64,1,64]{2,1,0:T(1,128)S(1)} async-done(((s32[64,1,64]{2,1,0:T(1,128)}), s32[64,1,64]{2,1,0:T(1,128)S(1)}, u32[]{:S(2)}, u32[]{:S(2)}) %all-to-all-start) | async-done | bytes 16416 | tf_op jit(solution)/shard_map/all_to_all | solution.py:73
  37.2 4.7 %all-to-all-start.1 = ((bf16[64,32,256]{2,1,0:T(8,128)(2,1)}), bf16[64,32,256]{2,1,0:T(8,128)(2,1)S(1)}, u32[]{:S(2)}, u32[]{:S(2)}) async-start(bf16[64,32,256]{2,1,0:T(8,128)(2,1)} %bitcast.8), calls=%async_computation.1 | async-start | bytes 2097152 | tf_op jit(solution)/shard_map/all_to_all | solution.py:73
  42.0 1.2 select_reduce_fusion
  43.3 48.9 %all-to-all-done.1 = bf16[64,32,256]{2,1,0:T(8,128)(2,1)S(1)} async-done(((bf16[64,32,256]{2,1,0:T(8,128)(2,1)}), bf16[64,32,256]{2,1,0:T(8,128)(2,1)S(1)}, u32[]{:S(2)}, u32[]{:S(2)}) %all-to-all-start.1) | async-done | bytes 1048608 | tf_op jit(solution)/shard_map/all_to_all | solution.py:73
  92.1 1.0 convolution_add_fusion.1
  93.8 10.3 %all-to-all-start.2 = ((bf16[8,32,256]{2,1,0:T(8,128)(2,1)}), bf16[8,32,256]{2,1,0:T(8,128)(2,1)S(1)}, u32[]{:S(2)}, u32[]{:S(2)}) async-start(bf16[8,32,256]{2,1,0:T(8,128)(2,1)} %pad_maximum_fusion.1), calls=%async_computation.2 | async-start | bytes 262144 | tf_op jit(solution)/shard_map/all_to_all | solution.py:73
  104.1 5.3 %all-to-all-done.2 = bf16[8,32,256]{2,1,0:T(8,128)(2,1)S(1)} async-done(((bf16[8,32,256]{2,1,0:T(8,128)(2,1)}), bf16[8,32,256]{2,1,0:T(8,128)(2,1)S(1)}, u32[]{:S(2)}, u32[]{:S(2)}) %all-to-all-start.2) | async-done | bytes 131104 | tf_op jit(solution)/shard_map/all_to_all | solution.py:73
  109.5 8.1 %all_to_all.47 = bf16[8,16,256]{2,1,0:T(8,128)(2,1)S(1)} all-to-all(bf16[8,16,256]{2,1,0:T(8,128)(2,1)S(1)} %constant_dynamic-update-slice_fusion), channel_id=1, replica_groups=mesh['tm'=8,'dp'=64] {'tm'}, dimensions={0} | all-to-all | bytes 131072 | tf_op jit(solution)/shard_map/all_to_all | solution.py:73
  117.6 1.5 convolution_convert_fusion.1
  119.1 5.7 %all-to-all-start.4 = ((bf16[64,32,256]{2,1,0:T(8,128)(2,1)}), bf16[64,32,256]{2,1,0:T(8,128)(2,1)S(1)}, u32[]{:S(2)}, u32[]{:S(2)}) async-start(bf16[64,32,256]{2,1,0:T(8,128)(2,1)} %bitcast.34), calls=%async_computation.4 | async-start | bytes 2097152 | tf_op jit(solution)/shard_map/all_to_all | solution.py:73
  125.0 0.8 copy.44
  126.0 50.3 %all-to-all-done.4 = bf16[64,32,256]{2,1,0:T(8,128)(2,1)S(1)} async-done(((bf16[64,32,256]{2,1,0:T(8,128)(2,1)}), bf16[64,32,256]{2,1,0:T(8,128)(2,1)S(1)}, u32[]{:S(2)}, u32[]{:S(2)}) %all-to-all-start.4) | async-done | bytes 1048608 | tf_op jit(solution)/shard_map/all_to_all | solution.py:73
  176.3 1.2 gather_fusion
  177.4 7.6 %gather_fusion.1 = bf16[2560,256]{1,0:T(8,128)(2,1)S(1)} fusion(bf16[2048,256]{1,0:T(8,128)(2,1)S(1)} %bitcast.271, s32[3072]{0:T(1024)S(1)} %pad_clamp_fusion), kind=kCustom, calls=%fused_computation.1 | custom fusion | bytes 2631680 | tf_op jit(solution)/shard_map/jit(_take)/gather | solution.py:27
  185.3 10.1 %add_convert_fusion = bf16[20,128,256]{2,1,0:T(8,128)(2,1)S(1)} fusion(f32[256]{0:T(256)S(1)} %copy-done.8, f32[20,128]{1,0:T(8,128)S(1)} %bitcast.289, bf16[20,128,256]{2,1,0:T(8,128)(2,1)S(1)} %bitcast.272, pred[20,128]{1,0:T(8,128)(4,1)S(1)} %compare_and_fusion), kind=kLoop, calls=%fused_computation.4 | loop fusion | flops 3276800 | bytes 2635264 | tf_op jit(solution)/shard_map/convert_element_type | solution.py:29
  196.2 1.1 multiply_reduce_fusion
  197.4 1.1 fusion.1
  198.7 0.8 multiply_convert_fusion
  200.4 15.2 %all_to_all.48 = bf16[8,96,256]{2,1,0:T(8,128)(2,1)S(1)} all-to-all(bf16[8,96,256]{2,1,0:T(8,128)(2,1)S(1)} %bitcast.273), channel_id=1, replica_groups=mesh['tm'=8,'dp'=64] {'tm'}, dimensions={0} | all-to-all | bytes 786432 | tf_op jit(solution)/shard_map/all_to_all | solution.py:73
  216.4 5.6 %all-to-all-start.6 = ((bf16[64,3,128]{2,1,0:T(4,128)(2,1)}), bf16[64,3,128]{2,1,0:T(4,128)(2,1)S(1)}, u32[]{:S(2)}, u32[]{:S(2)}) async-start(bf16[64,3,128]{2,1,0:T(4,128)(2,1)} %reshape.230), calls=%async_computation.6 | async-start | bytes 131072 | tf_op jit(solution)/shard_map/all_to_all | solution.py:73
  222.0 14.0 %all-to-all-done.6 = bf16[64,3,128]{2,1,0:T(4,128)(2,1)S(1)} async-done(((bf16[64,3,128]{2,1,0:T(4,128)(2,1)}), bf16[64,3,128]{2,1,0:T(4,128)(2,1)S(1)}, u32[]{:S(2)}, u32[]{:S(2)}) %all-to-all-start.6) | async-done | bytes 49184 | tf_op jit(solution)/shard_map/all_to_all | solution.py:73
  236.7 4.6 %all-to-all-start.7 = ((bf16[64,3,128]{2,1,0:T(4,128)(2,1)}), bf16[64,3,128]{2,1,0:T(4,128)(2,1)S(1)}, u32[]{:S(2)}, u32[]{:S(2)}) async-start(bf16[64,3,128]{2,1,0:T(4,128)(2,1)} %broadcast_in_dim.73), calls=%async_computation.7 | async-start | bytes 131072 | tf_op jit(solution)/shard_map/all_to_all | solution.py:73
  241.3 0.8 add_bitcast_fusion
  242.1 13.3 %all-to-all-done.7 = bf16[64,3,128]{2,1,0:T(4,128)(2,1)S(1)} async-done(((bf16[64,3,128]{2,1,0:T(4,128)(2,1)}), bf16[64,3,128]{2,1,0:T(4,128)(2,1)S(1)}, u32[]{:S(2)}, u32[]{:S(2)}) %all-to-all-start.7) | async-done | bytes 49184 | tf_op jit(solution)/shard_map/all_to_all | solution.py:73
  255.4 16.4 %all_gather.3 = bf16[768,256]{1,0:T(8,128)(2,1)S(1)} all-gather(bf16[96,256]{1,0:T(8,128)(2,1)S(1)} %reshape.231), channel_id=1, replica_groups=mesh['tm'=8,'dp'=64] {'tm'}, dimensions={0}, use_global_device_ids=true | all-gather | bytes 442368 | tf_op jit(solution)/shard_map/all_gather | solution.py:87
  271.8 0.7 slice.153
  272.5 0.8 slice.154
  (72 shorter events, 6.0 us)
Async XLA Ops:
  0.6 91.5 %copy-start = (bf16[256,512]{1,0:T(8,128)(2,1)S(1)}, bf16[256,512]{1,0:T(8,128)(2,1)}, u32[]{:S(2)}) copy-start(bf16[256,512]{1,0:T(8,128)(2,1)} %param.22) | copy-start | bytes 786436
  4.5 32.7 %all-to-all-start = ((s32[64,1,64]{2,1,0:T(1,128)}), s32[64,1,64]{2,1,0:T(1,128)S(1)}, u32[]{:S(2)}, u32[]{:S(2)}) async-start(s32[64,1,64]{2,1,0:T(1,128)} %bitcast.4), calls=%async_computation | async-start | bytes 65536 | tf_op jit(solution)/shard_map/all_to_all | solution.py:73
  26.3 65.8 %copy-start.9 = (f32[512]{0:T(512)S(1)}, f32[512]{0:T(512)}, u32[]{:S(2)}) copy-start(f32[512]{0:T(512)} %param.23) | copy-start | bytes 6148
  37.2 54.9 %all-to-all-start.1 = ((bf16[64,32,256]{2,1,0:T(8,128)(2,1)}), bf16[64,32,256]{2,1,0:T(8,128)(2,1)S(1)}, u32[]{:S(2)}, u32[]{:S(2)}) async-start(bf16[64,32,256]{2,1,0:T(8,128)(2,1)} %bitcast.8), calls=%async_computation.1 | async-start | bytes 2097152 | tf_op jit(solution)/shard_map/all_to_all | solution.py:73
  92.1 12.0 %copy-start.3 = (f32[128,256]{1,0:T(8,128)S(1)}, f32[128,256]{1,0:T(8,128)}, u32[]{:S(2)}) copy-start(f32[128,256]{1,0:T(8,128)} %param.20) | copy-start | bytes 393220
  93.8 15.5 %all-to-all-start.2 = ((bf16[8,32,256]{2,1,0:T(8,128)(2,1)}), bf16[8,32,256]{2,1,0:T(8,128)(2,1)S(1)}, u32[]{:S(2)}, u32[]{:S(2)}) async-start(bf16[8,32,256]{2,1,0:T(8,128)(2,1)} %pad_maximum_fusion.1), calls=%async_computation.2 | async-start | bytes 262144 | tf_op jit(solution)/shard_map/all_to_all | solution.py:73
  119.1 5.7 %copy-start.6 = (s32[1,20,128]{2,0,1:T(1,128)S(1)}, s32[1,20,128]{2,0,1:T(1,128)}, u32[]{:S(2)}) copy-start(s32[1,20,128]{2,0,1:T(1,128)} %param.17) | copy-start | bytes 30724
  119.1 5.8 %copy-start.2 = (bf16[4,256,256]{2,1,0:T(8,128)(2,1)S(1)}, bf16[4,256,256]{2,1,0:T(8,128)(2,1)}, u32[]{:S(2)}) copy-start(bf16[4,256,256]{2,1,0:T(8,128)(2,1)} %param.25) | copy-start | bytes 1572868
  119.1 57.2 %all-to-all-start.4 = ((bf16[64,32,256]{2,1,0:T(8,128)(2,1)}), bf16[64,32,256]{2,1,0:T(8,128)(2,1)S(1)}, u32[]{:S(2)}, u32[]{:S(2)}) async-start(bf16[64,32,256]{2,1,0:T(8,128)(2,1)} %bitcast.34), calls=%async_computation.4 | async-start | bytes 2097152 | tf_op jit(solution)/shard_map/all_to_all | solution.py:73
  124.8 1.1 copy-start.7
  124.8 1.1 copy-start.5
  177.4 7.9 %copy-start.8 = (f32[256]{0:T(256)S(1)}, f32[256]{0:T(256)}, u32[]{:S(2)}) copy-start(f32[256]{0:T(256)} %param.24) | copy-start | bytes 3076
  185.3 10.1 %copy-start.4 = (bf16[256,256]{1,0:T(8,128)(2,1)S(1)}, bf16[256,256]{1,0:T(8,128)(2,1)}, u32[]{:S(2)}) copy-start(bf16[256,256]{1,0:T(8,128)(2,1)} %copy.44) | copy-start | bytes 393220
  196.1 2.4 copy-start.1
  196.1 2.6 copy-start.10
  196.1 2.6 copy-start.11
  216.4 19.6 %all-to-all-start.6 = ((bf16[64,3,128]{2,1,0:T(4,128)(2,1)}), bf16[64,3,128]{2,1,0:T(4,128)(2,1)S(1)}, u32[]{:S(2)}, u32[]{:S(2)}) async-start(bf16[64,3,128]{2,1,0:T(4,128)(2,1)} %reshape.230), calls=%async_computation.6 | async-start | bytes 131072 | tf_op jit(solution)/shard_map/all_to_all | solution.py:73
  236.7 18.6 %all-to-all-start.7 = ((bf16[64,3,128]{2,1,0:T(4,128)(2,1)}), bf16[64,3,128]{2,1,0:T(4,128)(2,1)S(1)}, u32[]{:S(2)}, u32[]{:S(2)}) async-start(bf16[64,3,128]{2,1,0:T(4,128)(2,1)} %broadcast_in_dim.73), calls=%async_computation.7 | async-start | bytes 131072 | tf_op jit(solution)/shard_map/all_to_all | solution.py:73

commit v2 on v0

v2 whole, which is shorter than its diff:
```python
import math

import jax
import jax.numpy as jnp
from jax import lax
from jax.experimental import pallas as pl
from jax.experimental.pallas import tpu as pltpu
from jax.sharding import PartitionSpec as P

HEADS = 2
LANES = 128
HALF = LANES // 2
NT = (((1,), (1,)), ((), ()))
TN = (((0,), (0,)), ((), ()))
F32 = jnp.float32
BF16 = jnp.bfloat16
PARAMS = pltpu.CompilerParams(vmem_limit_bytes=40 * 1024 * 1024)


def lane_index(shape):
    return lax.broadcasted_iota(jnp.int32, shape, len(shape) - 1)


def dot(left, right, dims=(((1,), (0,)), ((), ()))):
    return lax.dot_general(left, right, dims, preferred_element_type=F32)


def dense_call(body, out_shape, args, scratch=()):
    return pl.pallas_call(
        body,
        out_shape=out_shape,
        in_specs=[pl.BlockSpec(memory_space=pltpu.VMEM)] * len(args),
        scratch_shapes=list(scratch),
        compiler_params=PARAMS,
    )(*args)


def pack_body(feat_ref, ends_ref, list_ref, out_ref, wide_ref):
    rest = feat_ref.shape[0] - LANES
    wide_ref[...] = jnp.zeros_like(wide_ref)
    wide_ref[0:rest, :] = feat_ref[LANES:, :].astype(F32)
    tail = wide_ref[...].astype(BF16)
    empty = jnp.zeros_like(tail)
    tails = jnp.concatenate(
        [
            jnp.concatenate([tail, empty], axis=0),
            jnp.concatenate([empty, tail], axis=0),
        ],
        axis=1,
    )
    head = feat_ref[0:LANES, :]
    per_owner = out_ref.shape[1] * 2 // 3
    low = per_owner // 2
    owners = LANES // per_owner
    slot_of = lax.broadcasted_iota(jnp.int32, (LANES, LANES), 0)
    diagonal = slot_of == lane_index((LANES, LANES))
    ends = ends_ref[...]
    lane = lane_index((1, 1, LANES))
    for block in range(list_ref.shape[1] // LANES):
        hits = jnp.where(ends[0:1, :] == slot_of + block * LANES, 1.0, 0.0) + jnp.where(
            ends[1:2, :] == slot_of + block * LANES, 1.0, 0.0
        )
        tally = jnp.sum(hits, axis=1, keepdims=True).reshape(owners, per_owner, 1)
        named = list_ref[0:1, block * LANES : (block + 1) * LANES].astype(F32)
        named = jnp.sum(jnp.where(diagonal, named, 0.0), axis=1, keepdims=True)
        named = named.reshape(owners, per_owner, 1)
        first = dot(hits.astype(BF16), head, NT).reshape(owners, per_owner, LANES)
        split = hits.reshape(owners, per_owner, LANES)
        both = jnp.concatenate(
            [
                split[:, :low].reshape(owners * low, LANES),
                split[:, low:].reshape(owners * low, LANES),
            ],
            axis=1,
        ).astype(BF16)
        second = dot(both, tails, NT).reshape(owners, low, LANES)
        second = jnp.where(lane == rest, tally[:, :low], second)
        second = jnp.where(lane == rest + 1, named[:, :low], second)
        second = jnp.where(lane == HALF + rest, tally[:, low:], second)
        second = jnp.where(lane == HALF + rest + 1, named[:, low:], second)
        spot = slice(block * owners, (block + 1) * owners)
        out_ref[spot, 0:per_owner, :] = first.astype(BF16)
        out_ref[spot, per_owner:, :] = second.astype(BF16)


def pick(tails, column, nodes):
    column = tails[:, column : column + 1].astype(F32).astype(jnp.int32)
    return jnp.where(column == lane_index((tails.shape[0], nodes)), 1.0, 0.0).astype(BF16)


CHUNK = 16


def mean_body(rest, nodes, got_ref, out_ref):
    low = got_ref.shape[1] // 3
    size = CHUNK * low
    sum_low = jnp.zeros((nodes, 2 * LANES), F32)
    sum_high = jnp.zeros((nodes, 2 * LANES), F32)
    for start in range(0, got_ref.shape[0], CHUNK):
        spot = slice(start, start + CHUNK)
        tails = got_ref[spot, 2 * low :, :].reshape(size, LANES)
        heads = got_ref[spot, 0:low, :].reshape(size, LANES)
        pick_low = pick(tails, rest + 1, nodes)
        sum_low += dot(pick_low, jnp.concatenate([heads, tails], axis=1), TN)
        heads = got_ref[spot, low : 2 * low, :].reshape(size, LANES)
        pick_high = pick(tails, HALF + rest + 1, nodes)
        sum_high += dot(pick_high, jnp.concatenate([heads, tails], axis=1), TN)
    head = sum_low[:, :LANES] + sum_high[:, :LANES]
    tail = sum_low[:, LANES:] + pltpu.roll(sum_high[:, LANES:], HALF, 1)
    count = jnp.maximum(tail[:, rest : rest + 1], 1.0)
    head = head / count
    tail = jnp.where(lane_index(tail.shape) <= rest, tail / count, 0.0)
    cut = nodes // 2
    tail = jnp.where(
        lane_index((cut, LANES)) < HALF, tail[:cut], pltpu.roll(tail[cut:], HALF, 1)
    )
    for part in range(out_ref.shape[0]):
        out_ref[part, 0:nodes, :] = head.astype(BF16)
        out_ref[part, nodes:, :] = tail.astype(BF16)


def rows_body(
    rest,
    section_ref,
    mean_ref,
    got_ref,
    memory_ref,
    head_w_ref,
    low_w_ref,
    high_w_ref,
    gate_ref,
    bias_ref,
    rows_ref,
    memory_out_ref,
):
    nodes, width = memory_ref.shape
    section = section_ref[0]
    cut = nodes // 2
    state = memory_ref[...]
    for batch in range(mean_ref.shape[0]):
        tail = mean_ref[batch, nodes:, :]
        message = dot(mean_ref[batch, 0:nodes, :], head_w_ref[...]) + jnp.concatenate(
            [dot(tail, low_w_ref[...]), dot(tail, high_w_ref[...])], axis=0
        )
        touched = jnp.concatenate(
            [
                tail[:, rest : rest + 1].astype(F32),
                tail[:, HALF + rest : HALF + rest + 1].astype(F32),
            ],
            axis=0,
        )
        gate = dot(message.astype(BF16), gate_ref[...]) + bias_ref[...]
        update = jax.nn.sigmoid(gate[:, :width]) * jnp.where(touched > 0.5, 1.0, 0.0)
        after = (1.0 - update) * state + update * jnp.tanh(gate[:, width:])

        @pl.when(section == batch)
        def _():
            memory_out_ref[...] = after

        state = jnp.where(section > batch, after, state)
    before = state.astype(BF16)
    low = got_ref.shape[1] // 3
    size = CHUNK * low
    for start in range(0, got_ref.shape[0], CHUNK):
        spot = slice(start, start + CHUNK)
        tails = got_ref[spot, 2 * low :, :].reshape(size, LANES)
        rows = dot(pick(tails, rest + 1, nodes), before).astype(BF16)
        rows_ref[spot, 0:low, :] = rows.reshape(CHUNK, low, width)
        rows = dot(pick(tails, HALF + rest + 1, nodes), before).astype(BF16)
        rows_ref[spot, low:, :] = rows.reshape(CHUNK, low, width)


def event_body(
    rows_ref,
    ends_ref,
    near_ref,
    cos_ref,
    cot_ref,
    attn_ref,
    pred_ref,
    pred_flip_ref,
    pred_out_ref,
    scores_ref,
    grads_ref,
    flip_ref,
    value_ref,
):
    slots, width = rows_ref.shape
    events = ends_ref.shape[1]
    near_count = near_ref.shape[0] // 2
    pair = 2 * events
    head_dim = width // HEADS
    for start in range(0, slots, width):
        flip_ref[:, start : start + width] = rows_ref[start : start + width, :].T
    slot_of = lax.broadcasted_iota(jnp.int32, (slots, pair), 0)

    def fetch(index):
        return dot(flip_ref[...], jnp.where(slot_of == index, 1.0, 0.0).astype(BF16))

    own = fetch(jnp.concatenate([ends_ref[0:1, :], ends_ref[1:2, :]], axis=1))
    query = dot(attn_ref[0], own.astype(BF16)) * (1.0 / math.sqrt(head_dim))
    logits = []
    for near in range(near_count):
        index = jnp.concatenate(
            [near_ref[near : near + 1, :], near_ref[near_count + near : near_count + near + 1, :]],
            axis=1,
        )
        feat = fetch(index) + cos_ref[:, near * pair : (near + 1) * pair]
        feat = feat.astype(BF16)
        match = query * dot(attn_ref[1], feat)
        logits.append(
            [
                jnp.sum(match[head * head_dim : (head + 1) * head_dim], axis=0, keepdims=True)
                for head in range(HEADS)
            ]
        )
        value_ref[near] = dot(attn_ref[2], feat)
    mixed = []
    for head in range(HEADS):
        top = logits[0][head]
        for near in range(1, near_count):
            top = jnp.maximum(top, logits[near][head])
        powers = [jnp.exp(logits[near][head] - top) for near in range(near_count)]
        total = powers[0]
        for near in range(1, near_count):
            total = total + powers[near]
        spot = slice(head * head_dim, (head + 1) * head_dim)
        part = (powers[0] / total) * value_ref[0, spot, :]
        for near in range(1, near_count):
            part = part + (powers[near] / total) * value_ref[near, spot, :]
        mixed.append(part)
    mixed = jnp.concatenate(mixed, axis=0).astype(BF16)
    state = (own + dot(attn_ref[3], mixed)).astype(BF16)
    source, target = state[:, :events], state[:, events:]
    pre = dot(pred_flip_ref[0], source) + dot(pred_flip_ref[1], target)
    gate = jax.nn.sigmoid(pre)
    pred_out = pred_out_ref[...]
    scores_ref[...] = jnp.sum(pre * gate * pred_out, axis=0, keepdims=True)
    slope = (cot_ref[...] * pred_out * (gate * (1.0 + pre * (1.0 - gate)))).astype(BF16)
    back = jnp.concatenate([dot(pred_ref[0], slope), dot(pred_ref[1], slope)], axis=1)
    grads_ref[0:width, :] = dot(mixed, back.astype(BF16), NT).astype(BF16)
    grads_ref[width : 2 * width, :] = dot(source, slope, NT).astype(BF16)
    grads_ref[2 * width :, :] = dot(target, slope, NT).astype(BF16)


def exchange(value, axis, groups=None):
    return lax.all_to_all(
        value, axis, split_axis=0, concat_axis=0, tiled=True, axis_index_groups=groups
    )


def sum_everywhere(grads, columns, rings):
    plane = [
        [section * columns * rings + ring * columns + column for section in range(lax.axis_size("tm")) for column in range(columns)]
        for ring in range(rings)
    ]
    line = [[ring * columns + column for ring in range(rings)] for column in range(columns)]
    peers = len(plane[0])
    rows, width = grads.shape
    own = rows // peers
    pieces = exchange(grads.reshape(peers, own, width), ("tm", "dp"), plane)
    mine = jnp.sum(pieces.astype(F32), axis=0).astype(BF16)
    pieces = exchange(jnp.broadcast_to(mine[None], (rings, own, width)), "dp", line)
    mine = jnp.sum(pieces.astype(F32), axis=0).astype(BF16)
    whole = exchange(jnp.broadcast_to(mine[None], (peers, own, width)), ("tm", "dp"), plane)
    return whole.reshape(rows, width).astype(F32)


def per_device(
    edge_feat,
    endpoint_slots,
    neighbor_slots,
    neighbor_gap,
    score_grad,
    node_list,
    memory0,
    msg_weight,
    gate_weight,
    gate_bias,
    omega,
    attn_weights,
    pred_weights,
    pred_out,
):
    groups = lax.axis_size("dp")
    batches = lax.axis_size("tm")
    nodes, width = memory0.shape
    list_len = node_list.shape[2]
    per_owner = list_len // groups
    features = edge_feat.shape[2]
    rest = features - LANES
    events = endpoint_slots.shape[2]
    near_count = neighbor_slots.shape[1] // 2
    sent = dense_call(
        pack_body,
        jax.ShapeDtypeStruct((groups, per_owner * 3 // 2, LANES), BF16),
        (jnp.swapaxes(edge_feat[0], 0, 1), endpoint_slots[0], node_list[0]),
        [pltpu.VMEM((HALF, LANES), F32)],
    )
    got = exchange(sent, "dp")
    gaps = neighbor_gap[0].reshape(2, near_count, events)
    gaps = jnp.swapaxes(gaps, 0, 1).reshape(1, 2 * near_count * events).astype(F32)
    cosines = lax.optimization_barrier(jnp.cos(omega[:, None] * gaps))
    means = dense_call(
        lambda *refs: mean_body(rest, nodes, *refs),
        jax.ShapeDtypeStruct((batches, nodes + nodes // 2, LANES), BF16),
        (got,),
    )
    means = exchange(means, "tm")
    tail_w = jnp.pad(msg_weight[LANES:], ((0, HALF - rest), (0, 0)))
    section = lax.axis_index("tm").astype(jnp.int32)
    rows, new_memory = pl.pallas_call(
        lambda *refs: rows_body(rest, *refs),
        out_shape=(
            jax.ShapeDtypeStruct((groups, per_owner, width), BF16),
            jax.ShapeDtypeStruct((nodes, width), F32),
        ),
        in_specs=[pl.BlockSpec(memory_space=pltpu.SMEM)]
        + [pl.BlockSpec(memory_space=pltpu.VMEM)] * 8,
        compiler_params=PARAMS,
    )(
        section[None],
        means,
        got,
        memory0,
        msg_weight[:LANES],
        jnp.pad(tail_w, ((0, HALF), (0, 0))),
        jnp.pad(tail_w, ((HALF, 0), (0, 0))),
        gate_weight,
        gate_bias[None],
    )
    slot_rows = exchange(rows, "dp").reshape(list_len, width)
    scores, grads = dense_call(
        event_body,
        (
            jax.ShapeDtypeStruct((1, events), F32),
            jax.ShapeDtypeStruct((3 * width, width), BF16),
        ),
        (
            slot_rows,
            endpoint_slots[0],
            neighbor_slots[0],
            cosines,
            score_grad,
            jnp.swapaxes(attn_weights, 1, 2),
            pred_weights,
            jnp.swapaxes(pred_weights, 1, 2),
            pred_out[:, None],
        ),
        [
            pltpu.VMEM((width, list_len), BF16),
            pltpu.VMEM((near_count, width, 2 * events), F32),
        ],
    )
    columns = 4
    grads = sum_everywhere(grads, columns, groups // columns)
    grads = grads.reshape(3, width, width)
    return (scores, new_memory[None], grads[0], grads[1:])


def solution(mesh):
    in_specs = (
        P("tm", "dp", None),
        P("tm", None, "dp"),
        P("tm", None, "dp"),
        P("tm", None, "dp"),
        P("tm", "dp"),
        P("tm", "dp", None),
        P("dp", None),
        P(),
        P(),
        P(),
        P(),
        P(),
        P(),
        P(),
    )
    out_specs = (P("tm", "dp"), P("tm", "dp", None), P(), P())
    return jax.shard_map(
        per_device, mesh=mesh, in_specs=in_specs, out_specs=out_specs, check_vma=False
    )
```

time: 858 us -> 211 us (0.25)
  waiting for transfers between devices: 718 us -> 48.1 us
  blocking collectives: 0 us -> 112 us
  starting transfers between devices: 66.1 us -> 14.8 us
  local copies, waits for them, and re-layouts: 26.3 us -> 7.28 us
  Pallas kernels: 0 us -> 18.2 us
  between operations: 14.6 us -> 0.83 us
  other arithmetic: 22.7 us -> 9.33 us
  matrix products: 9.08 us -> 0 us
    psum x1 -> x0, waiting for transfers between devices: 470 us -> none  [per_device(): grad_out, grad_pair = lax.psum((grad_out, grad_pair), ('tm', 'dp'))]
    all_gather x1 -> x0, waiting for transfers between devices: 129 us -> none  [per_device(): full_table = lax.all_gather(memory_bf, 'dp', axis=0, tiled=True)]
    all_to_all x0 -> x4, blocking collectives: none -> 112 us  [exchange(): lax.all_to_all(value, axis, split_axis=0, concat_axis=0, tiled=True, axis...]
    all_to_all x3 -> x2, waiting for transfers between devices: 110 us -> 48.1 us  [exchange(): lax.all_to_all(value, axis, split_axis=0, concat_axis=0, tiled=True, axis...]
    ppermute x7 -> x0, starting transfers between devices: 36.5 us -> none  [shifted(): lax.ppermute(value, axis, [(source, source + steps) for source in range(i...]
    pallas_call x0 -> x4, Pallas kernels: none -> 18.2 us  [the longest x3 13.8 us: dense_call(): pl.pallas_call(body, out_shape=out_shape, in_specs=[pl.BlockSpec(memory_s...]
    gather x3 -> x0, local copies, waits for them, and re-layouts: 18.1 us -> none  [the longest x1 9.36 us: per_device(): slot_rows = jnp.take(full_table, global_row, axis=0)]
    all_to_all x3 -> x2, starting transfers between devices: 29.4 us -> 14.8 us  [exchange(): lax.all_to_all(value, axis, split_axis=0, concat_axis=0, tiled=True, axis...]
  transfers between devices with their start and end apart: 12 -> 2, of which waited for: 12 -> 2; matrix products, arithmetic and copies ran while one was open for 1% -> 5% of each run, Pallas kernels for 0% -> 0%
where the time goes in v2:
time: 211 us
  blocking collectives  112 us (53%)
  waiting for transfers between devices  48.1 us (23%)
  Pallas kernels  18.2 us (9%)
  starting transfers between devices  14.8 us (7%)
  other arithmetic  9.33 us (4%)
  local copies, waits for them, and re-layouts  7.28 us (3%)
    all_to_all x4, blocking collectives, exchange(): lax.all_to_all(value, axis, split_axis=0, concat_axis=0, tiled=True, axis...  112 us
    all_to_all x2, waiting for transfers between devices, exchange(): lax.all_to_all(value, axis, split_axis=0, concat_axis=0, tiled=True, axis...  48.1 us
    all_to_all x2, starting transfers between devices, exchange(): lax.all_to_all(value, axis, split_axis=0, concat_axis=0, tiled=True, axis...  14.8 us
    pallas_call x3, Pallas kernels, dense_call(): pl.pallas_call(body, out_shape=out_shape, in_specs=[pl.BlockSpec(memory_s...  13.8 us
    cos x1, other arithmetic, per_device(): cosines = lax.optimization_barrier(jnp.cos(omega[:, None] * gaps))  9.11 us
    unnamed x33, local copies, waits for them, and re-layouts  4.91 us
    pallas_call x1, Pallas kernels, per_device(): pl.pallas_call(lambda *refs: rows_body(rest, *refs), out_shape=(jax.Shape...  4.43 us
  transfers between devices with their start and end apart: 2, of which 2 were waited for; matrix products, arithmetic and copies ran while one was open for 5% of the time, Pallas kernels for 0%

profile of v2, /device:TPU:1, one launch (start us, length us, event | category | flops | bytes accessed | tf_op | source)
XLA Modules:
  0.0 210.6 jit_solution(7909974680856842258)
XLA Ops:
  0.7 0.8 copy-done.4
  1.5 0.7 copy-done.5
  2.2 0.7 copy-done.6
  2.9 0.8 shard_map.165
  3.7 59.8 %all_to_all.30.refs_0_.refs_2_ = bf16[64,48,128]{2,1,0:T(8,128)(2,1)S(1)} all-to-all(bf16[64,48,128]{2,1,0:T(8,128)(2,1)S(1)} %shard_map.165), channel_id=1, replica_groups=mesh['tm'=8,'dp'=64] {'dp'}, dimensions={0} | all-to-all | bytes 1572864 | tf_op jit(solution)/shard_map/all_to_all | solution.py:247
  63.5 1.8 shard_map.166
  65.3 8.8 %all-to-all-start.1 = ((bf16[8,192,128]{2,1,0:T(8,128)(2,1)}), bf16[8,192,128]{2,1,0:T(8,128)(2,1)S(1)}, u32[]{:S(2)}, u32[]{:S(2)}) async-start(bf16[8,192,128]{2,1,0:T(8,128)(2,1)} %shard_map.166), calls=%async_computation.1 | async-start | bytes 786432 | tf_op jit(solution)/shard_map/all_to_all | solution.py:247
  74.2 8.0 %all-to-all-done.1.refs_1_ = bf16[8,192,128]{2,1,0:T(8,128)(2,1)S(1)} async-done(((bf16[8,192,128]{2,1,0:T(8,128)(2,1)}), bf16[8,192,128]{2,1,0:T(8,128)(2,1)S(1)}, u32[]{:S(2)}, u32[]{:S(2)}) %all-to-all-start.1) | async-done | bytes 393248 | tf_op jit(solution)/shard_map/all_to_all | solution.py:247
  82.2 0.0 copy-done.2
  82.2 0.0 copy-done.8
  82.2 4.4 %shard_map.167 = (bf16[64,32,256]{2,1,0:T(8,128)(2,1)}, f32[128,256]{1,0:T(8,128)}) custom-call(s32[1]{0:T(128)} %bitcast.refs_0_, bf16[8,192,128]{2,1,0:T(8,128)(2,1)S(1)} %all-to-all-done.1.refs_1_, bf16[64,48,128]{2,1,0:T(8,128)(2,1)S(1)} %all_to_all.30.refs_0_.refs_2_, f32[128,256]{1,0:T(8,128)S(1)} %copy-done.3, bf16[128,256]{1,0:T(8,128)(2,1)S(1)} %slice.16.refs_4_, ...), custom_call_target="tpu_custom_call" | custom-call | tf_op jit(solution)/shard_map/pallas_call | solution.py:312
  86.6 6.0 %all-to-all-start.2 = ((bf16[64,32,256]{2,1,0:T(8,128)(2,1)}), bf16[64,32,256]{2,1,0:T(8,128)(2,1)}, u32[]{:S(2)}, u32[]{:S(2)}) async-start(bf16[64,32,256]{2,1,0:T(8,128)(2,1)} %get-tuple-element.8), calls=%async_computation.2 | async-start | bytes 2097152 | tf_op jit(solution)/shard_map/all_to_all | solution.py:247
  92.6 0.0 copy-start.7
  92.7 0.6 convert_element_type.36
  93.3 0.0 copy-done.14
  93.3 0.1 copy.27.pred_out_ref
  93.5 0.8 copy.26
  94.3 0.0 copy-done.10
  94.3 0.2 copy.25
  94.5 9.1 %multiply_cosine_fusion.cos_ref = f32[256,2560]{1,0:T(8,128)S(1)} fusion(f32[2560]{0:T(1024)} %convert_element_type.36, f32[256]{0:T(256)} %param.24), kind=kLoop, calls=%fused_computation | loop fusion | flops 655360 | bytes 2632704 | tf_op jit(solution)/shard_map/cos | solution.py:303
  103.7 40.1 %all-to-all-done.2 = bf16[64,32,256]{2,1,0:T(8,128)(2,1)} async-done(((bf16[64,32,256]{2,1,0:T(8,128)(2,1)}), bf16[64,32,256]{2,1,0:T(8,128)(2,1)}, u32[]{:S(2)}, u32[]{:S(2)}) %all-to-all-start.2) | async-done | bytes 1048608 | tf_op jit(solution)/shard_map/all_to_all | solution.py:247
  143.8 0.0 copy-done.7
  143.8 0.9 copy-done.1
  144.7 0.7 copy-done.9
  145.4 11.1 %shard_map.168 = (f32[1,128]{1,0:T(1,128)}, bf16[768,256]{1,0:T(8,128)(2,1)S(1)}) custom-call(bf16[2048,256]{1,0:T(8,128)(2,1)} %bitcast.6.rows_ref, s32[2,128]{1,0:T(2,128)S(1)} %bitcast.30, s32[20,128]{1,0:T(8,128)S(1)} %bitcast.26, f32[256,2560]{1,0:T(8,128)S(1)} %multiply_cosine_fusion.cos_ref, f32[1,128]{1,0:T(1,128)S(1)} %copy-done.9, ...), custom_call_target="tpu_custom_call" | custom-call | tf_op jit(solution)/shard_map/pallas_call | solution.py:29
  156.5 19.6 %all_to_all.31 = bf16[32,24,256]{2,1,0:T(8,128)(2,1)S(1)} all-to-all(bf16[32,24,256]{2,1,0:T(8,128)(2,1)S(1)} %bitcast.25), channel_id=1, replica_groups={{0,1,2,3,64,65,66,67,128,129,130,131,192,193,194,195,256,257,258,259,32..., dimensions={0} | all-to-all | bytes 786432 | tf_op jit(solution)/shard_map/all_to_all | solution.py:247
  176.1 0.1 reduce_sum.24
  176.2 15.4 %all_to_all.32 = bf16[16,24,256]{2,1,0:T(8,128)(2,1)S(1)} all-to-all(bf16[16,24,256]{2,1,0:T(8,128)(2,1)S(1)} %broadcast_in_dim.29), channel_id=1, replica_groups={{0,4,8,12,16,20,24,28,32,36,40,44,48,52,56,60},{1,5,9,13,17,21,25,29,33..., dimensions={0} | all-to-all | bytes 393216 | tf_op jit(solution)/shard_map/all_to_all | solution.py:247
  191.7 17.2 %all_to_all.33 = bf16[32,24,256]{2,1,0:T(8,128)(2,1)S(1)} all-to-all(bf16[32,24,256]{2,1,0:T(8,128)(2,1)S(1)} %broadcast_in_dim.30), channel_id=1, replica_groups={{0,1,2,3,64,65,66,67,128,129,130,131,192,193,194,195,256,257,258,259,32..., dimensions={0} | all-to-all | bytes 786432 | tf_op jit(solution)/shard_map/all_to_all | solution.py:247
  208.9 0.1 bitcast_convert_fusion
  209.0 0.7 slice.21
  209.7 0.8 slice.22
  (31 shorter events, 0.2 us)
Async XLA Ops:
  0.6 81.5 %copy-start.2 = (bf16[256,512]{1,0:T(8,128)(2,1)S(1)}, bf16[256,512]{1,0:T(8,128)(2,1)}, u32[]{:S(2)}) copy-start(bf16[256,512]{1,0:T(8,128)(2,1)} %refs_7_.1) | copy-start | bytes 786436
  0.6 81.5 %copy-start.3 = (f32[128,256]{1,0:T(8,128)S(1)}, f32[128,256]{1,0:T(8,128)}, u32[]{:S(2)}) copy-start(f32[128,256]{1,0:T(8,128)} %refs_3_.1) | copy-start | bytes 393220
  0.7 0.8 copy-start.4
  1.5 0.7 copy-start.5
  2.2 0.7 copy-start.6
  2.9 71.2 %copy-start.11 = (bf16[186,256]{1,0:T(8,128)(2,1)S(1)}, bf16[186,256]{1,0:T(8,128)(2,1)}, u32[]{:S(2)}) copy-start(bf16[186,256]{1,0:T(8,128)(2,1)} %param.21) | copy-start | bytes 285700
  2.9 71.2 %slice-start = ((bf16[186,256]{1,0:T(8,128)(2,1)}), bf16[58,256]{1,0:T(8,128)(2,1)S(1)}, s32[]{:S(2)}) async-start(bf16[186,256]{1,0:T(8,128)(2,1)} %param.21), calls=%async_computation.6 | async-start | bytes 65536 | tf_op jit(solution)/shard_map/slice | solution.py:310
  2.9 79.3 %copy-start.8 = (f32[512]{0:T(512)S(1)}, f32[512]{0:T(512)}, u32[]{:S(2)}) copy-start(f32[512]{0:T(512)} %param.23) | copy-start | bytes 6148
  65.3 27.3 %copy-start.12 = (s32[1,20,128]{2,0,1:T(1,128)S(1)}, s32[1,20,128]{2,0,1:T(1,128)}, u32[]{:S(2)}) copy-start(s32[1,20,128]{2,0,1:T(1,128)} %param.16) | copy-start | bytes 30724
  65.3 27.3 %copy-start.13 = (s32[1,20,128]{2,0,1:T(1,128)S(1)}, s32[1,20,128]{2,0,1:T(1,128)}, u32[]{:S(2)}) copy-start(s32[1,20,128]{2,0,1:T(1,128)} %param.17) | copy-start | bytes 30724
  65.3 28.0 %copy-start.14 = (f32[256]{0:T(256)S(1)}, f32[256]{0:T(256)}, u32[]{:S(2)}) copy-start(f32[256]{0:T(256)} %param.27) | copy-start | bytes 3076
  65.3 28.2 %copy-start = (bf16[2,256,256]{2,1,0:T(8,128)(2,1)S(1)}, bf16[2,256,256]{2,1,0:T(8,128)(2,1)}, u32[]{:S(2)}) copy-start(bf16[2,256,256]{2,1,0:T(8,128)(2,1)} %pred_ref.1) | copy-start | bytes 786436
  65.3 16.8 %all-to-all-start.1 = ((bf16[8,192,128]{2,1,0:T(8,128)(2,1)}), bf16[8,192,128]{2,1,0:T(8,128)(2,1)S(1)}, u32[]{:S(2)}, u32[]{:S(2)}) async-start(bf16[8,192,128]{2,1,0:T(8,128)(2,1)} %shard_map.166), calls=%async_computation.1 | async-start | bytes 786432 | tf_op jit(solution)/shard_map/all_to_all | solution.py:247
  74.1 20.2 %copy-start.10 = (bf16[4,256,256]{2,1,0:T(8,128)(2,1)S(1)}, bf16[4,256,256]{2,1,0:T(8,128)(2,1)}, u32[]{:S(2)}) copy-start(bf16[4,256,256]{2,1,0:T(8,128)(2,1)} %param.25) | copy-start | bytes 1572868
  86.6 57.2 %all-to-all-start.2 = ((bf16[64,32,256]{2,1,0:T(8,128)(2,1)}), bf16[64,32,256]{2,1,0:T(8,128)(2,1)}, u32[]{:S(2)}, u32[]{:S(2)}) async-start(bf16[64,32,256]{2,1,0:T(8,128)(2,1)} %get-tuple-element.8), calls=%async_computation.2 | async-start | bytes 2097152 | tf_op jit(solution)/shard_map/all_to_all | solution.py:247
  92.6 51.2 %copy-start.7 = (s32[1,2,128]{2,1,0:T(2,128)S(1)}, s32[1,2,128]{2,1,0:T(2,128)}, u32[]{:S(2)}) copy-start(s32[1,2,128]{2,1,0:T(2,128)} %param.15) | copy-start | bytes 3076
  143.8 1.0 copy-start.1
  144.7 0.7 copy-start.9

commit v3 on v2

v3 whole, which is shorter than its diff:
```python
import math

import jax
import jax.numpy as jnp
from jax import lax
from jax.experimental import pallas as pl
from jax.experimental.pallas import tpu as pltpu
from jax.sharding import PartitionSpec as P

HEADS = 2
LANES = 128
HALF = LANES // 2
NT = (((1,), (1,)), ((), ()))
TN = (((0,), (0,)), ((), ()))
F32 = jnp.float32
BF16 = jnp.bfloat16
PARAMS = pltpu.CompilerParams(vmem_limit_bytes=12 * 1024 * 1024)
ALONE = pltpu.CompilerParams(vmem_limit_bytes=63 * 1024 * 1024)


def lane_index(shape):
    return lax.broadcasted_iota(jnp.int32, shape, len(shape) - 1)


def dot(left, right, dims=(((1,), (0,)), ((), ()))):
    return lax.dot_general(left, right, dims, preferred_element_type=F32)


def dense_call(body, out_shape, args, scratch=()):
    return pl.pallas_call(
        body,
        out_shape=out_shape,
        in_specs=[pl.BlockSpec(memory_space=pltpu.VMEM)] * len(args),
        scratch_shapes=list(scratch),
        compiler_params=PARAMS,
    )(*args)


def copies(sources, targets, sems):
    return [
        pltpu.make_async_copy(source, target, sems.at[index])
        for index, (source, target) in enumerate(zip(sources, targets))
    ]


def load(sources, targets, sems):
    started = copies(sources, targets, sems)
    for copy in started:
        copy.start()
    for copy in started:
        copy.wait()


def pack_body(feat_hbm, ends_hbm, list_hbm, out_ref, wide_ref, feat_ref, ends_ref, list_ref, sems):
    load((feat_hbm, ends_hbm, list_hbm), (feat_ref, ends_ref, list_ref), sems)
    rest = feat_ref.shape[0] - LANES
    wide_ref[...] = jnp.zeros_like(wide_ref)
    wide_ref[0:rest, :] = feat_ref[LANES:, :].astype(F32)
    tail = wide_ref[...].astype(BF16)
    empty = jnp.zeros_like(tail)
    tails = jnp.concatenate(
        [
            jnp.concatenate([tail, empty], axis=0),
            jnp.concatenate([empty, tail], axis=0),
        ],
        axis=1,
    )
    head = feat_ref[0:LANES, :]
    per_owner = out_ref.shape[1] * 2 // 3
    low = per_owner // 2
    owners = LANES // per_owner
    slot_of = lax.broadcasted_iota(jnp.int32, (LANES, LANES), 0)
    diagonal = slot_of == lane_index((LANES, LANES))
    ends = ends_ref[...]
    lane = lane_index((1, 1, LANES))
    for block in range(list_ref.shape[1] // LANES):
        hits = jnp.where(ends[0:1, :] == slot_of + block * LANES, 1.0, 0.0) + jnp.where(
            ends[1:2, :] == slot_of + block * LANES, 1.0, 0.0
        )
        tally = jnp.sum(hits, axis=1, keepdims=True).reshape(owners, per_owner, 1)
        named = list_ref[0:1, block * LANES : (block + 1) * LANES].astype(F32)
        named = jnp.sum(jnp.where(diagonal, named, 0.0), axis=1, keepdims=True)
        named = named.reshape(owners, per_owner, 1)
        first = dot(hits.astype(BF16), head, NT).reshape(owners, per_owner, LANES)
        split = hits.reshape(owners, per_owner, LANES)
        both = jnp.concatenate(
            [
                split[:, :low].reshape(owners * low, LANES),
                split[:, low:].reshape(owners * low, LANES),
            ],
            axis=1,
        ).astype(BF16)
        second = dot(both, tails, NT).reshape(owners, low, LANES)
        second = jnp.where(lane == rest, tally[:, :low], second)
        second = jnp.where(lane == rest + 1, named[:, :low], second)
        second = jnp.where(lane == HALF + rest, tally[:, low:], second)
        second = jnp.where(lane == HALF + rest + 1, named[:, low:], second)
        spot = slice(block * owners, (block + 1) * owners)
        out_ref[spot, 0:per_owner, :] = first.astype(BF16)
        out_ref[spot, per_owner:, :] = second.astype(BF16)


def pick(tails, column, nodes):
    column = tails[:, column : column + 1].astype(F32).astype(jnp.int32)
    return jnp.where(column == lane_index((tails.shape[0], nodes)), 1.0, 0.0).astype(BF16)


CHUNK = 16


def mean_body(rest, nodes, got_ref, out_ref):
    low = got_ref.shape[1] // 3
    size = CHUNK * low
    sum_low = jnp.zeros((nodes, 2 * LANES), F32)
    sum_high = jnp.zeros((nodes, 2 * LANES), F32)
    for start in range(0, got_ref.shape[0], CHUNK):
        spot = slice(start, start + CHUNK)
        tails = got_ref[spot, 2 * low :, :].reshape(size, LANES)
        heads = got_ref[spot, 0:low, :].reshape(size, LANES)
        pick_low = pick(tails, rest + 1, nodes)
        sum_low += dot(pick_low, jnp.concatenate([heads, tails], axis=1), TN)
        heads = got_ref[spot, low : 2 * low, :].reshape(size, LANES)
        pick_high = pick(tails, HALF + rest + 1, nodes)
        sum_high += dot(pick_high, jnp.concatenate([heads, tails], axis=1), TN)
    head = sum_low[:, :LANES] + sum_high[:, :LANES]
    tail = sum_low[:, LANES:] + pltpu.roll(sum_high[:, LANES:], HALF, 1)
    count = jnp.maximum(tail[:, rest : rest + 1], 1.0)
    head = head / count
    tail = jnp.where(lane_index(tail.shape) <= rest, tail / count, 0.0)
    cut = nodes // 2
    tail = jnp.where(
        lane_index((cut, LANES)) < HALF, tail[:cut], pltpu.roll(tail[cut:], HALF, 1)
    )
    for part in range(out_ref.shape[0]):
        out_ref[part, 0:nodes, :] = head.astype(BF16)
        out_ref[part, nodes:, :] = tail.astype(BF16)


def gates(rest, head, tail, head_w_ref, low_w_ref, high_w_ref, gate_ref, bias_ref):
    width = head_w_ref.shape[1]
    message = dot(head, head_w_ref[...]) + jnp.concatenate(
        [dot(tail, low_w_ref[...]), dot(tail, high_w_ref[...])], axis=0
    )
    touched = jnp.concatenate(
        [
            tail[:, rest : rest + 1].astype(F32),
            tail[:, HALF + rest : HALF + rest + 1].astype(F32),
        ],
        axis=0,
    )
    gate = dot(message.astype(BF16), gate_ref[...]) + bias_ref[...]
    update = jax.nn.sigmoid(gate[:, :width]) * jnp.where(touched > 0.5, 1.0, 0.0)
    return 1.0 - update, update * jnp.tanh(gate[:, width:])


def advance(rest, section, mean_ref, batches, memory_ref, weights):
    nodes = memory_ref.shape[0]
    state = memory_ref[...]
    for batch in range(batches):
        head, tail = mean_ref[batch, 0:nodes, :], mean_ref[batch, nodes:, :]
        decay, inject = gates(rest, head, tail, *weights)
        state = jnp.where(section > batch, decay * state + inject, state)
    return state


def rows_body(rest, section_ref, mean_ref, got_ref, memory_ref, *refs):
    weights, rows_ref = refs[:-1], refs[-1]
    nodes, width = memory_ref.shape
    batches = mean_ref.shape[0] - 1
    before = advance(rest, section_ref[0], mean_ref, batches, memory_ref, weights).astype(BF16)
    low = got_ref.shape[1] // 3
    size = CHUNK * low
    for start in range(0, got_ref.shape[0], CHUNK):
        spot = slice(start, start + CHUNK)
        tails = got_ref[spot, 2 * low :, :].reshape(size, LANES)
        rows = dot(pick(tails, rest + 1, nodes), before).astype(BF16)
        rows_ref[spot, 0:low, :] = rows.reshape(CHUNK, low, width)
        rows = dot(pick(tails, HALF + rest + 1, nodes), before).astype(BF16)
        rows_ref[spot, low:, :] = rows.reshape(CHUNK, low, width)


def memory_body(rest, section_ref, mean_ref, memory_ref, *refs):
    weights, out_ref = refs[:-1], refs[-1]
    out_ref[...] = advance(rest, section_ref[0] + 1, mean_ref, mean_ref.shape[0], memory_ref, weights)


def event_body(*refs):
    sources, (scores_ref, grads_ref), targets = refs[:8], refs[8:10], refs[10:18]
    feat_ref, sems = refs[18:]
    rows_ref, ends_ref, near_ref, cos_ref, cot_ref, attn_ref, pred_ref, pred_out_ref = targets
    started = copies(sources, targets, sems)
    rows_copy, ends_copy, near_copy, cos_copy, cot_copy, attn_copy, pred_copy, out_copy = started
    for copy in (ends_copy, rows_copy, near_copy, cos_copy, attn_copy, cot_copy, out_copy, pred_copy):
        copy.start()
    ends_copy.wait()
    rows_copy.wait()
    slots, width = rows_ref.shape
    events = ends_ref.shape[1]
    pair = 2 * events
    near_count = near_ref.shape[0] // 2
    head_dim = width // HEADS
    diagonal = lax.broadcasted_iota(jnp.int32, (events, events), 0) == lane_index((events, events))

    def upright(index):
        index = jnp.where(diagonal, index.astype(F32), 0.0)
        return jnp.sum(index, axis=1, keepdims=True).astype(jnp.int32)

    def fetch(source, target):
        index = jnp.concatenate([upright(source), upright(target)], axis=0)
        lanes = lane_index((pair, slots))
        return dot(jnp.where(index == lanes, 1.0, 0.0).astype(BF16), rows_ref[...])

    own = fetch(ends_ref[0:1, :], ends_ref[1:2, :])
    near_copy.wait()
    for near in range(near_count):
        spot = slice(near * pair, (near + 1) * pair)
        other = near_count + near
        feat = fetch(near_ref[near : near + 1, :], near_ref[other : other + 1, :])
        if near == 0:
            cos_copy.wait()
        feat_ref[spot, :] = (feat + cos_ref[spot, :]).astype(BF16)
    attn_copy.wait()
    query = dot(own.astype(BF16), attn_ref[0]) * (1.0 / math.sqrt(head_dim))
    keys = dot(feat_ref[...], attn_ref[1])
    logits = [[] for _ in range(HEADS)]
    for near in range(near_count):
        match = query * keys[near * pair : (near + 1) * pair]
        for head in range(HEADS):
            part = match[:, head * head_dim : (head + 1) * head_dim]
            logits[head].append(jnp.sum(part, axis=1, keepdims=True))
    values = dot(feat_ref[...], attn_ref[2])
    mixed = []
    for head in range(HEADS):
        top = logits[head][0]
        for near in range(1, near_count):
            top = jnp.maximum(top, logits[head][near])
        powers = [jnp.exp(logit - top) for logit in logits[head]]
        total = powers[0]
        for near in range(1, near_count):
            total = total + powers[near]
        part = jnp.zeros((pair, head_dim), F32)
        for near in range(near_count):
            value = values[near * pair : (near + 1) * pair, head * head_dim : (head + 1) * head_dim]
            part = part + (powers[near] / total) * value
        mixed.append(part)
    mixed = jnp.concatenate(mixed, axis=1).astype(BF16)
    state = (own + dot(mixed, attn_ref[3])).astype(BF16)
    source, target = state[:events], state[events:]
    cot_copy.wait()
    out_copy.wait()
    pred_copy.wait()
    pre = dot(source, pred_ref[0]) + dot(target, pred_ref[1])
    gate = jax.nn.sigmoid(pre)
    pred_out = pred_out_ref[...]
    column = jnp.sum(pre * gate * pred_out, axis=1, keepdims=True)
    scores_ref[...] = jnp.sum(jnp.where(diagonal, column, 0.0), axis=0, keepdims=True)
    cot = jnp.sum(jnp.where(diagonal, cot_ref[...], 0.0), axis=1, keepdims=True)
    slope = (cot * pred_out * (gate * (1.0 + pre * (1.0 - gate)))).astype(BF16)
    back = jnp.concatenate([dot(slope, pred_ref[0], NT), dot(slope, pred_ref[1], NT)], axis=0)
    grads_ref[0:width, :] = dot(mixed, back.astype(BF16), TN).astype(BF16)
    grads_ref[width : 2 * width, :] = dot(source, slope, TN).astype(BF16)
    grads_ref[2 * width :, :] = dot(target, slope, TN).astype(BF16)


def grads_body(whole_ref, first_ref, rest_ref):
    width = first_ref.shape[0]
    whole = whole_ref[...].astype(F32).reshape(3 * width, width)
    first_ref[...] = whole[:width]
    for part in range(2):
        rest_ref[part] = whole[(part + 1) * width : (part + 2) * width]


def exchange(value, axis, groups=None):
    return lax.all_to_all(
        value, axis, split_axis=0, concat_axis=0, tiled=True, axis_index_groups=groups
    )


def sum_everywhere(grads, columns, rings):
    sections = lax.axis_size("tm")
    plane = [
        [
            (section * rings + ring) * columns + column
            for section in range(sections)
            for column in range(columns)
        ]
        for ring in range(rings)
    ]
    line = [[ring * columns + column for ring in range(rings)] for column in range(columns)]
    peers = len(plane[0])
    rows, width = grads.shape
    own = rows // peers
    pieces = exchange(grads.reshape(peers, own, width), ("tm", "dp"), plane)
    mine = jnp.sum(pieces.astype(F32), axis=0).astype(BF16)
    pieces = exchange(jnp.broadcast_to(mine[None], (rings, own, width)), "dp", line)
    mine = jnp.sum(pieces.astype(F32), axis=0).astype(BF16)
    whole = exchange(jnp.broadcast_to(mine[None], (peers, own, width)), ("tm", "dp"), plane)
    return dense_call(
        grads_body,
        (
            jax.ShapeDtypeStruct((width, width), F32),
            jax.ShapeDtypeStruct((rows // width - 1, width, width), F32),
        ),
        (whole,),
    )


def per_device(
    edge_feat,
    endpoint_slots,
    neighbor_slots,
    neighbor_gap,
    score_grad,
    node_list,
    memory0,
    msg_weight,
    gate_weight,
    gate_bias,
    omega,
    attn_weights,
    pred_weights,
    pred_out,
):
    groups = lax.axis_size("dp")
    batches = lax.axis_size("tm")
    nodes, width = memory0.shape
    list_len = node_list.shape[2]
    per_owner = list_len // groups
    features = edge_feat.shape[2]
    rest = features - LANES
    events = endpoint_slots.shape[2]
    near_count = neighbor_slots.shape[1] // 2
    sent = pl.pallas_call(
        pack_body,
        out_shape=jax.ShapeDtypeStruct((groups, per_owner * 3 // 2, LANES), BF16),
        in_specs=[pl.BlockSpec(memory_space=pltpu.HBM)] * 3,
        scratch_shapes=[
            pltpu.VMEM((HALF, LANES), F32),
            pltpu.VMEM((features, events), BF16),
            pltpu.VMEM((2, events), jnp.int32),
            pltpu.VMEM((1, list_len), jnp.int32),
            pltpu.SemaphoreType.DMA((3,)),
        ],
        compiler_params=ALONE,
    )(jnp.swapaxes(edge_feat[0], 0, 1), endpoint_slots[0], node_list[0])
    got = exchange(sent, "dp")
    pairs = 2 * near_count * events

    def by_neighbour(value):
        return jnp.swapaxes(value[0].reshape(2, near_count, events), 0, 1).reshape(pairs, 1)

    cosines = jnp.cos(by_neighbour(neighbor_gap).astype(F32) * omega[None, :])
    means = dense_call(
        lambda *refs: mean_body(rest, nodes, *refs),
        jax.ShapeDtypeStruct((batches, nodes + nodes // 2, LANES), BF16),
        (got,),
    )
    means = exchange(means, "tm")
    tail_w = jnp.pad(msg_weight[LANES:], ((0, HALF - rest), (0, 0)))
    section = lax.axis_index("tm").astype(jnp.int32)
    weights = (
        msg_weight[:LANES],
        jnp.pad(tail_w, ((0, HALF), (0, 0))),
        jnp.pad(tail_w, ((HALF, 0), (0, 0))),
        gate_weight,
        gate_bias[None],
    )

    def section_call(body, out_shape, args):
        return pl.pallas_call(
            lambda *refs: body(rest, *refs),
            out_shape=out_shape,
            in_specs=[pl.BlockSpec(memory_space=pltpu.SMEM)]
            + [pl.BlockSpec(memory_space=pltpu.VMEM)] * (len(args) + len(weights)),
            compiler_params=PARAMS,
        )(section[None], *args, *weights)

    rows = section_call(
        rows_body,
        jax.ShapeDtypeStruct((groups, per_owner, width), BF16),
        (means, got, memory0),
    )
    new_memory = section_call(
        memory_body, jax.ShapeDtypeStruct((nodes, width), F32), (means, memory0)
    )
    slot_rows = exchange(rows, "dp").reshape(list_len, width)
    cosines, new_memory = lax.optimization_barrier((cosines, new_memory))
    inputs = (
        slot_rows,
        endpoint_slots[0],
        neighbor_slots[0],
        cosines,
        score_grad,
        attn_weights,
        pred_weights,
        pred_out[None],
    )
    scores, grads = pl.pallas_call(
        event_body,
        out_shape=(
            jax.ShapeDtypeStruct((1, events), F32),
            jax.ShapeDtypeStruct((3 * width, width), BF16),
        ),
        in_specs=[pl.BlockSpec(memory_space=pltpu.HBM)] * len(inputs),
        scratch_shapes=[pltpu.VMEM(value.shape, value.dtype) for value in inputs]
        + [pltpu.VMEM((pairs, width), BF16), pltpu.SemaphoreType.DMA((len(inputs),))],
        compiler_params=ALONE,
    )(*inputs)
    columns = 4
    grad_out, grad_pair = sum_everywhere(grads, columns, groups // columns)
    return (scores, new_memory[None], grad_out, grad_pair)


def solution(mesh):
    in_specs = (
        P("tm", "dp", None),
        P("tm", None, "dp"),
        P("tm", None, "dp"),
        P("tm", None, "dp"),
        P("tm", "dp"),
        P("tm", "dp", None),
        P("dp", None),
        P(),
        P(),
        P(),
        P(),
        P(),
        P(),
        P(),
    )
    out_specs = (P("tm", "dp"), P("tm", "dp", None), P(), P())
    return jax.shard_map(
        per_device, mesh=mesh, in_specs=in_specs, out_specs=out_specs, check_vma=False
    )
```

time: 211 us -> 204 us (0.967)
  local copies, waits for them, and re-layouts: 7.28 us -> 0.74 us
    pallas_call x1 -> x4, Pallas kernels: 4.43 us -> 15.5 us  [the longest x1 8.92 us: per_device(): pl.pallas_call(event_body, out_shape=(jax.ShapeDtypeStruct((1, events), F...]
    pallas_call x3 -> x2, Pallas kernels: 13.8 us -> 2.73 us  [dense_call(): pl.pallas_call(body, out_shape=out_shape, in_specs=[pl.BlockSpec(memory_s...]
    unnamed x33 -> x15, local copies, waits for them, and re-layouts: 4.91 us -> 0.64 us
  transfers between devices with their start and end apart: 2 -> 2, of which waited for: 2 -> 2; matrix products, arithmetic and copies ran while one was open for 5% -> 5% of each run, Pallas kernels for 0% -> 1%
where the time goes in v3:
time: 204 us
  blocking collectives  113 us (55%)
  waiting for transfers between devices  46.6 us (23%)
  Pallas kernels  18.3 us (9%)
  starting transfers between devices  14.6 us (7%)
  other arithmetic  10.1 us (5%)
    all_to_all x4, blocking collectives, exchange(): lax.all_to_all(value, axis, split_axis=0, concat_axis=0, tiled=True, axis...  113 us
    all_to_all x2, waiting for transfers between devices, exchange(): lax.all_to_all(value, axis, split_axis=0, concat_axis=0, tiled=True, axis...  46.6 us
    all_to_all x2, starting transfers between devices, exchange(): lax.all_to_all(value, axis, split_axis=0, concat_axis=0, tiled=True, axis...  14.6 us
    cos x1, other arithmetic, per_device(): cosines = jnp.cos(by_neighbour(neighbor_gap).astype(F32) * omega[None, :])  9.91 us
    pallas_call x1, Pallas kernels, per_device(): pl.pallas_call(event_body, out_shape=(jax.ShapeDtypeStruct((1, events), F...  8.92 us
  transfers between devices with their start and end apart: 2, of which 2 were waited for; matrix products, arithmetic and copies ran while one was open for 5% of the time, Pallas kernels for 1%

profile of v3, /device:TPU:1, one launch (start us, length us, event | category | flops | bytes accessed | tf_op | source)
XLA Modules:
  0.0 203.8 jit_solution(14075865735473144969)
XLA Ops:
  0.6 0.0 copy-start.3
  0.6 0.0 copy-start
  0.7 0.0 copy-start.1
  0.7 0.0 copy-start.2
  0.7 2.6 %shard_map.165 = bf16[64,48,128]{2,1,0:T(8,128)(2,1)} custom-call(bf16[186,128]{1,0:T(8,128)(2,1)} %bitcast.23, s32[2,128]{1,0:T(2,128)} %bitcast.25, s32[1,2048]{1,0:T(1,128)} %bitcast.24), custom_call_target="tpu_custom_call" | custom-call | tf_op jit(solution)/shard_map/pallas_call | solution.py:333
  3.3 0.0 slice-start
  3.3 60.0 %all_to_all.30.refs_0_.refs_2_ = bf16[64,48,128]{2,1,0:T(8,128)(2,1)S(1)} all-to-all(bf16[64,48,128]{2,1,0:T(8,128)(2,1)} %shard_map.165), channel_id=1, replica_groups=mesh['tm'=8,'dp'=64] {'dp'}, dimensions={0} | all-to-all | bytes 1572864 | tf_op jit(solution)/shard_map/all_to_all | solution.py:274
  63.3 1.8 shard_map.166
  65.1 8.6 %all-to-all-start.1 = ((bf16[8,192,128]{2,1,0:T(8,128)(2,1)}), bf16[8,192,128]{2,1,0:T(8,128)(2,1)S(1)}, u32[]{:S(2)}, u32[]{:S(2)}) async-start(bf16[8,192,128]{2,1,0:T(8,128)(2,1)} %shard_map.166), calls=%async_computation.1 | async-start | bytes 786432 | tf_op jit(solution)/shard_map/all_to_all | solution.py:274
  73.7 0.0 copy-done.3
  73.8 0.0 copy-start.5
  73.8 0.0 slice-done
  73.8 0.0 copy-start.6
  73.8 8.0 %all-to-all-done.1.refs_1_ = bf16[8,192,128]{2,1,0:T(8,128)(2,1)S(1)} async-done(((bf16[8,192,128]{2,1,0:T(8,128)(2,1)}), bf16[8,192,128]{2,1,0:T(8,128)(2,1)S(1)}, u32[]{:S(2)}, u32[]{:S(2)}) %all-to-all-start.1) | async-done | bytes 393248 | tf_op jit(solution)/shard_map/all_to_all | solution.py:274
  81.8 0.0 copy-done
  81.8 0.0 copy-done.1
  81.8 0.0 copy-done.2
  81.8 2.4 %shard_map.167 = bf16[64,32,256]{2,1,0:T(8,128)(2,1)} custom-call(s32[1]{0:T(128)} %bitcast.refs_0_, bf16[8,192,128]{2,1,0:T(8,128)(2,1)S(1)} %all-to-all-done.1.refs_1_, bf16[64,48,128]{2,1,0:T(8,128)(2,1)S(1)} %all_to_all.30.refs_0_.refs_2_, f32[128,256]{1,0:T(8,128)S(1)} %copy-done.1, bf16[128,256]{1,0:T(8,128)(2,1)S(1)} %slice.6.refs_4_.refs_3_, ...), custom_call_target="tpu_custom_call" | custom-call | tf_op jit(solution)/shard_map/pallas_call | solution.py:370
  84.2 6.0 %all-to-all-start.2 = ((bf16[64,32,256]{2,1,0:T(8,128)(2,1)}), bf16[64,32,256]{2,1,0:T(8,128)(2,1)}, u32[]{:S(2)}, u32[]{:S(2)}) async-start(bf16[64,32,256]{2,1,0:T(8,128)(2,1)} %shard_map.167), calls=%async_computation.2 | async-start | bytes 2097152 | tf_op jit(solution)/shard_map/all_to_all | solution.py:274
  90.2 0.0 copy-done.4
  90.2 0.6 copy.25
  90.8 0.0 copy-done.5
  90.9 0.0 copy-done.6
  90.9 9.9 %multiply_cosine_fusion.refs_3_ = f32[2560,256]{1,0:T(8,128)} fusion(f32[256]{0:T(256)S(1)} %copy-done.6, f32[2560]{0:T(1024)S(1)} %convert_element_type.30), kind=kLoop, calls=%fused_computation | loop fusion | flops 655360 | bytes 2632704 | tf_op jit(solution)/shard_map/cos | solution.py:352
  100.8 1.6 shard_map.168
  102.5 38.6 %all-to-all-done.2 = bf16[64,32,256]{2,1,0:T(8,128)(2,1)} async-done(((bf16[64,32,256]{2,1,0:T(8,128)(2,1)}), bf16[64,32,256]{2,1,0:T(8,128)(2,1)}, u32[]{:S(2)}, u32[]{:S(2)}) %all-to-all-start.2) | async-done | bytes 1048608 | tf_op jit(solution)/shard_map/all_to_all | solution.py:274
  141.1 8.9 %shard_map.169 = (f32[1,128]{1,0:T(1,128)}, bf16[768,256]{1,0:T(8,128)(2,1)}) custom-call(bf16[2048,256]{1,0:T(8,128)(2,1)} %bitcast.6.refs_0_, s32[2,128]{1,0:T(2,128)} %bitcast.26, s32[20,128]{1,0:T(8,128)} %bitcast.22, f32[2560,256]{1,0:T(8,128)} %multiply_cosine_fusion.refs_3_, f32[1,128]{1,0:T(1,128)} %refs_4_.1, bf16[4,256,256]{2,1,0:T(8,128)(2,1)} %refs_5_.1, ...), custom_call_target="tpu_custom_call" | custom-call | tf_op jit(solution)/shard_map/pallas_call | solution.py:398
  150.0 20.1 %all_to_all.31 = bf16[32,24,256]{2,1,0:T(8,128)(2,1)S(1)} all-to-all(bf16[32,24,256]{2,1,0:T(8,128)(2,1)} %bitcast.19), channel_id=1, replica_groups={{0,1,2,3,64,65,66,67,128,129,130,131,192,193,194,195,256,257,258,259,32..., dimensions={0} | all-to-all | bytes 786432 | tf_op jit(solution)/shard_map/all_to_all | solution.py:274
  170.1 0.1 reduce_sum.24
  170.2 15.4 %all_to_all.32 = bf16[16,24,256]{2,1,0:T(8,128)(2,1)S(1)} all-to-all(bf16[16,24,256]{2,1,0:T(8,128)(2,1)S(1)} %broadcast_in_dim.30), channel_id=1, replica_groups={{0,4,8,12,16,20,24,28,32,36,40,44,48,52,56,60},{1,5,9,13,17,21,25,29,33..., dimensions={0} | all-to-all | bytes 393216 | tf_op jit(solution)/shard_map/all_to_all | solution.py:274
  185.7 17.2 %all_to_all.33.whole_ref = bf16[32,24,256]{2,1,0:T(8,128)(2,1)S(1)} all-to-all(bf16[32,24,256]{2,1,0:T(8,128)(2,1)S(1)} %broadcast_in_dim.31), channel_id=1, replica_groups={{0,1,2,3,64,65,66,67,128,129,130,131,192,193,194,195,256,257,258,259,32..., dimensions={0} | all-to-all | bytes 786432 | tf_op jit(solution)/shard_map/all_to_all | solution.py:274
  202.9 0.9 shard_map.170
  (11 shorter events, 0.2 us)
Async XLA Ops:
  0.6 73.1 %copy-start.3 = (bf16[186,256]{1,0:T(8,128)(2,1)S(1)}, bf16[186,256]{1,0:T(8,128)(2,1)}, u32[]{:S(2)}) copy-start(bf16[186,256]{1,0:T(8,128)(2,1)} %param.21) | copy-start | bytes 285700
  0.6 81.2 %copy-start = (bf16[256,512]{1,0:T(8,128)(2,1)S(1)}, bf16[256,512]{1,0:T(8,128)(2,1)}, u32[]{:S(2)}) copy-start(bf16[256,512]{1,0:T(8,128)(2,1)} %refs_6_.2) | copy-start | bytes 786436
  0.7 81.2 %copy-start.1 = (f32[128,256]{1,0:T(8,128)S(1)}, f32[128,256]{1,0:T(8,128)}, u32[]{:S(2)}) copy-start(f32[128,256]{1,0:T(8,128)} %refs_2_.1) | copy-start | bytes 393220
  0.7 81.2 %copy-start.2 = (f32[512]{0:T(512)S(1)}, f32[512]{0:T(512)}, u32[]{:S(2)}) copy-start(f32[512]{0:T(512)} %param.23) | copy-start | bytes 6148
  3.3 70.5 %slice-start = ((bf16[186,256]{1,0:T(8,128)(2,1)}), bf16[58,256]{1,0:T(8,128)(2,1)S(1)}, s32[]{:S(2)}) async-start(bf16[186,256]{1,0:T(8,128)(2,1)} %param.21), calls=%async_computation.6 | async-start | bytes 65536 | tf_op jit(solution)/shard_map/slice | solution.py:359
  65.1 16.7 %all-to-all-start.1 = ((bf16[8,192,128]{2,1,0:T(8,128)(2,1)}), bf16[8,192,128]{2,1,0:T(8,128)(2,1)S(1)}, u32[]{:S(2)}, u32[]{:S(2)}) async-start(bf16[8,192,128]{2,1,0:T(8,128)(2,1)} %shard_map.166), calls=%async_computation.1 | async-start | bytes 786432 | tf_op jit(solution)/shard_map/all_to_all | solution.py:274
  73.7 16.4 %copy-start.4 = (s32[1,20,128]{2,0,1:T(1,128)S(1)}, s32[1,20,128]{2,0,1:T(1,128)}, u32[]{:S(2)}) copy-start(s32[1,20,128]{2,0,1:T(1,128)} %param.16) | copy-start | bytes 30724
  73.8 17.0 %copy-start.5 = (s32[1,20,128]{2,0,1:T(1,128)S(1)}, s32[1,20,128]{2,0,1:T(1,128)}, u32[]{:S(2)}) copy-start(s32[1,20,128]{2,0,1:T(1,128)} %param.17) | copy-start | bytes 30724
  73.8 17.1 %copy-start.6 = (f32[256]{0:T(256)S(1)}, f32[256]{0:T(256)}, u32[]{:S(2)}) copy-start(f32[256]{0:T(256)} %param.24) | copy-start | bytes 3076
  84.2 56.9 %all-to-all-start.2 = ((bf16[64,32,256]{2,1,0:T(8,128)(2,1)}), bf16[64,32,256]{2,1,0:T(8,128)(2,1)}, u32[]{:S(2)}, u32[]{:S(2)}) async-start(bf16[64,32,256]{2,1,0:T(8,128)(2,1)} %shard_map.167), calls=%async_computation.2 | async-start | bytes 2097152 | tf_op jit(solution)/shard_map/all_to_all | solution.py:274

commit v4 on v3

--- a/solution.py
+++ b/solution.py
@@ -51,89 +51,121 @@
         copy.wait()
 
 
-def pack_body(feat_hbm, ends_hbm, list_hbm, out_ref, wide_ref, feat_ref, ends_ref, list_ref, sems):
+WIRE = LANES + HALF
+CHUNK = 16
+
+
+def pack_body(per_owner, feat_hbm, ends_hbm, list_hbm, out_ref, *refs):
+    wide_ref, rows_ref, feat_ref, ends_ref, list_ref, sems = refs
     load((feat_hbm, ends_hbm, list_hbm), (feat_ref, ends_ref, list_ref), sems)
     rest = feat_ref.shape[0] - LANES
-    wide_ref[...] = jnp.zeros_like(wide_ref)
-    wide_ref[0:rest, :] = feat_ref[LANES:, :].astype(F32)
-    tail = wide_ref[...].astype(BF16)
-    empty = jnp.zeros_like(tail)
-    tails = jnp.concatenate(
-        [
-            jnp.concatenate([tail, empty], axis=0),
-            jnp.concatenate([empty, tail], axis=0),
-        ],
-        axis=1,
-    )
-    head = feat_ref[0:LANES, :]
-    per_owner = out_ref.shape[1] * 2 // 3
-    low = per_owner // 2
-    owners = LANES // per_owner
+    list_len = list_ref.shape[1]
+    blocks = list_len // LANES
     slot_of = lax.broadcasted_iota(jnp.int32, (LANES, LANES), 0)
     diagonal = slot_of == lane_index((LANES, LANES))
     ends = ends_ref[...]
-    lane = lane_index((1, 1, LANES))
-    for block in range(list_ref.shape[1] // LANES):
-        hits = jnp.where(ends[0:1, :] == slot_of + block * LANES, 1.0, 0.0) + jnp.where(
-            ends[1:2, :] == slot_of + block * LANES, 1.0, 0.0
-        )
-        tally = jnp.sum(hits, axis=1, keepdims=True).reshape(owners, per_owner, 1)
+    found = [jnp.zeros((LANES, LANES), F32) for _ in range(2)]
+    for block in range(blocks):
         named = list_ref[0:1, block * LANES : (block + 1) * LANES].astype(F32)
+        rows_ref[block : block + 1, :] = named
         named = jnp.sum(jnp.where(diagonal, named, 0.0), axis=1, keepdims=True)
-        named = named.reshape(owners, per_owner, 1)
-        first = dot(hits.astype(BF16), head, NT).reshape(owners, per_owner, LANES)
-        split = hits.reshape(owners, per_owner, LANES)
-        both = jnp.concatenate(
-            [
-                split[:, :low].reshape(owners * low, LANES),
-                split[:, low:].reshape(owners * low, LANES),
-            ],
-            axis=1,
-        ).astype(BF16)
-        second = dot(both, tails, NT).reshape(owners, low, LANES)
-        second = jnp.where(lane == rest, tally[:, :low], second)
-        second = jnp.where(lane == rest + 1, named[:, :low], second)
-        second = jnp.where(lane == HALF + rest, tally[:, low:], second)
-        second = jnp.where(lane == HALF + rest + 1, named[:, low:], second)
-        spot = slice(block * owners, (block + 1) * owners)
-        out_ref[spot, 0:per_owner, :] = first.astype(BF16)
-        out_ref[spot, per_owner:, :] = second.astype(BF16)
-
-
-def pick(tails, column, nodes):
-    column = tails[:, column : column + 1].astype(F32).astype(jnp.int32)
-    return jnp.where(column == lane_index((tails.shape[0], nodes)), 1.0, 0.0).astype(BF16)
-
-
-CHUNK = 16
+        for side in range(2):
+            hit = ends[side : side + 1, :] == slot_of + block * LANES
+            found[side] = found[side] + jnp.where(hit, named, 0.0)
+    wide_ref[...] = jnp.zeros_like(wide_ref)
+    wide_ref[0:rest, :] = feat_ref[LANES:, :].astype(F32)
+    wide_ref[rest : rest + 1, :] = jnp.ones((1, LANES), F32)
+    for side in range(2):
+        spot = rest + 1 + 2 * side
+        wide_ref[spot : spot + 1, :] = (ends[side : side + 1, :] // per_owner).astype(F32)
+        wide_ref[spot + 1 : spot + 2, :] = jnp.sum(found[side], axis=0, keepdims=True)
+    out_ref[0:LANES, :] = feat_ref[0:LANES, :]
+    out_ref[LANES:WIRE, :] = wide_ref[...].astype(BF16)
+    out_ref[WIRE:, :] = rows_ref[...].astype(BF16)
+
+
+def sums_body(rest, nodes, ring_ref, got_ref, out_ref, rows_ref):
+    rings = got_ref.shape[0]
+    columns = out_ref.shape[0]
+    ring = ring_ref[0]
+    base = ring * columns * nodes
+    node_of = lax.broadcasted_iota(jnp.int32, (columns * nodes, 2 * LANES), 0)
+    total = jnp.zeros((columns * nodes, 2 * LANES), F32)
+
+    def keys(part, side):
+        spot = rest + 1 + 2 * side
+        rows = got_ref[part, LANES:WIRE, :].astype(F32)
+        key = rows[spot : spot + 1, :] * nodes + rows[spot + 1 : spot + 2, :]
+        return key.astype(jnp.int32) - base
+
+    for part in range(0, rings, 2):
+        hits = jnp.zeros((columns * nodes, 2 * LANES), F32)
+        for side in range(2):
+            key = jnp.concatenate([keys(part, side), keys(part + 1, side)], axis=1)
+            hits = hits + jnp.where(node_of == key, 1.0, 0.0)
+        feats = []
+        for source in (part, part + 1):
+            tail = got_ref[source, LANES:WIRE, :]
+            feats.append(jnp.concatenate([got_ref[source, 0:LANES, :], tail, tail], axis=0))
+        total = total + dot(hits.astype(BF16), jnp.concatenate(feats, axis=1), NT)
+    list_rows = lax.broadcasted_iota(jnp.int32, (rings, LANES), 0)
+    for part in range(rings):
+        named = jnp.where(list_rows == ring, got_ref[part, WIRE:, :].astype(F32), 0.0)
+        rows_ref[part : part + 1, :] = jnp.sum(named, axis=0, keepdims=True)
+    cut = nodes // 2
+    lane = lane_index((cut, LANES))
+    low_lane = lane < HALF
+    spot = jnp.where(low_lane, lane, lane - HALF)
+    for column in range(columns):
+        mine = total[column * nodes : (column + 1) * nodes]
+        tail = jnp.where(low_lane, mine[:cut, LANES:], mine[cut:, LANES:])
+        high = jnp.floor(tail * (1.0 / LANES))
+        tail = jnp.where(spot == rest, tail - high * LANES, tail)
+        tail = jnp.where(spot == rest + 1, pltpu.roll(high, 1, 1), tail)
+        out_ref[column, 0:LANES, :] = mine[:, :LANES].astype(BF16)
+        out_ref[column, LANES:WIRE, :] = tail.astype(BF16)
+        out_ref[column, WIRE:, :] = rows_ref[...].astype(BF16)
 
 
 def mean_body(rest, nodes, got_ref, out_ref):
-    low = got_ref.shape[1] // 3
-    size = CHUNK * low
-    sum_low = jnp.zeros((nodes, 2 * LANES), F32)
-    sum_high = jnp.zeros((nodes, 2 * LANES), F32)
-    for start in range(0, got_ref.shape[0], CHUNK):
-        spot = slice(start, start + CHUNK)
-        tails = got_ref[spot, 2 * low :, :].reshape(size, LANES)
-        heads = got_ref[spot, 0:low, :].reshape(size, LANES)
-        pick_low = pick(tails, rest + 1, nodes)
-        sum_low += dot(pick_low, jnp.concatenate([heads, tails], axis=1), TN)
-        heads = got_ref[spot, low : 2 * low, :].reshape(size, LANES)
-        pick_high = pick(tails, HALF + rest + 1, nodes)
-        sum_high += dot(pick_high, jnp.concatenate([heads, tails], axis=1), TN)
-    head = sum_low[:, :LANES] + sum_high[:, :LANES]
-    tail = sum_low[:, LANES:] + pltpu.roll(sum_high[:, LANES:], HALF, 1)
-    count = jnp.maximum(tail[:, rest : rest + 1], 1.0)
-    head = head / count
-    tail = jnp.where(lane_index(tail.shape) <= rest, tail / count, 0.0)
+    total = got_ref[0, 0:WIRE, :].astype(F32)
+    for column in range(1, got_ref.shape[0]):
+        total = total + got_ref[column, 0:WIRE, :].astype(F32)
     cut = nodes // 2
-    tail = jnp.where(
-        lane_index((cut, LANES)) < HALF, tail[:cut], pltpu.roll(tail[cut:], HALF, 1)
-    )
+    head, tail = total[:nodes], total[nodes:]
+
+    def count(start):
+        spot = start + rest
+        return tail[:, spot : spot + 1] + LANES * tail[:, spot + 1 : spot + 2]
+
+    low, high = count(0), count(HALF)
+    low_safe, high_safe = jnp.maximum(low, 1.0), jnp.maximum(high, 1.0)
+    head = jnp.concatenate([head[:cut] / low_safe, head[cut:] / high_safe], axis=0)
+    lane = lane_index((cut, LANES))
+    low_lane = lane < HALF
+    spot = jnp.where(low_lane, lane, lane - HALF)
+    touched = jnp.where(jnp.where(low_lane, low, high) > 0.5, 1.0, 0.0)
+    tail = tail / jnp.where(low_lane, low_safe, high_safe)
+    tail = jnp.where(spot < rest, tail, jnp.where(spot == rest, touched, 0.0))
     for part in range(out_ref.shape[0]):
         out_ref[part, 0:nodes, :] = head.astype(BF16)
         out_ref[part, nodes:, :] = tail.astype(BF16)
+
+
+def pick_body(column_ref, got_ref, out_ref):
+    columns = got_ref.shape[0]
+    rings = got_ref.shape[1] - WIRE
+    per_owner, nodes = out_ref.shape[1:]
+    shift = lax.rem((columns - column_ref[0]) * per_owner, LANES)
+    upright = lax.broadcasted_iota(jnp.int32, (per_owner, LANES), 0) == lane_index((per_owner, LANES))
+    node_of = lane_index((per_owner, nodes))
+    for column in range(columns):
+        named = pltpu.roll(got_ref[column, WIRE:, :].astype(F32), shift, 1)
+        for ring in range(rings):
+            asked = jnp.where(upright, named[ring : ring + 1, :], 0.0)
+            asked = jnp.sum(asked, axis=1, keepdims=True).astype(jnp.int32)
+            hits = jnp.where(asked == node_of, 1.0, 0.0).astype(BF16)
+            out_ref[ring * columns + column] = hits
 
 
 def gates(rest, head, tail, head_w_ref, low_w_ref, high_w_ref, gate_ref, bias_ref):
@@ -163,20 +195,16 @@
     return state
 
 
-def rows_body(rest, section_ref, mean_ref, got_ref, memory_ref, *refs):
+def rows_body(rest, section_ref, mean_ref, pick_ref, memory_ref, *refs):
     weights, rows_ref = refs[:-1], refs[-1]
-    nodes, width = memory_ref.shape
     batches = mean_ref.shape[0] - 1
     before = advance(rest, section_ref[0], mean_ref, batches, memory_ref, weights).astype(BF16)
-    low = got_ref.shape[1] // 3
-    size = CHUNK * low
-    for start in range(0, got_ref.shape[0], CHUNK):
+    groups, per_owner, nodes = pick_ref.shape
+    for start in range(0, groups, CHUNK):
         spot = slice(start, start + CHUNK)
-        tails = got_ref[spot, 2 * low :, :].reshape(size, LANES)
-        rows = dot(pick(tails, rest + 1, nodes), before).astype(BF16)
-        rows_ref[spot, 0:low, :] = rows.reshape(CHUNK, low, width)
-        rows = dot(pick(tails, HALF + rest + 1, nodes), before).astype(BF16)
-        rows_ref[spot, low:, :] = rows.reshape(CHUNK, low, width)
+        picks = pick_ref[spot].reshape(CHUNK * per_owner, nodes)
+        rows = dot(picks, before).astype(BF16)
+        rows_ref[spot] = rows.reshape(CHUNK, per_owner, before.shape[1])
 
 
 def memory_body(rest, section_ref, mean_ref, memory_ref, *refs):
@@ -330,12 +358,19 @@
     rest = features - LANES
     events = endpoint_slots.shape[2]
     near_count = neighbor_slots.shape[1] // 2
+    columns = 4
+    rings = groups // columns
+    line = [[ring * columns + column for ring in range(rings)] for column in range(columns)]
+    across = [[ring * columns + column for column in range(columns)] for ring in range(rings)]
+    place = lax.axis_index("dp").astype(jnp.int32)
+    blocks = list_len // LANES
     sent = pl.pallas_call(
-        pack_body,
-        out_shape=jax.ShapeDtypeStruct((groups, per_owner * 3 // 2, LANES), BF16),
+        lambda *refs: pack_body(per_owner, *refs),
+        out_shape=jax.ShapeDtypeStruct((WIRE + blocks, LANES), BF16),
         in_specs=[pl.BlockSpec(memory_space=pltpu.HBM)] * 3,
         scratch_shapes=[
             pltpu.VMEM((HALF, LANES), F32),
+            pltpu.VMEM((blocks, LANES), F32),
             pltpu.VMEM((features, events), BF16),
             pltpu.VMEM((2, events), jnp.int32),
             pltpu.VMEM((1, list_len), jnp.int32),
@@ -343,7 +378,22 @@
         ],
         compiler_params=ALONE,
     )(jnp.swapaxes(edge_feat[0], 0, 1), endpoint_slots[0], node_list[0])
-    got = exchange(sent, "dp")
+    got = lax.all_gather(sent, "dp", axis=0, tiled=True, axis_index_groups=line)
+    in_smem, in_vmem = pl.BlockSpec(memory_space=pltpu.SMEM), pl.BlockSpec(memory_space=pltpu.VMEM)
+    sums = pl.pallas_call(
+        lambda *refs: sums_body(rest, nodes, *refs),
+        out_shape=jax.ShapeDtypeStruct((columns, WIRE + blocks, LANES), BF16),
+        in_specs=[in_smem, in_vmem],
+        scratch_shapes=[pltpu.VMEM((rings, LANES), F32)],
+        compiler_params=PARAMS,
+    )((place // columns)[None], got.reshape(rings, WIRE + blocks, LANES))
+    got = exchange(sums, "dp", across)
+    picks = pl.pallas_call(
+        pick_body,
+        out_shape=jax.ShapeDtypeStruct((groups, per_owner, nodes), BF16),
+        in_specs=[in_smem, in_vmem],
+        compiler_params=PARAMS,
+    )((place % columns)[None], got)
     pairs = 2 * near_count * events
 
     def by_neighbour(value):
@@ -378,7 +428,7 @@
     rows = section_call(
         rows_body,
         jax.ShapeDtypeStruct((groups, per_owner, width), BF16),
-        (means, got, memory0),
+        (means, picks, memory0),
     )
     new_memory = section_call(
         memory_body, jax.ShapeDtypeStruct((nodes, width), F32), (means, memory0)
@@ -406,8 +456,7 @@
         + [pltpu.VMEM((pairs, width), BF16), pltpu.SemaphoreType.DMA((len(inputs),))],
         compiler_params=ALONE,
     )(*inputs)
-    columns = 4
-    grad_out, grad_pair = sum_everywhere(grads, columns, groups // columns)
+    grad_out, grad_pair = sum_everywhere(grads, columns, rings)
     return (scores, new_memory[None], grad_out, grad_pair)
 
 

time: 204 us -> 195 us (0.956)
  blocking collectives: 113 us -> 96.5 us
  starting transfers between devices: 14.6 us -> 21.9 us
    all_to_all x4, blocking collectives: 113 us -> 62 us  [exchange(): lax.all_to_all(value, axis, split_axis=0, concat_axis=0, tiled=True, axis...]
    all_gather x0 -> x1, blocking collectives: none -> 34.5 us  [per_device(): got = lax.all_gather(sent, 'dp', axis=0, tiled=True, axis_index_groups=line)]
    all_to_all x2, starting transfers between devices: 14.6 us -> 21.9 us  [exchange(): lax.all_to_all(value, axis, split_axis=0, concat_axis=0, tiled=True, axis...]
where the time goes in v4:
time: 195 us; the launch traced here: 194 us
  blocking collectives  96.5 us (49%)
  waiting for transfers between devices  45.9 us (24%)
  starting transfers between devices  21.9 us (11%)
  Pallas kernels  18.5 us (9%)
  other arithmetic  10.1 us (5%)
    all_to_all x4, blocking collectives, exchange(): lax.all_to_all(value, axis, split_axis=0, concat_axis=0, tiled=True, axis...  62 us
    all_to_all x2, waiting for transfers between devices, exchange(): lax.all_to_all(value, axis, split_axis=0, concat_axis=0, tiled=True, axis...  45.9 us
    all_gather x1, blocking collectives, per_device(): got = lax.all_gather(sent, 'dp', axis=0, tiled=True, axis_index_groups=line)  34.5 us
    all_to_all x2, starting transfers between devices, exchange(): lax.all_to_all(value, axis, split_axis=0, concat_axis=0, tiled=True, axis...  21.9 us
    cos x1, other arithmetic, per_device(): cosines = jnp.cos(by_neighbour(neighbor_gap).astype(F32) * omega[None, :])  9.91 us
    pallas_call x1, Pallas kernels, per_device(): pl.pallas_call(event_body, out_shape=(jax.ShapeDtypeStruct((1, events), F...  8.92 us
    pallas_call x2, Pallas kernels, section_call(): pl.pallas_call(lambda *refs: body(rest, *refs), out_shape=out_shape, in_s...  3.97 us
  transfers between devices with their start and end apart: 2, of which 2 were waited for; matrix products, arithmetic and copies ran while one was open for 5% of the time, Pallas kernels for 1%

profile of v4, /device:TPU:1, one launch (start us, length us, event | category | flops | bytes accessed | tf_op | source)
XLA Modules:
  0.0 194.5 jit_solution(6545928540790514368)
XLA Ops:
  0.6 0.0 copy-start.3
  0.6 0.0 slice-start
  0.7 0.0 copy-start
  0.7 0.0 copy-start.1
  0.7 0.0 copy-start.2
  0.7 2.0 %shard_map.165 = bf16[208,128]{1,0:T(8,128)(2,1)} custom-call(bf16[186,128]{1,0:T(8,128)(2,1)} %bitcast.27, s32[2,128]{1,0:T(2,128)} %bitcast.29, s32[1,2048]{1,0:T(1,128)} %bitcast.28), custom_call_target="tpu_custom_call" | custom-call | tf_op jit(solution)/shard_map/pallas_call | solution.py:367
  2.7 34.5 %all_gather.3 = bf16[3328,128]{1,0:T(8,128)(2,1)S(1)} all-gather(bf16[208,128]{1,0:T(8,128)(2,1)} %shard_map.165), channel_id=1, replica_groups={{0,4,8,12,16,20,24,28,32,36,40,44,48,52,56,60},{1,5,9,13,17,21,25,29,33..., dimensions={0}, use_global_device_ids=true | all-gather | bytes 905216 | tf_op jit(solution)/shard_map/all_gather | solution.py:381
  37.2 1.1 shard_map.166
  38.3 9.2 %all_to_all.30.refs_0_.got_ref = bf16[4,208,128]{2,1,0:T(8,128)(2,1)S(1)} all-to-all(bf16[4,208,128]{2,1,0:T(8,128)(2,1)S(1)} %shard_map.166), channel_id=1, replica_groups={{0,1,2,3},{4,5,6,7},{8,9,10,11},{12,13,14,15},{16,17,18,19},{20,21,22,2..., dimensions={0} | all-to-all | bytes 425984 | tf_op jit(solution)/shard_map/all_to_all | solution.py:302
  47.5 0.9 shard_map.167
  48.5 13.4 %all-to-all-start.1 = ((bf16[8,192,128]{2,1,0:T(8,128)(2,1)}), bf16[8,192,128]{2,1,0:T(8,128)(2,1)S(1)}, u32[]{:S(2)}, u32[]{:S(2)}) async-start(bf16[8,192,128]{2,1,0:T(8,128)(2,1)} %shard_map.167), calls=%async_computation.1 | async-start | bytes 786432 | tf_op jit(solution)/shard_map/all_to_all | solution.py:302
  61.9 0.0 copy-done.3
  62.0 0.0 slice-done
  62.0 0.0 copy-start.4
  62.0 0.0 copy-start.5
  62.0 0.0 copy-start.6
  62.0 0.7 shard_map.168.refs_2_
  62.7 7.3 %all-to-all-done.1.refs_1_ = bf16[8,192,128]{2,1,0:T(8,128)(2,1)S(1)} async-done(((bf16[8,192,128]{2,1,0:T(8,128)(2,1)}), bf16[8,192,128]{2,1,0:T(8,128)(2,1)S(1)}, u32[]{:S(2)}, u32[]{:S(2)}) %all-to-all-start.1) | async-done | bytes 393248 | tf_op jit(solution)/shard_map/all_to_all | solution.py:302
  70.0 0.0 copy-done.1
  70.0 2.3 %shard_map.169 = bf16[64,32,256]{2,1,0:T(8,128)(2,1)} custom-call(s32[1]{0:T(128)} %bitcast.refs_0_, bf16[8,192,128]{2,1,0:T(8,128)(2,1)S(1)} %all-to-all-done.1.refs_1_, bf16[64,32,128]{2,1,0:T(8,128)(2,1)S(1)} %shard_map.168.refs_2_, f32[128,256]{1,0:T(8,128)S(1)} %copy-done.1, bf16[128,256]{1,0:T(8,128)(2,1)S(1)} %slice.6.refs_4_.refs_3_, ...), custom_call_target="tpu_custom_call" | custom-call | tf_op jit(solution)/shard_map/pallas_call | solution.py:420
  72.3 8.5 %all-to-all-start.2 = ((bf16[64,32,256]{2,1,0:T(8,128)(2,1)}), bf16[64,32,256]{2,1,0:T(8,128)(2,1)}, u32[]{:S(2)}, u32[]{:S(2)}) async-start(bf16[64,32,256]{2,1,0:T(8,128)(2,1)} %shard_map.169), calls=%async_computation.2 | async-start | bytes 2097152 | tf_op jit(solution)/shard_map/all_to_all | solution.py:302
  80.8 0.6 copy.25
  81.4 0.0 copy-done.5
  81.5 9.9 %multiply_cosine_fusion.refs_3_ = f32[2560,256]{1,0:T(8,128)} fusion(f32[256]{0:T(256)S(1)} %copy-done.6, f32[2560]{0:T(1024)S(1)} %convert_element_type.30), kind=kLoop, calls=%fused_computation | loop fusion | flops 655360 | bytes 2632704 | tf_op jit(solution)/shard_map/cos | solution.py:402
  91.5 1.6 shard_map.170
  93.1 38.6 %all-to-all-done.2 = bf16[64,32,256]{2,1,0:T(8,128)(2,1)} async-done(((bf16[64,32,256]{2,1,0:T(8,128)(2,1)}), bf16[64,32,256]{2,1,0:T(8,128)(2,1)}, u32[]{:S(2)}, u32[]{:S(2)}) %all-to-all-start.2) | async-done | bytes 1048608 | tf_op jit(solution)/shard_map/all_to_all | solution.py:302
  131.7 8.9 %shard_map.171 = (f32[1,128]{1,0:T(1,128)}, bf16[768,256]{1,0:T(8,128)(2,1)}) custom-call(bf16[2048,256]{1,0:T(8,128)(2,1)} %bitcast.9.refs_0_, s32[2,128]{1,0:T(2,128)} %bitcast.30, s32[20,128]{1,0:T(8,128)} %bitcast.26, f32[2560,256]{1,0:T(8,128)} %multiply_cosine_fusion.refs_3_, f32[1,128]{1,0:T(1,128)} %refs_4_.1, bf16[4,256,256]{2,1,0:T(8,128)(2,1)} %refs_5_.1, ...), custom_call_target="tpu_custom_call" | custom-call | tf_op jit(solution)/shard_map/pallas_call | solution.py:448
  140.6 20.1 %all_to_all.31 = bf16[32,24,256]{2,1,0:T(8,128)(2,1)S(1)} all-to-all(bf16[32,24,256]{2,1,0:T(8,128)(2,1)} %bitcast.23), channel_id=1, replica_groups={{0,1,2,3,64,65,66,67,128,129,130,131,192,193,194,195,256,257,258,259,32..., dimensions={0} | all-to-all | bytes 786432 | tf_op jit(solution)/shard_map/all_to_all | solution.py:302
  160.7 0.1 reduce_sum.24
  160.8 15.4 %all_to_all.32 = bf16[16,24,256]{2,1,0:T(8,128)(2,1)S(1)} all-to-all(bf16[16,24,256]{2,1,0:T(8,128)(2,1)S(1)} %broadcast_in_dim.38), channel_id=1, replica_groups={{0,4,8,12,16,20,24,28,32,36,40,44,48,52,56,60},{1,5,9,13,17,21,25,29,33..., dimensions={0} | all-to-all | bytes 393216 | tf_op jit(solution)/shard_map/all_to_all | solution.py:302
  176.3 17.2 %all_to_all.33.whole_ref = bf16[32,24,256]{2,1,0:T(8,128)(2,1)S(1)} all-to-all(bf16[32,24,256]{2,1,0:T(8,128)(2,1)S(1)} %broadcast_in_dim.39), channel_id=1, replica_groups={{0,1,2,3,64,65,66,67,128,129,130,131,192,193,194,195,256,257,258,259,32..., dimensions={0} | all-to-all | bytes 786432 | tf_op jit(solution)/shard_map/all_to_all | solution.py:302
  193.6 0.9 shard_map.172
  (14 shorter events, 0.2 us)
Async XLA Ops:
  0.6 61.3 %copy-start.3 = (bf16[186,256]{1,0:T(8,128)(2,1)S(1)}, bf16[186,256]{1,0:T(8,128)(2,1)}, u32[]{:S(2)}) copy-start(bf16[186,256]{1,0:T(8,128)(2,1)} %param.21) | copy-start | bytes 285700
  0.6 61.3 %slice-start = ((bf16[186,256]{1,0:T(8,128)(2,1)}), bf16[58,256]{1,0:T(8,128)(2,1)S(1)}, s32[]{:S(2)}) async-start(bf16[186,256]{1,0:T(8,128)(2,1)} %param.21), calls=%async_computation.6 | async-start | bytes 65536 | tf_op jit(solution)/shard_map/slice | solution.py:409
  0.7 69.4 %copy-start = (bf16[256,512]{1,0:T(8,128)(2,1)S(1)}, bf16[256,512]{1,0:T(8,128)(2,1)}, u32[]{:S(2)}) copy-start(bf16[256,512]{1,0:T(8,128)(2,1)} %refs_6_.2) | copy-start | bytes 786436
  0.7 69.3 %copy-start.1 = (f32[128,256]{1,0:T(8,128)S(1)}, f32[128,256]{1,0:T(8,128)}, u32[]{:S(2)}) copy-start(f32[128,256]{1,0:T(8,128)} %refs_2_.1) | copy-start | bytes 393220
  0.7 69.3 %copy-start.2 = (f32[512]{0:T(512)S(1)}, f32[512]{0:T(512)}, u32[]{:S(2)}) copy-start(f32[512]{0:T(512)} %param.23) | copy-start | bytes 6148
  48.5 21.5 %all-to-all-start.1 = ((bf16[8,192,128]{2,1,0:T(8,128)(2,1)}), bf16[8,192,128]{2,1,0:T(8,128)(2,1)S(1)}, u32[]{:S(2)}, u32[]{:S(2)}) async-start(bf16[8,192,128]{2,1,0:T(8,128)(2,1)} %shard_map.167), calls=%async_computation.1 | async-start | bytes 786432 | tf_op jit(solution)/shard_map/all_to_all | solution.py:302
  62.0 18.8 %copy-start.4 = (s32[1,20,128]{2,0,1:T(1,128)S(1)}, s32[1,20,128]{2,0,1:T(1,128)}, u32[]{:S(2)}) copy-start(s32[1,20,128]{2,0,1:T(1,128)} %param.16) | copy-start | bytes 30724
  62.0 19.4 %copy-start.5 = (s32[1,20,128]{2,0,1:T(1,128)S(1)}, s32[1,20,128]{2,0,1:T(1,128)}, u32[]{:S(2)}) copy-start(s32[1,20,128]{2,0,1:T(1,128)} %param.17) | copy-start | bytes 30724
  62.0 19.5 %copy-start.6 = (f32[256]{0:T(256)S(1)}, f32[256]{0:T(256)}, u32[]{:S(2)}) copy-start(f32[256]{0:T(256)} %param.24) | copy-start | bytes 3076
  72.3 59.4 %all-to-all-start.2 = ((bf16[64,32,256]{2,1,0:T(8,128)(2,1)}), bf16[64,32,256]{2,1,0:T(8,128)(2,1)}, u32[]{:S(2)}, u32[]{:S(2)}) async-start(bf16[64,32,256]{2,1,0:T(8,128)(2,1)} %shard_map.169), calls=%async_computation.2 | async-start | bytes 2097152 | tf_op jit(solution)/shard_map/all_to_all | solution.py:302

commit v5 on v4

--- a/solution.py
+++ b/solution.py
@@ -52,22 +52,21 @@
 
 
 WIRE = LANES + HALF
-CHUNK = 16
-
-
-def pack_body(per_owner, feat_hbm, ends_hbm, list_hbm, out_ref, *refs):
-    wide_ref, rows_ref, feat_ref, ends_ref, list_ref, sems = refs
+
+
+def pack_body(per_owner, feat_hbm, ends_hbm, list_hbm, out_ref, rows_ref, *refs):
+    wide_ref, feat_ref, ends_ref, list_ref, sems = refs
     load((feat_hbm, ends_hbm, list_hbm), (feat_ref, ends_ref, list_ref), sems)
     rest = feat_ref.shape[0] - LANES
-    list_len = list_ref.shape[1]
-    blocks = list_len // LANES
+    hops = rows_ref.shape[0]
     slot_of = lax.broadcasted_iota(jnp.int32, (LANES, LANES), 0)
     diagonal = slot_of == lane_index((LANES, LANES))
     ends = ends_ref[...]
     found = [jnp.zeros((LANES, LANES), F32) for _ in range(2)]
-    for block in range(blocks):
+    for block in range(list_ref.shape[1] // LANES):
         named = list_ref[0:1, block * LANES : (block + 1) * LANES].astype(F32)
-        rows_ref[block : block + 1, :] = named
+        turn = block // hops
+        rows_ref[block % hops, turn : turn + 1, :] = named
         named = jnp.sum(jnp.where(diagonal, named, 0.0), axis=1, keepdims=True)
         for side in range(2):
             hit = ends[side : side + 1, :] == slot_of + block * LANES
@@ -80,51 +79,51 @@
         wide_ref[spot : spot + 1, :] = (ends[side : side + 1, :] // per_owner).astype(F32)
         wide_ref[spot + 1 : spot + 2, :] = jnp.sum(found[side], axis=0, keepdims=True)
     out_ref[0:LANES, :] = feat_ref[0:LANES, :]
-    out_ref[LANES:WIRE, :] = wide_ref[...].astype(BF16)
-    out_ref[WIRE:, :] = rows_ref[...].astype(BF16)
-
-
-def sums_body(rest, nodes, ring_ref, got_ref, out_ref, rows_ref):
-    rings = got_ref.shape[0]
-    columns = out_ref.shape[0]
-    ring = ring_ref[0]
-    base = ring * columns * nodes
-    node_of = lax.broadcasted_iota(jnp.int32, (columns * nodes, 2 * LANES), 0)
-    total = jnp.zeros((columns * nodes, 2 * LANES), F32)
+    out_ref[LANES:, :] = wide_ref[...].astype(BF16)
+
+
+def sums_body(rest, nodes, turn_ref, got_ref, list_hbm, out_ref, list_ref, sem):
+    copy = pltpu.make_async_copy(list_hbm, list_ref, sem)
+    copy.start()
+    turns = got_ref.shape[0]
+    peers = out_ref.shape[0]
+    hops = list_ref.shape[0]
+    span = peers * nodes
+    base = turn_ref[0] * span
+    node_of = lax.broadcasted_iota(jnp.int32, (span, 2 * LANES), 0)
+    total = jnp.zeros((span, 2 * LANES), F32)
 
     def keys(part, side):
         spot = rest + 1 + 2 * side
-        rows = got_ref[part, LANES:WIRE, :].astype(F32)
+        rows = got_ref[part, LANES:, :].astype(F32)
         key = rows[spot : spot + 1, :] * nodes + rows[spot + 1 : spot + 2, :]
         return key.astype(jnp.int32) - base
 
-    for part in range(0, rings, 2):
-        hits = jnp.zeros((columns * nodes, 2 * LANES), F32)
+    for part in range(0, turns, 2):
+        hits = jnp.zeros((span, 2 * LANES), F32)
         for side in range(2):
             key = jnp.concatenate([keys(part, side), keys(part + 1, side)], axis=1)
             hits = hits + jnp.where(node_of == key, 1.0, 0.0)
         feats = []
         for source in (part, part + 1):
-            tail = got_ref[source, LANES:WIRE, :]
+            tail = got_ref[source, LANES:, :]
             feats.append(jnp.concatenate([got_ref[source, 0:LANES, :], tail, tail], axis=0))
         total = total + dot(hits.astype(BF16), jnp.concatenate(feats, axis=1), NT)
-    list_rows = lax.broadcasted_iota(jnp.int32, (rings, LANES), 0)
-    for part in range(rings):
-        named = jnp.where(list_rows == ring, got_ref[part, WIRE:, :].astype(F32), 0.0)
-        rows_ref[part : part + 1, :] = jnp.sum(named, axis=0, keepdims=True)
     cut = nodes // 2
     lane = lane_index((cut, LANES))
     low_lane = lane < HALF
     spot = jnp.where(low_lane, lane, lane - HALF)
-    for column in range(columns):
-        mine = total[column * nodes : (column + 1) * nodes]
+    copy.wait()
+    for peer in range(peers):
+        mine = total[peer * nodes : (peer + 1) * nodes]
         tail = jnp.where(low_lane, mine[:cut, LANES:], mine[cut:, LANES:])
         high = jnp.floor(tail * (1.0 / LANES))
         tail = jnp.where(spot == rest, tail - high * LANES, tail)
         tail = jnp.where(spot == rest + 1, pltpu.roll(high, 1, 1), tail)
-        out_ref[column, 0:LANES, :] = mine[:, :LANES].astype(BF16)
-        out_ref[column, LANES:WIRE, :] = tail.astype(BF16)
-        out_ref[column, WIRE:, :] = rows_ref[...].astype(BF16)
+        out_ref[peer, 0:LANES, :] = mine[:, :LANES].astype(BF16)
+        out_ref[peer, LANES:WIRE, :] = tail.astype(BF16)
+        named = list_ref[peer // (peers // hops)]
+        out_ref[peer, WIRE:, :] = jnp.concatenate([named, named], axis=0).astype(BF16)
 
 
 def mean_body(rest, nodes, got_ref, out_ref):
@@ -152,20 +151,20 @@
         out_ref[part, nodes:, :] = tail.astype(BF16)
 
 
-def pick_body(column_ref, got_ref, out_ref):
-    columns = got_ref.shape[0]
-    rings = got_ref.shape[1] - WIRE
-    per_owner, nodes = out_ref.shape[1:]
+def pick_body(columns, column_ref, got_ref, out_ref):
+    turns, asked, nodes = out_ref.shape
+    peers = got_ref.shape[0]
+    per_owner = asked // peers
     shift = lax.rem((columns - column_ref[0]) * per_owner, LANES)
     upright = lax.broadcasted_iota(jnp.int32, (per_owner, LANES), 0) == lane_index((per_owner, LANES))
     node_of = lane_index((per_owner, nodes))
-    for column in range(columns):
-        named = pltpu.roll(got_ref[column, WIRE:, :].astype(F32), shift, 1)
-        for ring in range(rings):
-            asked = jnp.where(upright, named[ring : ring + 1, :], 0.0)
-            asked = jnp.sum(asked, axis=1, keepdims=True).astype(jnp.int32)
-            hits = jnp.where(asked == node_of, 1.0, 0.0).astype(BF16)
-            out_ref[ring * columns + column] = hits
+    for peer in range(peers):
+        named = pltpu.roll(got_ref[peer, WIRE:, :].astype(F32), shift, 1)
+        for turn in range(turns):
+            row = jnp.where(upright, named[turn : turn + 1, :], 0.0)
+            row = jnp.sum(row, axis=1, keepdims=True).astype(jnp.int32)
+            hits = jnp.where(row == node_of, 1.0, 0.0).astype(BF16)
+            out_ref[turn, peer * per_owner : (peer + 1) * per_owner, :] = hits
 
 
 def gates(rest, head, tail, head_w_ref, low_w_ref, high_w_ref, gate_ref, bias_ref):
@@ -195,16 +194,22 @@
     return state
 
 
-def rows_body(rest, section_ref, mean_ref, pick_ref, memory_ref, *refs):
-    weights, rows_ref = refs[:-1], refs[-1]
+def before_body(rest, section_ref, mean_ref, memory_ref, *refs):
+    weights, out_ref = refs[:-1], refs[-1]
     batches = mean_ref.shape[0] - 1
     before = advance(rest, section_ref[0], mean_ref, batches, memory_ref, weights).astype(BF16)
-    groups, per_owner, nodes = pick_ref.shape
-    for start in range(0, groups, CHUNK):
-        spot = slice(start, start + CHUNK)
-        picks = pick_ref[spot].reshape(CHUNK * per_owner, nodes)
-        rows = dot(picks, before).astype(BF16)
-        rows_ref[spot] = rows.reshape(CHUNK, per_owner, before.shape[1])
+    for turn in range(out_ref.shape[0]):
+        out_ref[turn] = before
+
+
+def rows_body(pick_ref, table_ref, out_ref):
+    turns, asked, nodes = pick_ref.shape
+    peers, _, width = out_ref.shape
+    per_owner = asked // peers
+    for turn in range(turns):
+        rows = dot(pick_ref[turn], table_ref[turn]).astype(BF16)
+        spot = slice(turn * per_owner, (turn + 1) * per_owner)
+        out_ref[:, spot, :] = rows.reshape(peers, per_owner, width)
 
 
 def memory_body(rest, section_ref, mean_ref, memory_ref, *refs):
@@ -359,18 +364,26 @@
     events = endpoint_slots.shape[2]
     near_count = neighbor_slots.shape[1] // 2
     columns = 4
+    hops = 2
     rings = groups // columns
-    line = [[ring * columns + column for ring in range(rings)] for column in range(columns)]
-    across = [[ring * columns + column for column in range(columns)] for ring in range(rings)]
+    turns = rings // hops
+    peers = hops * columns
+    line = [
+        [(turn * hops + hop) * columns + column for turn in range(turns)]
+        for column in range(columns)
+        for hop in range(hops)
+    ]
+    across = [[turn * peers + peer for peer in range(peers)] for turn in range(turns)]
     place = lax.axis_index("dp").astype(jnp.int32)
-    blocks = list_len // LANES
-    sent = pl.pallas_call(
+    sent, named = pl.pallas_call(
         lambda *refs: pack_body(per_owner, *refs),
-        out_shape=jax.ShapeDtypeStruct((WIRE + blocks, LANES), BF16),
+        out_shape=(
+            jax.ShapeDtypeStruct((WIRE, LANES), BF16),
+            jax.ShapeDtypeStruct((hops, turns, LANES), F32),
+        ),
         in_specs=[pl.BlockSpec(memory_space=pltpu.HBM)] * 3,
         scratch_shapes=[
             pltpu.VMEM((HALF, LANES), F32),
-            pltpu.VMEM((blocks, LANES), F32),
             pltpu.VMEM((features, events), BF16),
             pltpu.VMEM((2, events), jnp.int32),
             pltpu.VMEM((1, list_len), jnp.int32),
@@ -382,15 +395,19 @@
     in_smem, in_vmem = pl.BlockSpec(memory_space=pltpu.SMEM), pl.BlockSpec(memory_space=pltpu.VMEM)
     sums = pl.pallas_call(
         lambda *refs: sums_body(rest, nodes, *refs),
-        out_shape=jax.ShapeDtypeStruct((columns, WIRE + blocks, LANES), BF16),
-        in_specs=[in_smem, in_vmem],
-        scratch_shapes=[pltpu.VMEM((rings, LANES), F32)],
+        out_shape=jax.ShapeDtypeStruct((peers, WIRE + 2 * turns, LANES), BF16),
+        in_specs=[in_smem, in_vmem, pl.BlockSpec(memory_space=pltpu.HBM)],
+        scratch_shapes=[pltpu.VMEM((hops, turns, LANES), F32), pltpu.SemaphoreType.DMA],
         compiler_params=PARAMS,
-    )((place // columns)[None], got.reshape(rings, WIRE + blocks, LANES))
+    )(
+        (place // peers)[None],
+        got.reshape(turns, WIRE, LANES),
+        pltpu.with_memory_space_constraint(named, pltpu.HBM),
+    )
     got = exchange(sums, "dp", across)
     picks = pl.pallas_call(
-        pick_body,
-        out_shape=jax.ShapeDtypeStruct((groups, per_owner, nodes), BF16),
+        lambda *refs: pick_body(columns, *refs),
+        out_shape=jax.ShapeDtypeStruct((turns, peers * per_owner, nodes), BF16),
         in_specs=[in_smem, in_vmem],
         compiler_params=PARAMS,
     )((place % columns)[None], got)
@@ -425,20 +442,34 @@
             compiler_params=PARAMS,
         )(section[None], *args, *weights)
 
-    rows = section_call(
-        rows_body,
-        jax.ShapeDtypeStruct((groups, per_owner, width), BF16),
-        (means, picks, memory0),
-    )
+    before = section_call(
+        before_body,
+        jax.ShapeDtypeStruct((turns, nodes, width), BF16),
+        (means, memory0),
+    )
+    table = exchange(before, "dp", line)
     new_memory = section_call(
         memory_body, jax.ShapeDtypeStruct((nodes, width), F32), (means, memory0)
     )
-    slot_rows = exchange(rows, "dp").reshape(list_len, width)
-    cosines, new_memory = lax.optimization_barrier((cosines, new_memory))
+    def arrived(slot):
+        owner, spot = slot // per_owner, slot % per_owner
+        turn, peer = owner // peers, owner % peers
+        return (peer * turns + turn) * per_owner + spot
+
+    table, cosines, new_memory, end_spots, near_spots = lax.optimization_barrier(
+        (table, cosines, new_memory, arrived(endpoint_slots[0]), arrived(neighbor_slots[0]))
+    )
+    rows = dense_call(
+        rows_body,
+        jax.ShapeDtypeStruct((peers, turns * per_owner, width), BF16),
+        (picks, table),
+    )
+    slot_rows = exchange(rows, "dp", across).reshape(list_len, width)
+
     inputs = (
         slot_rows,
-        endpoint_slots[0],
-        neighbor_slots[0],
+        end_spots,
+        near_spots,
         cosines,
         score_grad,
         attn_weights,

time: 195 us -> 188 us (0.964)
  waiting for transfers between devices: 45.9 us -> 24.2 us
  blocking collectives: 96.5 us -> 113 us
  starting transfers between devices: 21.9 us -> 19.6 us
    all_to_all x2, waiting for transfers between devices: 45.9 us -> 24.2 us  [exchange(): lax.all_to_all(value, axis, split_axis=0, concat_axis=0, tiled=True, axis...]
    all_to_all x4 -> x5, blocking collectives: 62 us -> 80.7 us  [exchange(): lax.all_to_all(value, axis, split_axis=0, concat_axis=0, tiled=True, axis...]
    all_gather x1, blocking collectives: 34.5 us -> 32.1 us  [per_device(): got = lax.all_gather(sent, 'dp', axis=0, tiled=True, axis_index_groups=line)]
    all_to_all x2, starting transfers between devices: 21.9 us -> 19.6 us  [exchange(): lax.all_to_all(value, axis, split_axis=0, concat_axis=0, tiled=True, axis...]
  transfers between devices with their start and end apart: 2 -> 2, of which waited for: 2 -> 2; matrix products, arithmetic and copies ran while one was open for 5% -> 6% of each run, Pallas kernels for 1% -> 1%
where the time goes in v5:
time: 188 us; the launch traced here: 187 us
  blocking collectives  113 us (60%)
  waiting for transfers between devices  24.2 us (13%)
  starting transfers between devices  19.6 us (10%)
  Pallas kernels  18.3 us (10%)
  other arithmetic  11.3 us (6%)
    all_to_all x5, blocking collectives, exchange(): lax.all_to_all(value, axis, split_axis=0, concat_axis=0, tiled=True, axis...  80.7 us
    all_gather x1, blocking collectives, per_device(): got = lax.all_gather(sent, 'dp', axis=0, tiled=True, axis_index_groups=line)  32.1 us
    all_to_all x2, waiting for transfers between devices, exchange(): lax.all_to_all(value, axis, split_axis=0, concat_axis=0, tiled=True, axis...  24.2 us
    all_to_all x2, starting transfers between devices, exchange(): lax.all_to_all(value, axis, split_axis=0, concat_axis=0, tiled=True, axis...  19.6 us
    cos x1, other arithmetic, per_device(): cosines = jnp.cos(by_neighbour(neighbor_gap).astype(F32) * omega[None, :])  9.88 us
    pallas_call x1, Pallas kernels, per_device(): pl.pallas_call(event_body, out_shape=(jax.ShapeDtypeStruct((1, events), F...  8.91 us
  transfers between devices with their start and end apart: 2, of which 2 were waited for; matrix products, arithmetic and copies ran while one was open for 6% of the time, Pallas kernels for 1%

profile of v5, /device:TPU:1, one launch (start us, length us, event | category | flops | bytes accessed | tf_op | source)
XLA Modules:
  0.0 187.2 jit_solution(12356521461416371666)
XLA Ops:
  0.6 0.0 copy-start.3
  0.6 0.0 slice-start
  0.7 2.0 %shard_map.165 = (bf16[192,128]{1,0:T(8,128)(2,1)}, f32[2,8,128]{2,1,0:T(8,128)}) custom-call(bf16[186,128]{1,0:T(8,128)(2,1)} %bitcast.41, s32[2,128]{1,0:T(2,128)} %bitcast.43, s32[1,2048]{1,0:T(1,128)} %bitcast.42), custom_call_target="tpu_custom_call" | custom-call | tf_op jit(solution)/shard_map/pallas_call | solution.py:378
  2.7 32.1 %all_gather.3 = bf16[1536,128]{1,0:T(8,128)(2,1)S(1)} all-gather(bf16[192,128]{1,0:T(8,128)(2,1)} %get-tuple-element.15), channel_id=1, replica_groups={{0,8,16,24,32,40,48,56},{4,12,20,28,36,44,52,60},{1,9,17,25,33,41,49,57..., dimensions={0}, use_global_device_ids=true | all-gather | bytes 442368 | tf_op jit(solution)/shard_map/all_gather | solution.py:394
  34.7 1.2 shard_map.166
  35.9 0.0 copy-start.4
  35.9 0.0 copy-start.6
  36.0 0.0 copy-start.5
  36.0 0.0 copy-start.7
  36.0 11.1 %all_to_all.35.refs_1_.refs_0_ = bf16[8,208,128]{2,1,0:T(8,128)(2,1)S(1)} all-to-all(bf16[8,208,128]{2,1,0:T(8,128)(2,1)S(1)} %shard_map.166), channel_id=1, replica_groups={{0,1,2,3,4,5,6,7},{8,9,10,11,12,13,14,15},{16,17,18,19,20,21,22,23},{24..., dimensions={0} | all-to-all | bytes 851968 | tf_op jit(solution)/shard_map/all_to_all | solution.py:307
  47.1 1.0 shard_map.168
  48.1 12.6 %all-to-all-start.1 = ((bf16[8,192,128]{2,1,0:T(8,128)(2,1)}), bf16[8,192,128]{2,1,0:T(8,128)(2,1)S(1)}, u32[]{:S(2)}, u32[]{:S(2)}) async-start(bf16[8,192,128]{2,1,0:T(8,128)(2,1)} %shard_map.168), calls=%async_computation.1 | async-start | bytes 786432 | tf_op jit(solution)/shard_map/all_to_all | solution.py:307
  60.6 0.0 slice-done
  60.7 8.0 %all-to-all-done.1.refs_1_ = bf16[8,192,128]{2,1,0:T(8,128)(2,1)S(1)} async-done(((bf16[8,192,128]{2,1,0:T(8,128)(2,1)}), bf16[8,192,128]{2,1,0:T(8,128)(2,1)S(1)}, u32[]{:S(2)}, u32[]{:S(2)}) %all-to-all-start.1) | async-done | bytes 393248 | tf_op jit(solution)/shard_map/all_to_all | solution.py:307
  68.7 0.0 copy-done
  68.7 0.0 copy-done.2
  68.7 1.7 shard_map.169
  70.4 7.1 %all-to-all-start.2 = ((bf16[8,128,256]{2,1,0:T(8,128)(2,1)}), bf16[8,128,256]{2,1,0:T(8,128)(2,1)S(1)}, u32[]{:S(2)}, u32[]{:S(2)}) async-start(bf16[8,128,256]{2,1,0:T(8,128)(2,1)} %shard_map.169), calls=%async_computation.2 | async-start | bytes 1048576 | tf_op jit(solution)/shard_map/all_to_all | solution.py:307
  77.6 0.6 fusion.13.refs_1_
  78.2 0.6 fusion.3.refs_2_
  78.8 9.9 %multiply_cosine_fusion.refs_3_ = f32[2560,256]{1,0:T(8,128)} fusion(f32[256]{0:T(256)S(1)} %copy-done.7, f32[2560]{0:T(1024)S(1)} %convert_element_type.30), kind=kLoop, calls=%fused_computation | loop fusion | flops 655360 | bytes 2632704 | tf_op jit(solution)/shard_map/cos | solution.py:419
  88.7 0.7 shard_map.167.pick_ref
  89.4 1.6 shard_map.170
  91.0 16.2 %all-to-all-done.2.table_ref = bf16[8,128,256]{2,1,0:T(8,128)(2,1)S(1)} async-done(((bf16[8,128,256]{2,1,0:T(8,128)(2,1)}), bf16[8,128,256]{2,1,0:T(8,128)(2,1)S(1)}, u32[]{:S(2)}, u32[]{:S(2)}) %all-to-all-start.2) | async-done | bytes 524320 | tf_op jit(solution)/shard_map/all_to_all | solution.py:307
  107.2 0.4 shard_map.171
  107.6 16.1 %all_to_all.36 = bf16[8,256,256]{2,1,0:T(8,128)(2,1)} all-to-all(bf16[8,256,256]{2,1,0:T(8,128)(2,1)S(1)} %shard_map.171), channel_id=1, replica_groups={{0,1,2,3,4,5,6,7},{8,9,10,11,12,13,14,15},{16,17,18,19,20,21,22,23},{24..., dimensions={0} | all-to-all | bytes 2097152 | tf_op jit(solution)/shard_map/all_to_all | solution.py:307
  123.7 8.9 %shard_map.172 = (f32[1,128]{1,0:T(1,128)}, bf16[768,256]{1,0:T(8,128)(2,1)}) custom-call(bf16[2048,256]{1,0:T(8,128)(2,1)} %bitcast.37, s32[2,128]{1,0:T(2,128)} %fusion.13.refs_1_, s32[20,128]{1,0:T(8,128)} %fusion.3.refs_2_, f32[2560,256]{1,0:T(8,128)} %multiply_cosine_fusion.refs_3_, f32[1,128]{1,0:T(1,128)} %refs_4_.1, bf16[4,256,256]{2,1,0:T(8,128)(2,1)} %refs_5_.1, ...), custom_call_target="tpu_custom_call" | custom-call | tf_op jit(solution)/shard_map/pallas_call | solution.py:479
  132.6 17.4 %all_to_all.37 = bf16[32,24,256]{2,1,0:T(8,128)(2,1)S(1)} all-to-all(bf16[32,24,256]{2,1,0:T(8,128)(2,1)} %bitcast.38), channel_id=1, replica_groups={{0,1,2,3,64,65,66,67,128,129,130,131,192,193,194,195,256,257,258,259,32..., dimensions={0} | all-to-all | bytes 786432 | tf_op jit(solution)/shard_map/all_to_all | solution.py:307
  150.0 0.1 reduce_sum.24
  150.1 18.0 %all_to_all.38 = bf16[16,24,256]{2,1,0:T(8,128)(2,1)S(1)} all-to-all(bf16[16,24,256]{2,1,0:T(8,128)(2,1)S(1)} %broadcast_in_dim.38), channel_id=1, replica_groups={{0,4,8,12,16,20,24,28,32,36,40,44,48,52,56,60},{1,5,9,13,17,21,25,29,33..., dimensions={0} | all-to-all | bytes 393216 | tf_op jit(solution)/shard_map/all_to_all | solution.py:307
  168.2 18.1 %all_to_all.39.whole_ref = bf16[32,24,256]{2,1,0:T(8,128)(2,1)S(1)} all-to-all(bf16[32,24,256]{2,1,0:T(8,128)(2,1)S(1)} %broadcast_in_dim.39), channel_id=1, replica_groups={{0,1,2,3,64,65,66,67,128,129,130,131,192,193,194,195,256,257,258,259,32..., dimensions={0} | all-to-all | bytes 786432 | tf_op jit(solution)/shard_map/all_to_all | solution.py:307
  186.3 0.9 shard_map.173
  (19 shorter events, 0.2 us)
Async XLA Ops:
  0.6 60.0 %copy-start.3 = (bf16[186,256]{1,0:T(8,128)(2,1)S(1)}, bf16[186,256]{1,0:T(8,128)(2,1)}, u32[]{:S(2)}) copy-start(bf16[186,256]{1,0:T(8,128)(2,1)} %param.21) | copy-start | bytes 285700
  0.6 60.0 %slice-start = ((bf16[186,256]{1,0:T(8,128)(2,1)}), bf16[58,256]{1,0:T(8,128)(2,1)S(1)}, s32[]{:S(2)}) async-start(bf16[186,256]{1,0:T(8,128)(2,1)} %param.21), calls=%async_computation.7 | async-start | bytes 65536 | tf_op jit(solution)/shard_map/slice | solution.py:426
  0.7 68.1 %copy-start = (bf16[256,512]{1,0:T(8,128)(2,1)S(1)}, bf16[256,512]{1,0:T(8,128)(2,1)}, u32[]{:S(2)}) copy-start(bf16[256,512]{1,0:T(8,128)(2,1)} %refs_6_.4) | copy-start | bytes 786436
  0.7 68.1 %copy-start.1 = (f32[128,256]{1,0:T(8,128)S(1)}, f32[128,256]{1,0:T(8,128)}, u32[]{:S(2)}) copy-start(f32[128,256]{1,0:T(8,128)} %refs_2_.3) | copy-start | bytes 393220
  0.7 68.0 %copy-start.2 = (f32[512]{0:T(512)S(1)}, f32[512]{0:T(512)}, u32[]{:S(2)}) copy-start(f32[512]{0:T(512)} %param.23) | copy-start | bytes 6148
  35.9 41.6 %copy-start.4 = (s32[1,20,128]{2,0,1:T(1,128)S(1)}, s32[1,20,128]{2,0,1:T(1,128)}, u32[]{:S(2)}) copy-start(s32[1,20,128]{2,0,1:T(1,128)} %param.17) | copy-start | bytes 30724
  35.9 41.6 %copy-start.6 = (s32[1,2,128]{2,1,0:T(2,128)S(1)}, s32[1,2,128]{2,1,0:T(2,128)}, u32[]{:S(2)}) copy-start(s32[1,2,128]{2,1,0:T(2,128)} %param.15) | copy-start | bytes 3076
  36.0 42.3 %copy-start.5 = (s32[1,20,128]{2,0,1:T(1,128)S(1)}, s32[1,20,128]{2,0,1:T(1,128)}, u32[]{:S(2)}) copy-start(s32[1,20,128]{2,0,1:T(1,128)} %param.16) | copy-start | bytes 30724
  36.0 42.9 %copy-start.7 = (f32[256]{0:T(256)S(1)}, f32[256]{0:T(256)}, u32[]{:S(2)}) copy-start(f32[256]{0:T(256)} %param.24) | copy-start | bytes 3076
  48.1 20.6 %all-to-all-start.1 = ((bf16[8,192,128]{2,1,0:T(8,128)(2,1)}), bf16[8,192,128]{2,1,0:T(8,128)(2,1)S(1)}, u32[]{:S(2)}, u32[]{:S(2)}) async-start(bf16[8,192,128]{2,1,0:T(8,128)(2,1)} %shard_map.168), calls=%async_computation.1 | async-start | bytes 786432 | tf_op jit(solution)/shard_map/all_to_all | solution.py:307
  70.4 36.7 %all-to-all-start.2 = ((bf16[8,128,256]{2,1,0:T(8,128)(2,1)}), bf16[8,128,256]{2,1,0:T(8,128)(2,1)S(1)}, u32[]{:S(2)}, u32[]{:S(2)}) async-start(bf16[8,128,256]{2,1,0:T(8,128)(2,1)} %shard_map.169), calls=%async_computation.2 | async-start | bytes 1048576 | tf_op jit(solution)/shard_map/all_to_all | solution.py:307

commit v6 on v5

--- a/solution.py
+++ b/solution.py
@@ -197,9 +197,8 @@
 def before_body(rest, section_ref, mean_ref, memory_ref, *refs):
     weights, out_ref = refs[:-1], refs[-1]
     batches = mean_ref.shape[0] - 1
-    before = advance(rest, section_ref[0], mean_ref, batches, memory_ref, weights).astype(BF16)
-    for turn in range(out_ref.shape[0]):
-        out_ref[turn] = before
+    before = advance(rest, section_ref[0], mean_ref, batches, memory_ref, weights)
+    out_ref[...] = before.astype(BF16)
 
 
 def rows_body(pick_ref, table_ref, out_ref):
@@ -218,12 +217,16 @@
 
 
 def event_body(*refs):
-    sources, (scores_ref, grads_ref), targets = refs[:8], refs[8:10], refs[10:18]
-    feat_ref, sems = refs[18:]
-    rows_ref, ends_ref, near_ref, cos_ref, cot_ref, attn_ref, pred_ref, pred_out_ref = targets
+    sources, (scores_ref, grads_ref), targets = refs[:9], refs[9:11], refs[11:20]
+    feat_ref, sems = refs[20:]
+    rows_ref, ends_ref, near_ref, early_ref, late_ref = targets[:5]
+    cot_ref, attn_ref, pred_ref, pred_out_ref = targets[5:]
     started = copies(sources, targets, sems)
-    rows_copy, ends_copy, near_copy, cos_copy, cot_copy, attn_copy, pred_copy, out_copy = started
-    for copy in (ends_copy, rows_copy, near_copy, cos_copy, attn_copy, cot_copy, out_copy, pred_copy):
+    rows_copy, ends_copy, near_copy, early_copy, late_copy = started[:5]
+    cot_copy, attn_copy, pred_copy, out_copy = started[5:]
+    for copy in (ends_copy, rows_copy, near_copy, early_copy, late_copy):
+        copy.start()
+    for copy in (attn_copy, cot_copy, out_copy, pred_copy):
         copy.start()
     ends_copy.wait()
     rows_copy.wait()
@@ -249,9 +252,14 @@
         spot = slice(near * pair, (near + 1) * pair)
         other = near_count + near
         feat = fetch(near_ref[near : near + 1, :], near_ref[other : other + 1, :])
+        half = near_count // 2
         if near == 0:
-            cos_copy.wait()
-        feat_ref[spot, :] = (feat + cos_ref[spot, :]).astype(BF16)
+            early_copy.wait()
+        if near == half:
+            late_copy.wait()
+        cos_ref = early_ref if near < half else late_ref
+        cosines = cos_ref[near % half * pair : (near % half + 1) * pair, :]
+        feat_ref[spot, :] = (feat + cosines).astype(BF16)
     attn_copy.wait()
     query = dot(own.astype(BF16), attn_ref[0]) * (1.0 / math.sqrt(head_dim))
     keys = dot(feat_ref[...], attn_ref[1])
@@ -416,13 +424,28 @@
     def by_neighbour(value):
         return jnp.swapaxes(value[0].reshape(2, near_count, events), 0, 1).reshape(pairs, 1)
 
-    cosines = jnp.cos(by_neighbour(neighbor_gap).astype(F32) * omega[None, :])
+    gaps = by_neighbour(neighbor_gap).astype(F32)
+    cut = pairs // 2
+    early = jnp.cos(gaps[:cut] * omega[None, :])
     means = dense_call(
         lambda *refs: mean_body(rest, nodes, *refs),
         jax.ShapeDtypeStruct((batches, nodes + nodes // 2, LANES), BF16),
         (got,),
     )
-    means = exchange(means, "tm")
+    def arrived(slot):
+        owner, spot = slot // per_owner, slot % per_owner
+        turn, peer = owner // peers, owner % peers
+        return (peer * turns + turn) * per_owner + spot
+
+    means, picks, early, end_spots, near_spots = lax.optimization_barrier(
+        (
+            exchange(means, "tm"),
+            picks,
+            early,
+            arrived(endpoint_slots[0]),
+            arrived(neighbor_slots[0]),
+        )
+    )
     tail_w = jnp.pad(msg_weight[LANES:], ((0, HALF - rest), (0, 0)))
     section = lax.axis_index("tm").astype(jnp.int32)
     weights = (
@@ -444,33 +467,30 @@
 
     before = section_call(
         before_body,
-        jax.ShapeDtypeStruct((turns, nodes, width), BF16),
+        jax.ShapeDtypeStruct((nodes, width), BF16),
         (means, memory0),
     )
-    table = exchange(before, "dp", line)
+    table = lax.all_gather(before, "dp", axis=0, tiled=True, axis_index_groups=line)
+    table = table.reshape(turns, nodes, width)
     new_memory = section_call(
         memory_body, jax.ShapeDtypeStruct((nodes, width), F32), (means, memory0)
-    )
-    def arrived(slot):
-        owner, spot = slot // per_owner, slot % per_owner
-        turn, peer = owner // peers, owner % peers
-        return (peer * turns + turn) * per_owner + spot
-
-    table, cosines, new_memory, end_spots, near_spots = lax.optimization_barrier(
-        (table, cosines, new_memory, arrived(endpoint_slots[0]), arrived(neighbor_slots[0]))
     )
     rows = dense_call(
         rows_body,
         jax.ShapeDtypeStruct((peers, turns * per_owner, width), BF16),
         (picks, table),
     )
+    rows, omega_late = lax.optimization_barrier((rows, omega))
     slot_rows = exchange(rows, "dp", across).reshape(list_len, width)
+    late = jnp.cos(gaps[cut:] * omega_late[None, :])
+    late, new_memory = lax.optimization_barrier((late, new_memory))
 
     inputs = (
         slot_rows,
         end_spots,
         near_spots,
-        cosines,
+        early,
+        late,
         score_grad,
         attn_weights,
         pred_weights,

time: 188 us -> 180 us (0.957)
  waiting for transfers between devices: 24.2 us -> 9.56 us
  blocking collectives: 113 us -> 116 us
    all_gather x0 -> x1, blocking collectives: none -> 24.8 us  [per_device(): lax.all_gather(before, 'dp', axis=0, tiled=True, axis_index_groups=line)]
    all_to_all x5 -> x3, blocking collectives: 80.7 us -> 58.7 us  [exchange(): lax.all_to_all(value, axis, split_axis=0, concat_axis=0, tiled=True, axis...]
    all_to_all x2 -> x3, waiting for transfers between devices: 24.2 us -> 9.56 us  [exchange(): lax.all_to_all(value, axis, split_axis=0, concat_axis=0, tiled=True, axis...]
    all_to_all x2 -> x3, starting transfers between devices: 19.6 us -> 21.3 us  [exchange(): lax.all_to_all(value, axis, split_axis=0, concat_axis=0, tiled=True, axis...]
    cos x1 -> x2, other arithmetic: 9.88 us -> 10.7 us  [the longest x1 5.38 us: per_device(): early = jnp.cos(gaps[:cut] * omega[None, :])]
  transfers between devices with their start and end apart: 2 -> 3, of which waited for: 2 -> 3; matrix products, arithmetic and copies ran while one was open for 6% -> 7% of each run, Pallas kernels for 1% -> 1%
where the time goes in v6:
time: 180 us
  blocking collectives  116 us (64%)
  starting transfers between devices  21.3 us (12%)
  Pallas kernels  20 us (11%)
  other arithmetic  12.1 us (7%)
  waiting for transfers between devices  9.56 us (5%)
    all_to_all x3, blocking collectives, exchange(): lax.all_to_all(value, axis, split_axis=0, concat_axis=0, tiled=True, axis...  58.7 us
    all_gather x1, blocking collectives, per_device(): got = lax.all_gather(sent, 'dp', axis=0, tiled=True, axis_index_groups=line)  32.1 us
    all_gather x1, blocking collectives, per_device(): lax.all_gather(before, 'dp', axis=0, tiled=True, axis_index_groups=line)  24.8 us
    all_to_all x3, starting transfers between devices, exchange(): lax.all_to_all(value, axis, split_axis=0, concat_axis=0, tiled=True, axis...  21.3 us
    pallas_call x1, Pallas kernels, per_device(): pl.pallas_call(event_body, out_shape=(jax.ShapeDtypeStruct((1, events), F...  9.69 us
    all_to_all x3, waiting for transfers between devices, exchange(): lax.all_to_all(value, axis, split_axis=0, concat_axis=0, tiled=True, axis...  9.56 us
    cos x1, other arithmetic, per_device(): early = jnp.cos(gaps[:cut] * omega[None, :])  5.38 us
    cos x1, other arithmetic, per_device(): late = jnp.cos(gaps[cut:] * omega_late[None, :])  5.34 us
  transfers between devices with their start and end apart: 3, of which 3 were waited for; matrix products, arithmetic and copies ran while one was open for 7% of the time, Pallas kernels for 1%

profile of v6, /device:TPU:1, one launch (start us, length us, event | category | flops | bytes accessed | tf_op | source)
XLA Modules:
  0.0 179.6 jit_solution(16168941153788471013)
XLA Ops:
  0.6 0.0 copy-start.4
  0.6 0.0 copy-start.7
  0.7 1.9 %shard_map.165 = (bf16[192,128]{1,0:T(8,128)(2,1)}, f32[2,8,128]{2,1,0:T(8,128)}) custom-call(bf16[186,128]{1,0:T(8,128)(2,1)} %bitcast.44, s32[2,128]{1,0:T(2,128)} %bitcast.46, s32[1,2048]{1,0:T(1,128)} %bitcast.45), custom_call_target="tpu_custom_call" | custom-call | tf_op jit(solution)/shard_map/pallas_call | solution.py:386
  2.6 32.1 %all_gather.6 = bf16[1536,128]{1,0:T(8,128)(2,1)S(1)} all-gather(bf16[192,128]{1,0:T(8,128)(2,1)} %get-tuple-element.19), channel_id=1, replica_groups={{0,8,16,24,32,40,48,56},{4,12,20,28,36,44,52,60},{1,9,17,25,33,41,49,57..., dimensions={0}, use_global_device_ids=true | all-gather | bytes 442368 | tf_op jit(solution)/shard_map/all_gather | solution.py:402
  34.6 2.0 %shard_map.166 = bf16[8,208,128]{2,1,0:T(8,128)(2,1)} custom-call(s32[1]{0:T(128)} %bitcast.refs_0_, bf16[8,192,128]{2,1,0:T(8,128)(2,1)S(1)} %bitcast.38, f32[2,8,128]{2,1,0:T(8,128)} %get-tuple-element.20.refs_2_), custom_call_target="tpu_custom_call" | custom-call | tf_op jit(solution)/shard_map/pallas_call | solution.py:404
  36.6 4.2 %all-to-all-start = ((bf16[8,208,128]{2,1,0:T(8,128)(2,1)}), bf16[8,208,128]{2,1,0:T(8,128)(2,1)S(1)}, u32[]{:S(2)}, u32[]{:S(2)}) async-start(bf16[8,208,128]{2,1,0:T(8,128)(2,1)} %shard_map.166), calls=%async_computation | async-start | bytes 851968 | tf_op jit(solution)/shard_map/all_to_all | solution.py:315
  40.8 0.0 copy-done.4
  40.9 0.0 copy-start.6
  40.9 0.0 copy-start.3
  40.9 0.0 slice-start
  40.9 5.4 %multiply_cosine_fusion.1.refs_3_ = f32[1280,256]{1,0:T(8,128)} fusion(f32[256]{0:T(256)S(1)} %copy-done.7, f32[1280]{0:T(1024)S(1)} %mul.46), kind=kLoop, calls=%fused_computation.1 | loop fusion | flops 327680 | bytes 1316864 | tf_op jit(solution)/shard_map/cos | solution.py:429
  46.3 1.2 all-to-all-done.refs_0_.refs_1_
  47.5 1.0 shard_map.167
  48.5 12.7 %all-to-all-start.1 = ((bf16[8,192,128]{2,1,0:T(8,128)(2,1)}), bf16[8,192,128]{2,1,0:T(8,128)(2,1)S(1)}, u32[]{:S(2)}, u32[]{:S(2)}) async-start(bf16[8,192,128]{2,1,0:T(8,128)(2,1)} %shard_map.167), calls=%async_computation.1 | async-start | bytes 786432 | tf_op jit(solution)/shard_map/all_to_all | solution.py:315
  61.2 0.6 fusion.13.refs_1_
  61.9 0.6 fusion.3.refs_2_
  62.5 0.7 shard_map.168.pick_ref
  63.2 6.1 %all-to-all-done.1.refs_1_ = bf16[8,192,128]{2,1,0:T(8,128)(2,1)S(1)} async-done(((bf16[8,192,128]{2,1,0:T(8,128)(2,1)}), bf16[8,192,128]{2,1,0:T(8,128)(2,1)S(1)}, u32[]{:S(2)}, u32[]{:S(2)}) %all-to-all-start.1) | async-done | bytes 393248 | tf_op jit(solution)/shard_map/all_to_all | solution.py:315
  69.3 0.0 copy-done.2
  69.3 0.9 shard_map.169
  70.2 24.8 %all_gather.7 = bf16[1024,256]{1,0:T(8,128)(2,1)S(1)} all-gather(bf16[128,256]{1,0:T(8,128)(2,1)S(1)} %shard_map.169), channel_id=1, replica_groups={{0,8,16,24,32,40,48,56},{4,12,20,28,36,44,52,60},{1,9,17,25,33,41,49,57..., dimensions={0}, use_global_device_ids=true | all-gather | bytes 589824 | tf_op jit(solution)/shard_map/all_gather | solution.py:473
  95.0 1.4 shard_map.170
  96.4 4.4 %all-to-all-start.2 = ((bf16[8,256,256]{2,1,0:T(8,128)(2,1)}), bf16[8,256,256]{2,1,0:T(8,128)(2,1)}, u32[]{:S(2)}, u32[]{:S(2)}) async-start(bf16[8,256,256]{2,1,0:T(8,128)(2,1)} %shard_map.170), calls=%async_computation.2 | async-start | bytes 2097152 | tf_op jit(solution)/shard_map/all_to_all | solution.py:315
  100.9 1.6 shard_map.171
  102.5 5.3 %multiply_cosine_fusion.refs_4_ = f32[1280,256]{1,0:T(8,128)} fusion(f32[256]{0:T(256)S(1)} %copy-done.7, f32[1280]{0:T(1024)S(1)} %mul.54), kind=kLoop, calls=%fused_computation | loop fusion | flops 327680 | bytes 1316864 | tf_op jit(solution)/shard_map/cos | solution.py:485
  107.9 2.3 %all-to-all-done.2 = bf16[8,256,256]{2,1,0:T(8,128)(2,1)} async-done(((bf16[8,256,256]{2,1,0:T(8,128)(2,1)}), bf16[8,256,256]{2,1,0:T(8,128)(2,1)}, u32[]{:S(2)}, u32[]{:S(2)}) %all-to-all-start.2) | async-done | bytes 1048608 | tf_op jit(solution)/shard_map/all_to_all | solution.py:315
  110.1 9.7 %shard_map.172 = (f32[1,128]{1,0:T(1,128)}, bf16[768,256]{1,0:T(8,128)(2,1)}) custom-call(bf16[2048,256]{1,0:T(8,128)(2,1)} %bitcast.11.refs_0_, s32[2,128]{1,0:T(2,128)} %fusion.13.refs_1_, s32[20,128]{1,0:T(8,128)} %fusion.3.refs_2_, f32[1280,256]{1,0:T(8,128)} %multiply_cosine_fusion.1.refs_3_, f32[1280,256]{1,0:T(8,128)} %multiply_cosine_fusion.refs_4_, ...), custom_call_target="tpu_custom_call" | custom-call | tf_op jit(solution)/shard_map/pallas_call | solution.py:499
  119.8 21.4 %all_to_all.30 = bf16[32,24,256]{2,1,0:T(8,128)(2,1)S(1)} all-to-all(bf16[32,24,256]{2,1,0:T(8,128)(2,1)} %bitcast.41), channel_id=1, replica_groups={{0,1,2,3,64,65,66,67,128,129,130,131,192,193,194,195,256,257,258,259,32..., dimensions={0} | all-to-all | bytes 786432 | tf_op jit(solution)/shard_map/all_to_all | solution.py:315
  141.2 0.1 reduce_sum.24
  141.3 19.4 %all_to_all.31 = bf16[16,24,256]{2,1,0:T(8,128)(2,1)S(1)} all-to-all(bf16[16,24,256]{2,1,0:T(8,128)(2,1)S(1)} %broadcast_in_dim.39), channel_id=1, replica_groups={{0,4,8,12,16,20,24,28,32,36,40,44,48,52,56,60},{1,5,9,13,17,21,25,29,33..., dimensions={0} | all-to-all | bytes 393216 | tf_op jit(solution)/shard_map/all_to_all | solution.py:315
  160.8 18.0 %all_to_all.32.whole_ref = bf16[32,24,256]{2,1,0:T(8,128)(2,1)S(1)} all-to-all(bf16[32,24,256]{2,1,0:T(8,128)(2,1)S(1)} %broadcast_in_dim.40), channel_id=1, replica_groups={{0,1,2,3,64,65,66,67,128,129,130,131,192,193,194,195,256,257,258,259,32..., dimensions={0} | all-to-all | bytes 786432 | tf_op jit(solution)/shard_map/all_to_all | solution.py:315
  178.7 0.9 shard_map.173
  (24 shorter events, 0.2 us)
Async XLA Ops:
  0.6 40.2 %copy-start.4 = (s32[1,20,128]{2,0,1:T(1,128)S(1)}, s32[1,20,128]{2,0,1:T(1,128)}, u32[]{:S(2)}) copy-start(s32[1,20,128]{2,0,1:T(1,128)} %param.17) | copy-start | bytes 30724
  0.6 40.3 %copy-start.7 = (f32[256]{0:T(256)S(1)}, f32[256]{0:T(256)}, u32[]{:S(2)}) copy-start(f32[256]{0:T(256)} %param.24) | copy-start | bytes 3076
  36.6 10.9 %all-to-all-start = ((bf16[8,208,128]{2,1,0:T(8,128)(2,1)}), bf16[8,208,128]{2,1,0:T(8,128)(2,1)S(1)}, u32[]{:S(2)}, u32[]{:S(2)}) async-start(bf16[8,208,128]{2,1,0:T(8,128)(2,1)} %shard_map.166), calls=%async_computation | async-start | bytes 851968 | tf_op jit(solution)/shard_map/all_to_all | solution.py:315
  40.9 20.3 %copy-start.6 = (s32[1,2,128]{2,1,0:T(2,128)S(1)}, s32[1,2,128]{2,1,0:T(2,128)}, u32[]{:S(2)}) copy-start(s32[1,2,128]{2,1,0:T(2,128)} %param.15) | copy-start | bytes 3076
  40.9 20.9 %copy-start.3 = (bf16[186,256]{1,0:T(8,128)(2,1)S(1)}, bf16[186,256]{1,0:T(8,128)(2,1)}, u32[]{:S(2)}) copy-start(bf16[186,256]{1,0:T(8,128)(2,1)} %param.21) | copy-start | bytes 285700
  40.9 20.9 %slice-start = ((bf16[186,256]{1,0:T(8,128)(2,1)}), bf16[58,256]{1,0:T(8,128)(2,1)S(1)}, s32[]{:S(2)}) async-start(bf16[186,256]{1,0:T(8,128)(2,1)} %param.21), calls=%async_computation.6 | async-start | bytes 65536 | tf_op jit(solution)/shard_map/slice | solution.py:449
  46.3 15.6 %copy-start.5 = (s32[1,20,128]{2,0,1:T(1,128)S(1)}, s32[1,20,128]{2,0,1:T(1,128)}, u32[]{:S(2)}) copy-start(s32[1,20,128]{2,0,1:T(1,128)} %param.16) | copy-start | bytes 30724
  48.5 20.8 %copy-start = (bf16[256,512]{1,0:T(8,128)(2,1)S(1)}, bf16[256,512]{1,0:T(8,128)(2,1)}, u32[]{:S(2)}) copy-start(bf16[256,512]{1,0:T(8,128)(2,1)} %refs_6_.4) | copy-start | bytes 786436
  48.5 20.8 %copy-start.1 = (f32[128,256]{1,0:T(8,128)S(1)}, f32[128,256]{1,0:T(8,128)}, u32[]{:S(2)}) copy-start(f32[128,256]{1,0:T(8,128)} %refs_2_.3) | copy-start | bytes 393220
  48.5 20.8 %copy-start.2 = (f32[512]{0:T(512)S(1)}, f32[512]{0:T(512)}, u32[]{:S(2)}) copy-start(f32[512]{0:T(512)} %param.23) | copy-start | bytes 6148
  48.5 20.8 %all-to-all-start.1 = ((bf16[8,192,128]{2,1,0:T(8,128)(2,1)}), bf16[8,192,128]{2,1,0:T(8,128)(2,1)S(1)}, u32[]{:S(2)}, u32[]{:S(2)}) async-start(bf16[8,192,128]{2,1,0:T(8,128)(2,1)} %shard_map.167), calls=%async_computation.1 | async-start | bytes 786432 | tf_op jit(solution)/shard_map/all_to_all | solution.py:315
  96.4 13.7 %all-to-all-start.2 = ((bf16[8,256,256]{2,1,0:T(8,128)(2,1)}), bf16[8,256,256]{2,1,0:T(8,128)(2,1)}, u32[]{:S(2)}, u32[]{:S(2)}) async-start(bf16[8,256,256]{2,1,0:T(8,128)(2,1)} %shard_map.170), calls=%async_computation.2 | async-start | bytes 2097152 | tf_op jit(solution)/shard_map/all_to_all | solution.py:315

commit v7 on v6

--- a/solution.py
+++ b/solution.py
@@ -224,12 +224,12 @@
     started = copies(sources, targets, sems)
     rows_copy, ends_copy, near_copy, early_copy, late_copy = started[:5]
     cot_copy, attn_copy, pred_copy, out_copy = started[5:]
-    for copy in (ends_copy, rows_copy, near_copy, early_copy, late_copy):
-        copy.start()
-    for copy in (attn_copy, cot_copy, out_copy, pred_copy):
+    for copy in (ends_copy, rows_copy, near_copy):
         copy.start()
     ends_copy.wait()
     rows_copy.wait()
+    for copy in (early_copy, attn_copy, late_copy, cot_copy, out_copy, pred_copy):
+        copy.start()
     slots, width = rows_ref.shape
     events = ends_ref.shape[1]
     pair = 2 * events
@@ -298,17 +298,26 @@
     cot = jnp.sum(jnp.where(diagonal, cot_ref[...], 0.0), axis=1, keepdims=True)
     slope = (cot * pred_out * (gate * (1.0 + pre * (1.0 - gate)))).astype(BF16)
     back = jnp.concatenate([dot(slope, pred_ref[0], NT), dot(slope, pred_ref[1], NT)], axis=0)
-    grads_ref[0:width, :] = dot(mixed, back.astype(BF16), TN).astype(BF16)
-    grads_ref[width : 2 * width, :] = dot(source, slope, TN).astype(BF16)
-    grads_ref[2 * width :, :] = dot(target, slope, TN).astype(BF16)
+    halves = width // LANES
+    for index, (left, right) in enumerate(
+        ((mixed, back.astype(BF16)), (source, slope), (target, slope))
+    ):
+        grad = dot(left, right, TN).astype(BF16)
+        for half in range(halves):
+            start = (index * halves + half) * width
+            grads_ref[start : start + width, :] = grad[:, half * LANES : (half + 1) * LANES]
 
 
 def grads_body(whole_ref, first_ref, rest_ref):
     width = first_ref.shape[0]
-    whole = whole_ref[...].astype(F32).reshape(3 * width, width)
-    first_ref[...] = whole[:width]
-    for part in range(2):
-        rest_ref[part] = whole[(part + 1) * width : (part + 2) * width]
+    halves = width // LANES
+    whole = whole_ref[...].astype(F32).reshape(3 * halves * width, LANES)
+    for half in range(halves):
+        spot = slice(half * LANES, (half + 1) * LANES)
+        first_ref[:, spot] = whole[half * width : (half + 1) * width]
+        for part in range(2):
+            start = ((part + 1) * halves + half) * width
+            rest_ref[part, :, spot] = whole[start : start + width]
 
 
 def exchange(value, axis, groups=None):
@@ -317,30 +326,25 @@
     )
 
 
-def sum_everywhere(grads, columns, rings):
+def sum_everywhere(grads, line, peers, width):
     sections = lax.axis_size("tm")
-    plane = [
-        [
-            (section * rings + ring) * columns + column
-            for section in range(sections)
-            for column in range(columns)
-        ]
-        for ring in range(rings)
+    turns = len(line[0])
+    near = [
+        [(section * turns + turn) * peers + peer for section in range(sections) for peer in range(peers)]
+        for turn in range(turns)
     ]
-    line = [[ring * columns + column for ring in range(rings)] for column in range(columns)]
-    peers = len(plane[0])
-    rows, width = grads.shape
-    own = rows // peers
-    pieces = exchange(grads.reshape(peers, own, width), ("tm", "dp"), plane)
+    group = len(near[0])
+    own = grads.shape[0] // group
+    pieces = exchange(grads.reshape(group, own, LANES), ("tm", "dp"), near)
     mine = jnp.sum(pieces.astype(F32), axis=0).astype(BF16)
-    pieces = exchange(jnp.broadcast_to(mine[None], (rings, own, width)), "dp", line)
+    pieces = exchange(jnp.broadcast_to(mine[None], (turns, own, LANES)), "dp", line)
     mine = jnp.sum(pieces.astype(F32), axis=0).astype(BF16)
-    whole = exchange(jnp.broadcast_to(mine[None], (peers, own, width)), ("tm", "dp"), plane)
+    whole = exchange(jnp.broadcast_to(mine[None], (group, own, LANES)), ("tm", "dp"), near)
     return dense_call(
         grads_body,
         (
             jax.ShapeDtypeStruct((width, width), F32),
-            jax.ShapeDtypeStruct((rows // width - 1, width, width), F32),
+            jax.ShapeDtypeStruct((2, width, width), F32),
         ),
         (whole,),
     )
@@ -500,14 +504,14 @@
         event_body,
         out_shape=(
             jax.ShapeDtypeStruct((1, events), F32),
-            jax.ShapeDtypeStruct((3 * width, width), BF16),
+            jax.ShapeDtypeStruct((3 * width * width // LANES, LANES), BF16),
         ),
         in_specs=[pl.BlockSpec(memory_space=pltpu.HBM)] * len(inputs),
         scratch_shapes=[pltpu.VMEM(value.shape, value.dtype) for value in inputs]
         + [pltpu.VMEM((pairs, width), BF16), pltpu.SemaphoreType.DMA((len(inputs),))],
         compiler_params=ALONE,
     )(*inputs)
-    grad_out, grad_pair = sum_everywhere(grads, columns, rings)
+    grad_out, grad_pair = sum_everywhere(grads, line, peers, width)
     return (scores, new_memory[None], grad_out, grad_pair)
 
 

time: 180 us -> 180 us (level)
  no operation moved by 1% of the time
where the time goes in v7:
time: 180 us
  blocking collectives  116 us (64%)
  starting transfers between devices  21.3 us (12%)
  Pallas kernels  20 us (11%)
  other arithmetic  12.1 us (7%)
  waiting for transfers between devices  9.56 us (5%)
    all_to_all x3, blocking collectives, exchange(): lax.all_to_all(value, axis, split_axis=0, concat_axis=0, tiled=True, axis...  58.7 us
    all_gather x1, blocking collectives, per_device(): got = lax.all_gather(sent, 'dp', axis=0, tiled=True, axis_index_groups=line)  32.1 us
    all_gather x1, blocking collectives, per_device(): lax.all_gather(before, 'dp', axis=0, tiled=True, axis_index_groups=line)  24.8 us
    all_to_all x3, starting transfers between devices, exchange(): lax.all_to_all(value, axis, split_axis=0, concat_axis=0, tiled=True, axis...  21.3 us
    pallas_call x1, Pallas kernels, per_device(): pl.pallas_call(event_body, out_shape=(jax.ShapeDtypeStruct((1, events), F...  9.69 us
    all_to_all x3, waiting for transfers between devices, exchange(): lax.all_to_all(value, axis, split_axis=0, concat_axis=0, tiled=True, axis...  9.56 us
    cos x1, other arithmetic, per_device(): early = jnp.cos(gaps[:cut] * omega[None, :])  5.38 us
    cos x1, other arithmetic, per_device(): late = jnp.cos(gaps[cut:] * omega_late[None, :])  5.34 us
  transfers between devices with their start and end apart: 3, of which 3 were waited for; matrix products, arithmetic and copies ran while one was open for 7% of the time, Pallas kernels for 1%

profile of v7, /device:TPU:1, one launch (start us, length us, event | category | flops | bytes accessed | tf_op | source)
XLA Modules:
  0.0 179.6 jit_solution(14304601657608560668)
XLA Ops:
  0.6 0.0 copy-start.4
  0.7 1.9 %shard_map.165 = (bf16[192,128]{1,0:T(8,128)(2,1)}, f32[2,8,128]{2,1,0:T(8,128)}) custom-call(bf16[186,128]{1,0:T(8,128)(2,1)} %bitcast.44, s32[2,128]{1,0:T(2,128)} %bitcast.46, s32[1,2048]{1,0:T(1,128)} %bitcast.45), custom_call_target="tpu_custom_call" | custom-call | tf_op jit(solution)/shard_map/pallas_call | solution.py:390
  2.6 32.1 %all_gather.6 = bf16[1536,128]{1,0:T(8,128)(2,1)S(1)} all-gather(bf16[192,128]{1,0:T(8,128)(2,1)} %get-tuple-element.19), channel_id=1, replica_groups={{0,8,16,24,32,40,48,56},{4,12,20,28,36,44,52,60},{1,9,17,25,33,41,49,57..., dimensions={0}, use_global_device_ids=true | all-gather | bytes 442368 | tf_op jit(solution)/shard_map/all_gather | solution.py:406
  34.6 2.0 %shard_map.166 = bf16[8,208,128]{2,1,0:T(8,128)(2,1)} custom-call(s32[1]{0:T(128)} %bitcast.refs_0_, bf16[8,192,128]{2,1,0:T(8,128)(2,1)S(1)} %bitcast.38, f32[2,8,128]{2,1,0:T(8,128)} %get-tuple-element.20.refs_2_), custom_call_target="tpu_custom_call" | custom-call | tf_op jit(solution)/shard_map/pallas_call | solution.py:408
  36.6 4.2 %all-to-all-start = ((bf16[8,208,128]{2,1,0:T(8,128)(2,1)}), bf16[8,208,128]{2,1,0:T(8,128)(2,1)S(1)}, u32[]{:S(2)}, u32[]{:S(2)}) async-start(bf16[8,208,128]{2,1,0:T(8,128)(2,1)} %shard_map.166), calls=%async_computation | async-start | bytes 851968 | tf_op jit(solution)/shard_map/all_to_all | solution.py:324
  40.9 0.0 copy-start.6
  40.9 0.0 copy-start.3
  40.9 0.0 slice-start
  40.9 5.4 %multiply_cosine_fusion.1.refs_3_ = f32[1280,256]{1,0:T(8,128)} fusion(f32[256]{0:T(256)S(1)} %copy-done.7, f32[1280]{0:T(1024)S(1)} %mul.46), kind=kLoop, calls=%fused_computation.1 | loop fusion | flops 327680 | bytes 1316864 | tf_op jit(solution)/shard_map/cos | solution.py:433
  46.3 1.2 all-to-all-done.refs_0_.refs_1_
  47.5 1.0 shard_map.167
  48.5 12.7 %all-to-all-start.1 = ((bf16[8,192,128]{2,1,0:T(8,128)(2,1)}), bf16[8,192,128]{2,1,0:T(8,128)(2,1)S(1)}, u32[]{:S(2)}, u32[]{:S(2)}) async-start(bf16[8,192,128]{2,1,0:T(8,128)(2,1)} %shard_map.167), calls=%async_computation.1 | async-start | bytes 786432 | tf_op jit(solution)/shard_map/all_to_all | solution.py:324
  61.2 0.0 copy-done.6
  61.2 0.6 fusion.13.refs_1_
  61.9 0.6 fusion.3.refs_2_
  62.5 0.7 shard_map.168.pick_ref
  63.2 6.1 %all-to-all-done.1.refs_1_ = bf16[8,192,128]{2,1,0:T(8,128)(2,1)S(1)} async-done(((bf16[8,192,128]{2,1,0:T(8,128)(2,1)}), bf16[8,192,128]{2,1,0:T(8,128)(2,1)S(1)}, u32[]{:S(2)}, u32[]{:S(2)}) %all-to-all-start.1) | async-done | bytes 393248 | tf_op jit(solution)/shard_map/all_to_all | solution.py:324
  69.3 0.0 copy-done.1
  69.3 0.9 shard_map.169
  70.2 24.8 %all_gather.7 = bf16[1024,256]{1,0:T(8,128)(2,1)S(1)} all-gather(bf16[128,256]{1,0:T(8,128)(2,1)S(1)} %shard_map.169), channel_id=1, replica_groups={{0,8,16,24,32,40,48,56},{4,12,20,28,36,44,52,60},{1,9,17,25,33,41,49,57..., dimensions={0}, use_global_device_ids=true | all-gather | bytes 589824 | tf_op jit(solution)/shard_map/all_gather | solution.py:477
  95.0 1.4 shard_map.170
  96.4 4.4 %all-to-all-start.2 = ((bf16[8,256,256]{2,1,0:T(8,128)(2,1)}), bf16[8,256,256]{2,1,0:T(8,128)(2,1)}, u32[]{:S(2)}, u32[]{:S(2)}) async-start(bf16[8,256,256]{2,1,0:T(8,128)(2,1)} %shard_map.170), calls=%async_computation.2 | async-start | bytes 2097152 | tf_op jit(solution)/shard_map/all_to_all | solution.py:324
  100.9 1.6 shard_map.171
  102.5 5.3 %multiply_cosine_fusion.refs_4_ = f32[1280,256]{1,0:T(8,128)} fusion(f32[256]{0:T(256)S(1)} %copy-done.7, f32[1280]{0:T(1024)S(1)} %mul.54), kind=kLoop, calls=%fused_computation | loop fusion | flops 327680 | bytes 1316864 | tf_op jit(solution)/shard_map/cos | solution.py:489
  107.9 2.3 %all-to-all-done.2 = bf16[8,256,256]{2,1,0:T(8,128)(2,1)} async-done(((bf16[8,256,256]{2,1,0:T(8,128)(2,1)}), bf16[8,256,256]{2,1,0:T(8,128)(2,1)}, u32[]{:S(2)}, u32[]{:S(2)}) %all-to-all-start.2) | async-done | bytes 1048608 | tf_op jit(solution)/shard_map/all_to_all | solution.py:324
  110.1 9.7 %shard_map.172 = (f32[1,128]{1,0:T(1,128)}, bf16[1536,128]{1,0:T(8,128)(2,1)}) custom-call(bf16[2048,256]{1,0:T(8,128)(2,1)} %bitcast.11.refs_0_, s32[2,128]{1,0:T(2,128)} %fusion.13.refs_1_, s32[20,128]{1,0:T(8,128)} %fusion.3.refs_2_, f32[1280,256]{1,0:T(8,128)} %multiply_cosine_fusion.1.refs_3_, f32[1280,256]{1,0:T(8,128)} %multiply_cosine_fusion.refs_4_, ...), custom_call_target="tpu_custom_call" | custom-call | tf_op jit(solution)/shard_map/pallas_call | solution.py:503
  119.8 23.2 %all_to_all.30 = bf16[64,24,128]{2,1,0:T(8,128)(2,1)S(1)} all-to-all(bf16[64,24,128]{2,1,0:T(8,128)(2,1)} %bitcast.41), channel_id=1, replica_groups={{0,1,2,3,4,5,6,7,64,65,66,67,68,69,70,71,128,129,130,131,132,133,134,13..., dimensions={0} | all-to-all | bytes 786432 | tf_op jit(solution)/shard_map/all_to_all | solution.py:324
  143.0 0.1 reduce_sum.24
  143.1 18.6 %all_to_all.31 = bf16[8,24,128]{2,1,0:T(8,128)(2,1)S(1)} all-to-all(bf16[8,24,128]{2,1,0:T(8,128)(2,1)S(1)} %broadcast_in_dim.39), channel_id=1, replica_groups={{0,8,16,24,32,40,48,56},{4,12,20,28,36,44,52,60},{1,9,17,25,33,41,49,57..., dimensions={0} | all-to-all | bytes 98304 | tf_op jit(solution)/shard_map/all_to_all | solution.py:324
  161.8 0.1 broadcast_in_dim.40
  161.8 16.9 %all_to_all.32.whole_ref = bf16[64,24,128]{2,1,0:T(8,128)(2,1)S(1)} all-to-all(bf16[64,24,128]{2,1,0:T(8,128)(2,1)S(1)} %broadcast_in_dim.40), channel_id=1, replica_groups={{0,1,2,3,4,5,6,7,64,65,66,67,68,69,70,71,128,129,130,131,132,133,134,13..., dimensions={0} | all-to-all | bytes 786432 | tf_op jit(solution)/shard_map/all_to_all | solution.py:324
  178.7 0.9 shard_map.173
  (24 shorter events, 0.1 us)
Async XLA Ops:
  0.6 40.2 %copy-start.4 = (s32[1,20,128]{2,0,1:T(1,128)S(1)}, s32[1,20,128]{2,0,1:T(1,128)}, u32[]{:S(2)}) copy-start(s32[1,20,128]{2,0,1:T(1,128)} %param.17) | copy-start | bytes 30724
  0.6 40.3 %copy-start.7 = (f32[256]{0:T(256)S(1)}, f32[256]{0:T(256)}, u32[]{:S(2)}) copy-start(f32[256]{0:T(256)} %param.24) | copy-start | bytes 3076
  36.6 10.9 %all-to-all-start = ((bf16[8,208,128]{2,1,0:T(8,128)(2,1)}), bf16[8,208,128]{2,1,0:T(8,128)(2,1)S(1)}, u32[]{:S(2)}, u32[]{:S(2)}) async-start(bf16[8,208,128]{2,1,0:T(8,128)(2,1)} %shard_map.166), calls=%async_computation | async-start | bytes 851968 | tf_op jit(solution)/shard_map/all_to_all | solution.py:324
  40.9 20.3 %copy-start.6 = (s32[1,2,128]{2,1,0:T(2,128)S(1)}, s32[1,2,128]{2,1,0:T(2,128)}, u32[]{:S(2)}) copy-start(s32[1,2,128]{2,1,0:T(2,128)} %param.15) | copy-start | bytes 3076
  40.9 20.9 %copy-start.3 = (bf16[186,256]{1,0:T(8,128)(2,1)S(1)}, bf16[186,256]{1,0:T(8,128)(2,1)}, u32[]{:S(2)}) copy-start(bf16[186,256]{1,0:T(8,128)(2,1)} %param.21) | copy-start | bytes 285700
  40.9 20.9 %slice-start = ((bf16[186,256]{1,0:T(8,128)(2,1)}), bf16[58,256]{1,0:T(8,128)(2,1)S(1)}, s32[]{:S(2)}) async-start(bf16[186,256]{1,0:T(8,128)(2,1)} %param.21), calls=%async_computation.6 | async-start | bytes 65536 | tf_op jit(solution)/shard_map/slice | solution.py:453
  46.3 15.6 %copy-start.5 = (s32[1,20,128]{2,0,1:T(1,128)S(1)}, s32[1,20,128]{2,0,1:T(1,128)}, u32[]{:S(2)}) copy-start(s32[1,20,128]{2,0,1:T(1,128)} %param.16) | copy-start | bytes 30724
  48.5 20.8 %copy-start = (bf16[256,512]{1,0:T(8,128)(2,1)S(1)}, bf16[256,512]{1,0:T(8,128)(2,1)}, u32[]{:S(2)}) copy-start(bf16[256,512]{1,0:T(8,128)(2,1)} %refs_6_.4) | copy-start | bytes 786436
  48.5 20.8 %copy-start.1 = (f32[128,256]{1,0:T(8,128)S(1)}, f32[128,256]{1,0:T(8,128)}, u32[]{:S(2)}) copy-start(f32[128,256]{1,0:T(8,128)} %refs_2_.3) | copy-start | bytes 393220
  48.5 20.8 %copy-start.2 = (f32[512]{0:T(512)S(1)}, f32[512]{0:T(512)}, u32[]{:S(2)}) copy-start(f32[512]{0:T(512)} %param.23) | copy-start | bytes 6148
  48.5 20.8 %all-to-all-start.1 = ((bf16[8,192,128]{2,1,0:T(8,128)(2,1)}), bf16[8,192,128]{2,1,0:T(8,128)(2,1)S(1)}, u32[]{:S(2)}, u32[]{:S(2)}) async-start(bf16[8,192,128]{2,1,0:T(8,128)(2,1)} %shard_map.167), calls=%async_computation.1 | async-start | bytes 786432 | tf_op jit(solution)/shard_map/all_to_all | solution.py:324
  96.4 13.7 %all-to-all-start.2 = ((bf16[8,256,256]{2,1,0:T(8,128)(2,1)}), bf16[8,256,256]{2,1,0:T(8,128)(2,1)}, u32[]{:S(2)}, u32[]{:S(2)}) async-start(bf16[8,256,256]{2,1,0:T(8,128)(2,1)} %shard_map.170), calls=%async_computation.2 | async-start | bytes 2097152 | tf_op jit(solution)/shard_map/all_to_all | solution.py:324

commit v8 on v7

--- a/solution.py
+++ b/solution.py
@@ -222,14 +222,20 @@
     rows_ref, ends_ref, near_ref, early_ref, late_ref = targets[:5]
     cot_ref, attn_ref, pred_ref, pred_out_ref = targets[5:]
     started = copies(sources, targets, sems)
-    rows_copy, ends_copy, near_copy, early_copy, late_copy = started[:5]
+    _, ends_copy, near_copy, early_copy, late_copy = started[:5]
     cot_copy, attn_copy, pred_copy, out_copy = started[5:]
-    for copy in (ends_copy, rows_copy, near_copy):
+    piece = rows_ref.shape[0] // 2
+    rows_copies = [
+        pltpu.make_async_copy(
+            sources[0].at[pl.ds(part * piece, piece)],
+            rows_ref.at[pl.ds(part * piece, piece)],
+            sems.at[len(sources) * part],
+        )
+        for part in range(2)
+    ]
+    for copy in (ends_copy, *rows_copies, near_copy):
         copy.start()
     ends_copy.wait()
-    rows_copy.wait()
-    for copy in (early_copy, attn_copy, late_copy, cot_copy, out_copy, pred_copy):
-        copy.start()
     slots, width = rows_ref.shape
     events = ends_ref.shape[1]
     pair = 2 * events
@@ -246,7 +252,14 @@
         lanes = lane_index((pair, slots))
         return dot(jnp.where(index == lanes, 1.0, 0.0).astype(BF16), rows_ref[...])
 
-    own = fetch(ends_ref[0:1, :], ends_ref[1:2, :])
+    spots = jnp.concatenate([upright(ends_ref[0:1, :]), upright(ends_ref[1:2, :])], axis=0)
+    own = jnp.zeros((pair, width), F32)
+    for part in range(2):
+        rows_copies[part].wait()
+        hits = jnp.where(spots == lane_index((pair, piece)) + part * piece, 1.0, 0.0)
+        own = own + dot(hits.astype(BF16), rows_ref[part * piece : (part + 1) * piece, :])
+    for copy in (early_copy, attn_copy, late_copy, cot_copy, out_copy, pred_copy):
+        copy.start()
     near_copy.wait()
     for near in range(near_count):
         spot = slice(near * pair, (near + 1) * pair)
@@ -508,7 +521,7 @@
         ),
         in_specs=[pl.BlockSpec(memory_space=pltpu.HBM)] * len(inputs),
         scratch_shapes=[pltpu.VMEM(value.shape, value.dtype) for value in inputs]
-        + [pltpu.VMEM((pairs, width), BF16), pltpu.SemaphoreType.DMA((len(inputs),))],
+        + [pltpu.VMEM((pairs, width), BF16), pltpu.SemaphoreType.DMA((len(inputs) + 1,))],
         compiler_params=ALONE,
     )(*inputs)
     grad_out, grad_pair = sum_everywhere(grads, line, peers, width)

time: 180 us -> 180 us (level)
  no operation moved by 1% of the time
where the time goes in v8:
time: 180 us
  blocking collectives  116 us (64%)
  starting transfers between devices  21.3 us (12%)
  Pallas kernels  20 us (11%)
  other arithmetic  12.1 us (7%)
  waiting for transfers between devices  9.56 us (5%)
    all_to_all x3, blocking collectives, exchange(): lax.all_to_all(value, axis, split_axis=0, concat_axis=0, tiled=True, axis...  58.7 us
    all_gather x1, blocking collectives, per_device(): got = lax.all_gather(sent, 'dp', axis=0, tiled=True, axis_index_groups=line)  32.1 us
    all_gather x1, blocking collectives, per_device(): lax.all_gather(before, 'dp', axis=0, tiled=True, axis_index_groups=line)  24.8 us
    all_to_all x3, starting transfers between devices, exchange(): lax.all_to_all(value, axis, split_axis=0, concat_axis=0, tiled=True, axis...  21.3 us
    pallas_call x1, Pallas kernels, per_device(): pl.pallas_call(event_body, out_shape=(jax.ShapeDtypeStruct((1, events), F...  9.69 us
    all_to_all x3, waiting for transfers between devices, exchange(): lax.all_to_all(value, axis, split_axis=0, concat_axis=0, tiled=True, axis...  9.56 us
    cos x1, other arithmetic, per_device(): early = jnp.cos(gaps[:cut] * omega[None, :])  5.38 us
    cos x1, other arithmetic, per_device(): late = jnp.cos(gaps[cut:] * omega_late[None, :])  5.34 us
  transfers between devices with their start and end apart: 3, of which 3 were waited for; matrix products, arithmetic and copies ran while one was open for 7% of the time, Pallas kernels for 1%

profile of v8, /device:TPU:1, one launch (start us, length us, event | category | flops | bytes accessed | tf_op | source)
XLA Modules:
  0.0 179.6 jit_solution(16144819310141661307)
XLA Ops:
  0.6 0.0 copy-start.4
  0.7 1.9 %shard_map.165 = (bf16[192,128]{1,0:T(8,128)(2,1)}, f32[2,8,128]{2,1,0:T(8,128)}) custom-call(bf16[186,128]{1,0:T(8,128)(2,1)} %bitcast.44, s32[2,128]{1,0:T(2,128)} %bitcast.46, s32[1,2048]{1,0:T(1,128)} %bitcast.45), custom_call_target="tpu_custom_call" | custom-call | tf_op jit(solution)/shard_map/pallas_call | solution.py:403
  2.6 32.1 %all_gather.6 = bf16[1536,128]{1,0:T(8,128)(2,1)S(1)} all-gather(bf16[192,128]{1,0:T(8,128)(2,1)} %get-tuple-element.19), channel_id=1, replica_groups={{0,8,16,24,32,40,48,56},{4,12,20,28,36,44,52,60},{1,9,17,25,33,41,49,57..., dimensions={0}, use_global_device_ids=true | all-gather | bytes 442368 | tf_op jit(solution)/shard_map/all_gather | solution.py:419
  34.6 2.0 %shard_map.166 = bf16[8,208,128]{2,1,0:T(8,128)(2,1)} custom-call(s32[1]{0:T(128)} %bitcast.refs_0_, bf16[8,192,128]{2,1,0:T(8,128)(2,1)S(1)} %bitcast.38, f32[2,8,128]{2,1,0:T(8,128)} %get-tuple-element.20.refs_2_), custom_call_target="tpu_custom_call" | custom-call | tf_op jit(solution)/shard_map/pallas_call | solution.py:421
  36.6 4.2 %all-to-all-start = ((bf16[8,208,128]{2,1,0:T(8,128)(2,1)}), bf16[8,208,128]{2,1,0:T(8,128)(2,1)S(1)}, u32[]{:S(2)}, u32[]{:S(2)}) async-start(bf16[8,208,128]{2,1,0:T(8,128)(2,1)} %shard_map.166), calls=%async_computation | async-start | bytes 851968 | tf_op jit(solution)/shard_map/all_to_all | solution.py:337
  40.9 0.0 copy-start.6
  40.9 0.0 copy-start.3
  40.9 0.0 slice-start
  40.9 5.4 %multiply_cosine_fusion.1.refs_3_ = f32[1280,256]{1,0:T(8,128)} fusion(f32[256]{0:T(256)S(1)} %copy-done.7, f32[1280]{0:T(1024)S(1)} %mul.46), kind=kLoop, calls=%fused_computation.1 | loop fusion | flops 327680 | bytes 1316864 | tf_op jit(solution)/shard_map/cos | solution.py:446
  46.3 1.2 all-to-all-done.refs_0_.refs_1_
  47.5 1.0 shard_map.167
  48.5 12.7 %all-to-all-start.1 = ((bf16[8,192,128]{2,1,0:T(8,128)(2,1)}), bf16[8,192,128]{2,1,0:T(8,128)(2,1)S(1)}, u32[]{:S(2)}, u32[]{:S(2)}) async-start(bf16[8,192,128]{2,1,0:T(8,128)(2,1)} %shard_map.167), calls=%async_computation.1 | async-start | bytes 786432 | tf_op jit(solution)/shard_map/all_to_all | solution.py:337
  61.2 0.0 copy-done.6
  61.2 0.6 fusion.13.refs_1_
  61.9 0.6 fusion.3.refs_2_
  62.5 0.7 shard_map.168.pick_ref
  63.2 6.1 %all-to-all-done.1.refs_1_ = bf16[8,192,128]{2,1,0:T(8,128)(2,1)S(1)} async-done(((bf16[8,192,128]{2,1,0:T(8,128)(2,1)}), bf16[8,192,128]{2,1,0:T(8,128)(2,1)S(1)}, u32[]{:S(2)}, u32[]{:S(2)}) %all-to-all-start.1) | async-done | bytes 393248 | tf_op jit(solution)/shard_map/all_to_all | solution.py:337
  69.3 0.0 copy-done.1
  69.3 0.9 shard_map.169
  70.2 24.8 %all_gather.7 = bf16[1024,256]{1,0:T(8,128)(2,1)S(1)} all-gather(bf16[128,256]{1,0:T(8,128)(2,1)S(1)} %shard_map.169), channel_id=1, replica_groups={{0,8,16,24,32,40,48,56},{4,12,20,28,36,44,52,60},{1,9,17,25,33,41,49,57..., dimensions={0}, use_global_device_ids=true | all-gather | bytes 589824 | tf_op jit(solution)/shard_map/all_gather | solution.py:490
  95.0 1.4 shard_map.170
  96.4 4.4 %all-to-all-start.2 = ((bf16[8,256,256]{2,1,0:T(8,128)(2,1)}), bf16[8,256,256]{2,1,0:T(8,128)(2,1)}, u32[]{:S(2)}, u32[]{:S(2)}) async-start(bf16[8,256,256]{2,1,0:T(8,128)(2,1)} %shard_map.170), calls=%async_computation.2 | async-start | bytes 2097152 | tf_op jit(solution)/shard_map/all_to_all | solution.py:337
  100.9 1.6 shard_map.171
  102.5 5.3 %multiply_cosine_fusion.refs_4_ = f32[1280,256]{1,0:T(8,128)} fusion(f32[256]{0:T(256)S(1)} %copy-done.7, f32[1280]{0:T(1024)S(1)} %mul.54), kind=kLoop, calls=%fused_computation | loop fusion | flops 327680 | bytes 1316864 | tf_op jit(solution)/shard_map/cos | solution.py:502
  107.9 2.3 %all-to-all-done.2 = bf16[8,256,256]{2,1,0:T(8,128)(2,1)} async-done(((bf16[8,256,256]{2,1,0:T(8,128)(2,1)}), bf16[8,256,256]{2,1,0:T(8,128)(2,1)}, u32[]{:S(2)}, u32[]{:S(2)}) %all-to-all-start.2) | async-done | bytes 1048608 | tf_op jit(solution)/shard_map/all_to_all | solution.py:337
  110.1 9.7 %shard_map.172 = (f32[1,128]{1,0:T(1,128)}, bf16[1536,128]{1,0:T(8,128)(2,1)}) custom-call(bf16[2048,256]{1,0:T(8,128)(2,1)} %bitcast.11.refs_0_, s32[2,128]{1,0:T(2,128)} %fusion.13.refs_1_, s32[20,128]{1,0:T(8,128)} %fusion.3.refs_2_, f32[1280,256]{1,0:T(8,128)} %multiply_cosine_fusion.1.refs_3_, f32[1280,256]{1,0:T(8,128)} %multiply_cosine_fusion.refs_4_, ...), custom_call_target="tpu_custom_call" | custom-call | tf_op jit(solution)/shard_map/pallas_call | solution.py:516
  119.8 23.2 %all_to_all.30 = bf16[64,24,128]{2,1,0:T(8,128)(2,1)S(1)} all-to-all(bf16[64,24,128]{2,1,0:T(8,128)(2,1)} %bitcast.41), channel_id=1, replica_groups={{0,1,2,3,4,5,6,7,64,65,66,67,68,69,70,71,128,129,130,131,132,133,134,13..., dimensions={0} | all-to-all | bytes 786432 | tf_op jit(solution)/shard_map/all_to_all | solution.py:337
  143.0 0.1 reduce_sum.24
  143.1 18.6 %all_to_all.31 = bf16[8,24,128]{2,1,0:T(8,128)(2,1)S(1)} all-to-all(bf16[8,24,128]{2,1,0:T(8,128)(2,1)S(1)} %broadcast_in_dim.39), channel_id=1, replica_groups={{0,8,16,24,32,40,48,56},{4,12,20,28,36,44,52,60},{1,9,17,25,33,41,49,57..., dimensions={0} | all-to-all | bytes 98304 | tf_op jit(solution)/shard_map/all_to_all | solution.py:337
  161.8 0.1 broadcast_in_dim.40
  161.8 16.9 %all_to_all.32.whole_ref = bf16[64,24,128]{2,1,0:T(8,128)(2,1)S(1)} all-to-all(bf16[64,24,128]{2,1,0:T(8,128)(2,1)S(1)} %broadcast_in_dim.40), channel_id=1, replica_groups={{0,1,2,3,4,5,6,7,64,65,66,67,68,69,70,71,128,129,130,131,132,133,134,13..., dimensions={0} | all-to-all | bytes 786432 | tf_op jit(solution)/shard_map/all_to_all | solution.py:337
  178.7 0.9 shard_map.173
  (24 shorter events, 0.1 us)
Async XLA Ops:
  0.6 40.2 %copy-start.4 = (s32[1,20,128]{2,0,1:T(1,128)S(1)}, s32[1,20,128]{2,0,1:T(1,128)}, u32[]{:S(2)}) copy-start(s32[1,20,128]{2,0,1:T(1,128)} %param.17) | copy-start | bytes 30724
  0.6 40.3 %copy-start.7 = (f32[256]{0:T(256)S(1)}, f32[256]{0:T(256)}, u32[]{:S(2)}) copy-start(f32[256]{0:T(256)} %param.24) | copy-start | bytes 3076
  36.6 10.9 %all-to-all-start = ((bf16[8,208,128]{2,1,0:T(8,128)(2,1)}), bf16[8,208,128]{2,1,0:T(8,128)(2,1)S(1)}, u32[]{:S(2)}, u32[]{:S(2)}) async-start(bf16[8,208,128]{2,1,0:T(8,128)(2,1)} %shard_map.166), calls=%async_computation | async-start | bytes 851968 | tf_op jit(solution)/shard_map/all_to_all | solution.py:337
  40.9 20.3 %copy-start.6 = (s32[1,2,128]{2,1,0:T(2,128)S(1)}, s32[1,2,128]{2,1,0:T(2,128)}, u32[]{:S(2)}) copy-start(s32[1,2,128]{2,1,0:T(2,128)} %param.15) | copy-start | bytes 3076
  40.9 20.9 %copy-start.3 = (bf16[186,256]{1,0:T(8,128)(2,1)S(1)}, bf16[186,256]{1,0:T(8,128)(2,1)}, u32[]{:S(2)}) copy-start(bf16[186,256]{1,0:T(8,128)(2,1)} %param.21) | copy-start | bytes 285700
  40.9 20.9 %slice-start = ((bf16[186,256]{1,0:T(8,128)(2,1)}), bf16[58,256]{1,0:T(8,128)(2,1)S(1)}, s32[]{:S(2)}) async-start(bf16[186,256]{1,0:T(8,128)(2,1)} %param.21), calls=%async_computation.6 | async-start | bytes 65536 | tf_op jit(solution)/shard_map/slice | solution.py:466
  46.3 15.6 %copy-start.5 = (s32[1,20,128]{2,0,1:T(1,128)S(1)}, s32[1,20,128]{2,0,1:T(1,128)}, u32[]{:S(2)}) copy-start(s32[1,20,128]{2,0,1:T(1,128)} %param.16) | copy-start | bytes 30724
  48.5 20.8 %copy-start = (bf16[256,512]{1,0:T(8,128)(2,1)S(1)}, bf16[256,512]{1,0:T(8,128)(2,1)}, u32[]{:S(2)}) copy-start(bf16[256,512]{1,0:T(8,128)(2,1)} %refs_6_.4) | copy-start | bytes 786436
  48.5 20.8 %copy-start.1 = (f32[128,256]{1,0:T(8,128)S(1)}, f32[128,256]{1,0:T(8,128)}, u32[]{:S(2)}) copy-start(f32[128,256]{1,0:T(8,128)} %refs_2_.3) | copy-start | bytes 393220
  48.5 20.8 %copy-start.2 = (f32[512]{0:T(512)S(1)}, f32[512]{0:T(512)}, u32[]{:S(2)}) copy-start(f32[512]{0:T(512)} %param.23) | copy-start | bytes 6148
  48.5 20.8 %all-to-all-start.1 = ((bf16[8,192,128]{2,1,0:T(8,128)(2,1)}), bf16[8,192,128]{2,1,0:T(8,128)(2,1)S(1)}, u32[]{:S(2)}, u32[]{:S(2)}) async-start(bf16[8,192,128]{2,1,0:T(8,128)(2,1)} %shard_map.167), calls=%async_computation.1 | async-start | bytes 786432 | tf_op jit(solution)/shard_map/all_to_all | solution.py:337
  96.4 13.7 %all-to-all-start.2 = ((bf16[8,256,256]{2,1,0:T(8,128)(2,1)}), bf16[8,256,256]{2,1,0:T(8,128)(2,1)}, u32[]{:S(2)}, u32[]{:S(2)}) async-start(bf16[8,256,256]{2,1,0:T(8,128)(2,1)} %shard_map.170), calls=%async_computation.2 | async-start | bytes 2097152 | tf_op jit(solution)/shard_map/all_to_all | solution.py:337
